TPU v7x, 32 devices: a whole 2x2x4 slice. The times are simulated.
32 devices in a mesh: side: 2 (over x), grp: 2 (over core), pts: 8 (over z, y).
Axes of the slice: x: 2, y: 2, z: 4, core: 2. Of those that a mesh axis runs over, the one named last changes fastest.
Arguments:
- fields: bfloat16 [2, 4096, 2048], P('side', ('grp', 'pts')), may hold values from -6 to 6
- point_weight: float32 [2, 4096], P('side', ('grp', 'pts')), may hold values from 0.3 to 3
- start_modes: float32 [2, 32, 4096], P('side', None, ('grp', 'pts')), may hold values from -6 to 6
Outputs:
- modes: float32 [2, 32, 4096], P('side', None, ('grp', 'pts'))
All inputs are finite; a program needn't handle non-finite values.
Results may differ from a plain program's by a relative error of at most 0.0085.
Values may be sent and summed in bfloat16 or wider, within the bound.
No kernel may reach another device: no remote copies, remote signals or barrier semaphores. Data moves between devices by JAX's collectives and lax.ppermute only.
A program may use at most 64 MiB of HBM per device.

v0:
```python
import jax
import jax.numpy as jnp
from jax import lax
from jax.sharding import PartitionSpec as P

ITERS = 6


def from_partner(value, axis, apart):
    mask = 2**apart
    pairs = [(source, source ^ mask) for source in range(lax.axis_size(axis))]
    return lax.ppermute(value, axis, pairs)


def map_back(coeffs, anomaly):
    return lax.dot_general(
        coeffs, anomaly, (((1,), (1,)), ((), ())), preferred_element_type=jnp.float32
    )


def body(fields, point_weight, start_modes):
    local_field = fields[0]
    weight = point_weight[0]
    mode_rows = start_modes[0]
    samples = local_field.shape[1]
    total_points = local_field.shape[0] * lax.axis_size("grp") * lax.axis_size("pts")
    for iteration in range(ITERS):
        weighted = (mode_rows * weight[None, :]).astype(jnp.bfloat16)
        partial_value = jnp.dot(weighted, local_field, preferred_element_type=jnp.float32)
        coeffs = lax.psum(partial_value, ("grp", "pts")).astype(jnp.bfloat16)
        partner = from_partner(coeffs, "side", 0)
        mapped = map_back(partner, local_field)
        mapped = mapped * weight[None, :] / samples
        local_gram = lax.dot_general(
            mapped,
            mapped,
            (((1,), (1,)), ((), ())),
            precision=lax.Precision.HIGHEST,
            preferred_element_type=jnp.float32,
        )
        gram_sum = lax.psum(local_gram, ("grp", "pts")) / total_points
        factor = jnp.linalg.cholesky(gram_sum)
        mode_rows = lax.linalg.triangular_solve(factor, mapped, left_side=True, lower=True)
    return mode_rows[None]


def solution(mesh):
    placed = (
        P("side", ("grp", "pts"), None),
        P("side", ("grp", "pts")),
        P("side", None, ("grp", "pts")),
    )
    return jax.shard_map(
        body, mesh=mesh, in_specs=placed, out_specs=P("side", None, ("grp", "pts")), check_vma=False
    )
```

profile of v0, /device:TPU:0, one launch (start us, length us, event | category | flops | bytes accessed | tf_op | source)
XLA Modules:
  0.0 801.0 jit_solution(8234775146145503029)
XLA Ops:
  2.3 65.7 %all-reduce.6 = bf16[32,2048]{1,0:T(8,128)(2,1)S(1)} all-reduce(f32[32,2048]{1,0:T(8,128)S(1)} %fusion.27), channel_id=1, replica_groups=mesh['side'=2,'grp'=2,'pts'=8] {'grp','pts'}, use_global_device_ids=true, to_apply=%region_0.0 | all-reduce | flops 65536 | bytes 393216 | tf_op jit(solution)/shard_map/psum | solution.py:30
  69.8 4.1 collective-permute-done
  74.5 57.6 %psum.85 = f32[32,32]{0,1:T(8,128)S(1)} all-reduce(f32[32,32]{0,1:T(8,128)S(1)} %fusion.60), channel_id=1, replica_groups=mesh['side'=2,'grp'=2,'pts'=8] {'grp','pts'}, use_global_device_ids=true, to_apply=%region_1.0 | all-reduce | flops 1024 | bytes 8192 | tf_op jit(solution)/shard_map/psum | solution.py:41
  132.1 2.9 cholesky.104
  139.4 60.4 %all-reduce.7 = bf16[32,2048]{1,0:T(8,128)(2,1)S(1)} all-reduce(f32[32,2048]{1,0:T(8,128)S(1)} %fusion.24), channel_id=1, replica_groups=mesh['side'=2,'grp'=2,'pts'=8] {'grp','pts'}, use_global_device_ids=true, to_apply=%region_4.7 | all-reduce | flops 65536 | bytes 393216 | tf_op jit(solution)/shard_map/psum | solution.py:30
  201.2 4.3 collective-permute-done.1
  206.1 58.6 %psum.87 = f32[32,32]{0,1:T(8,128)S(1)} all-reduce(f32[32,32]{0,1:T(8,128)S(1)} %fusion.61), channel_id=1, replica_groups=mesh['side'=2,'grp'=2,'pts'=8] {'grp','pts'}, use_global_device_ids=true, to_apply=%region_5.8 | all-reduce | flops 1024 | bytes 8192 | tf_op jit(solution)/shard_map/psum | solution.py:41
  264.8 2.9 cholesky.115
  272.1 59.9 %all-reduce.8 = bf16[32,2048]{1,0:T(8,128)(2,1)S(1)} all-reduce(f32[32,2048]{1,0:T(8,128)S(1)} %fusion.21), channel_id=1, replica_groups=mesh['side'=2,'grp'=2,'pts'=8] {'grp','pts'}, use_global_device_ids=true, to_apply=%region_6.9 | all-reduce | flops 65536 | bytes 393216 | tf_op jit(solution)/shard_map/psum | solution.py:30
  333.5 4.3 collective-permute-done.2
  338.4 58.4 %psum.89 = f32[32,32]{0,1:T(8,128)S(1)} all-reduce(f32[32,32]{0,1:T(8,128)S(1)} %fusion.62), channel_id=1, replica_groups=mesh['side'=2,'grp'=2,'pts'=8] {'grp','pts'}, use_global_device_ids=true, to_apply=%region_7.10 | all-reduce | flops 1024 | bytes 8192 | tf_op jit(solution)/shard_map/psum | solution.py:41
  396.9 2.9 cholesky.126
  404.1 59.9 %all-reduce.9 = bf16[32,2048]{1,0:T(8,128)(2,1)S(1)} all-reduce(f32[32,2048]{1,0:T(8,128)S(1)} %fusion.18), channel_id=1, replica_groups=mesh['side'=2,'grp'=2,'pts'=8] {'grp','pts'}, use_global_device_ids=true, to_apply=%region_8.11 | all-reduce | flops 65536 | bytes 393216 | tf_op jit(solution)/shard_map/psum | solution.py:30
  465.5 3.6 collective-permute-done.3
  469.7 58.8 %psum.91 = f32[32,32]{0,1:T(8,128)S(1)} all-reduce(f32[32,32]{0,1:T(8,128)S(1)} %fusion.63), channel_id=1, replica_groups=mesh['side'=2,'grp'=2,'pts'=8] {'grp','pts'}, use_global_device_ids=true, to_apply=%region_9.12 | all-reduce | flops 1024 | bytes 8192 | tf_op jit(solution)/shard_map/psum | solution.py:41
  528.6 2.9 cholesky.137
  535.8 60.7 %all-reduce.10 = bf16[32,2048]{1,0:T(8,128)(2,1)S(1)} all-reduce(f32[32,2048]{1,0:T(8,128)S(1)} %fusion.15), channel_id=1, replica_groups=mesh['side'=2,'grp'=2,'pts'=8] {'grp','pts'}, use_global_device_ids=true, to_apply=%region_10.13 | all-reduce | flops 65536 | bytes 393216 | tf_op jit(solution)/shard_map/psum | solution.py:30
  598.0 3.6 collective-permute-done.4
  602.1 58.3 %psum.93 = f32[32,32]{0,1:T(8,128)S(1)} all-reduce(f32[32,32]{0,1:T(8,128)S(1)} %fusion.64), channel_id=1, replica_groups=mesh['side'=2,'grp'=2,'pts'=8] {'grp','pts'}, use_global_device_ids=true, to_apply=%region_11.14 | all-reduce | flops 1024 | bytes 8192 | tf_op jit(solution)/shard_map/psum | solution.py:41
  660.5 2.9 cholesky.148
  667.7 60.4 %all-reduce.11 = bf16[32,2048]{1,0:T(8,128)(2,1)S(1)} all-reduce(f32[32,2048]{1,0:T(8,128)S(1)} %fusion.12), channel_id=1, replica_groups=mesh['side'=2,'grp'=2,'pts'=8] {'grp','pts'}, use_global_device_ids=true, to_apply=%region_12.15 | all-reduce | flops 65536 | bytes 393216 | tf_op jit(solution)/shard_map/psum | solution.py:30
  729.6 3.6 collective-permute-done.5
  733.8 59.6 %psum.95 = f32[32,32]{0,1:T(8,128)S(1)} all-reduce(f32[32,32]{0,1:T(8,128)S(1)} %fusion.65), channel_id=1, replica_groups=mesh['side'=2,'grp'=2,'pts'=8] {'grp','pts'}, use_global_device_ids=true, to_apply=%region_13.16 | all-reduce | flops 1024 | bytes 8192 | tf_op jit(solution)/shard_map/psum | solution.py:41
  793.5 2.9 cholesky.159
  (76 shorter events, 41.5 us)
Async XLA Ops:
  0.0 1.2 copy-start
  0.0 1.2 copy-start.1
  68.0 5.9 collective-permute-start
  199.8 5.7 collective-permute-start.1
  332.0 5.8 collective-permute-start.2
  464.0 5.0 collective-permute-start.3
  596.5 5.0 collective-permute-start.4
  728.1 5.0 collective-permute-start.5
where the time goes:
time: 806 us; the launch traced here: 801 us
  blocking collectives  718 us (89%)
  other arithmetic  40.1 us (5%)
  waiting for transfers between devices  23.3 us (3%)
  starting transfers between devices  9.14 us (1%)
    psum x6, blocking collectives, body(): coeffs = lax.psum(partial_value, ('grp', 'pts')).astype(jnp.bfloat16)  367 us
    psum x6, blocking collectives, body(): gram_sum = lax.psum(local_gram, ('grp', 'pts')) / total_points  351 us
    ppermute x6, waiting for transfers between devices, from_partner(): return lax.ppermute(value, axis, pairs)  23.3 us
    another operation x18, other arithmetic, body(): factor = jnp.linalg.cholesky(gram_sum)  21.6 us
    another operation x12, other arithmetic, body(): lax.linalg.triangular_solve(factor, mapped, left_side=True, lower=True)  18.5 us
  transfers between devices with their start and end apart: 6, of which 6 were waited for; matrix products, arithmetic and copies ran while one was open for 0% of the time, Pallas kernels for 0%

commit v1 on v0

v1 whole, which is shorter than its diff:
```python
import jax
import jax.numpy as jnp
from jax import lax
from jax.experimental import pallas as pl
from jax.experimental.pallas import tpu as pltpu
from jax.sharding import PartitionSpec as P

ITERS = 6
ROWS, LANES = 8, 128
ALL = ("side", "grp", "pts")
F32, BF16 = jnp.float32, jnp.bfloat16
HIGHEST = lax.Precision.HIGHEST
VMEM = pl.BlockSpec(memory_space=pltpu.VMEM)
SMEM = pl.BlockSpec(memory_space=pltpu.SMEM)


def split3(x):
    high = x.astype(BF16)
    rest = x - high.astype(F32)
    mid = rest.astype(BF16)
    low = (rest - mid.astype(F32)).astype(BF16)
    return jnp.concatenate([high, mid, low], axis=0)


def dot_wide(x, field, contract):
    count = x.shape[0]
    out = lax.dot_general(
        split3(x), field, (((1,), (contract,)), ((), ())), preferred_element_type=F32
    )
    return out[2 * count :] + out[count : 2 * count] + out[:count]


def fold(gram, modes):
    return sum(
        pltpu.roll(gram[g * ROWS : (g + 1) * ROWS], g * modes, 1) if g else gram[:ROWS]
        for g in range(modes // ROWS)
    )


def unfold(tile, modes):
    lane = lax.broadcasted_iota(jnp.int32, (ROWS, LANES), 1)
    parts = [
        pltpu.roll(tile, LANES - g * modes, 1) if g else tile for g in range(modes // ROWS)
    ]
    return jnp.concatenate([jnp.where(lane < modes, part, 0.0) for part in parts], axis=0)


def inverse_factor(gram, modes):
    row = lax.broadcasted_iota(jnp.int32, (modes, LANES), 0)
    lane = lax.broadcasted_iota(jnp.int32, (modes, LANES), 1)
    work = gram + jnp.where(lane == row + modes, 1.0, 0.0)
    for k in range(modes):
        top = work[k : k + 1]
        pivot = top[:, k : k + 1]
        factor = jnp.where(row > k, work[:, k : k + 1] / pivot, 0.0)
        work = work - factor * top
    pivots = jnp.sum(jnp.where(lane == row, work, 0.0), axis=1, keepdims=True)
    inverse = pltpu.roll(work, LANES - modes, 1) / jnp.sqrt(pivots)
    return jnp.where(lane < modes, inverse, 0.0)


def store_tiles(send_ref, projected):
    columns = projected.shape[1] // LANES
    for d in range(send_ref.shape[0]):
        h, j = divmod(d, columns)
        send_ref[d, :ROWS, :] = projected[
            h * ROWS : (h + 1) * ROWS, j * LANES : (j + 1) * LANES
        ]


def first_kernel(weighted_ref, field_ref, send_ref):
    store_tiles(send_ref, dot_wide(weighted_ref[...], field_ref[...], 0))


def reduce_kernel(side_ref, recv_ref, send_ref, *gram_ref, grp, pts):
    side = side_ref[0]
    for s in range(2):
        for c in range(grp):
            first = (s * grp + c) * pts
            total = recv_ref[first, :ROWS, :]
            for p in range(1, pts):
                total = total + recv_ref[first + p, :ROWS, :]
            for p in range(pts):
                send_ref[((1 - s) * grp + c) * pts + p] = total
    if gram_ref:
        first = (1 - side) * (grp * pts)
        total = recv_ref[first, ROWS:, :]
        for p in range(1, pts):
            total = total + recv_ref[first + p, ROWS:, :]
        gram_ref[0][...] = total


def factor_kernel(gram_ref, out_ref, *, modes, points):
    out_ref[...] = inverse_factor(unfold(gram_ref[...], modes) / points, modes)


def back_kernel(recv_ref, field_ref, out_ref):
    columns = field_ref.shape[1] // LANES
    count = recv_ref.shape[0] // columns
    coeffs = jnp.concatenate(
        [
            jnp.concatenate([recv_ref[h * columns + j] for j in range(columns)], axis=1)
            for h in range(count)
        ],
        axis=0,
    )
    out_ref[...] = dot_wide(coeffs, field_ref[...], 1)


def map_kernel(*refs, samples, others, has_factor, last):
    refs = list(refs)
    mapped = refs.pop(0)[...]
    modes, points = mapped.shape
    block = points // (others + 1)
    for k in range(others):
        other = refs.pop(0)[...]
        cut = (others - k) * block
        mapped = mapped + jnp.concatenate([other[:, cut:], other[:, :cut]], axis=1)
    factor = refs.pop(0)[...][:, :modes] if has_factor else None
    weight = refs.pop(0)[...]
    if has_factor:
        mapped = jnp.dot(factor, mapped, precision=HIGHEST, preferred_element_type=F32)
    mapped = mapped * weight / samples
    padded = jnp.concatenate([mapped, jnp.zeros((LANES - modes, points), F32)], axis=0)
    gram = lax.dot_general(
        mapped, padded, (((1,), (1,)), ((), ())), precision=HIGHEST, preferred_element_type=F32
    )
    tile = fold(gram, modes)
    if last:
        out_ref, send_ref = refs
        out_ref[...] = mapped[:, :block]
        for d in range(send_ref.shape[0]):
            send_ref[d] = tile
        return
    field_ref, send_ref = refs
    store_tiles(send_ref, dot_wide(mapped * weight, field_ref[...], 0))
    for d in range(send_ref.shape[0]):
        send_ref[d, ROWS:, :] = tile


def finish_kernel(side_ref, recv_ref, mapped_ref, out_ref, *, grp, pts, points):
    first = side_ref[0] * (grp * pts)
    total = recv_ref[first]
    for p in range(1, pts):
        total = total + recv_ref[first + p]
    mapped = mapped_ref[...]
    modes = mapped.shape[0]
    factor = inverse_factor(unfold(total, modes) / points, modes)[:, :modes]
    out_ref[...] = jnp.dot(factor, mapped, precision=HIGHEST, preferred_element_type=F32)


def call(kernel, outs, *args):
    specs = [SMEM if a.dtype == jnp.int32 else VMEM for a in args]
    many = isinstance(outs, list)
    return pl.pallas_call(
        kernel,
        out_shape=[jax.ShapeDtypeStruct(o, F32) for o in outs] if many
        else jax.ShapeDtypeStruct(outs, F32),
        in_specs=specs,
        out_specs=[VMEM for _ in outs] if many else VMEM,
    )(*args)


def exchange(value):
    return lax.all_to_all(value, ALL, 0, 0)


def shifted(value, shift):
    grp = lax.axis_size("grp")
    return lax.ppermute(value, "grp", [((i + shift) % grp, i) for i in range(grp)])


def body_tiles(fields, point_weight, start_modes):
    local_field, weight, modes0 = fields[0], point_weight, start_modes[0]
    modes, samples = modes0.shape[0], local_field.shape[1]
    grp, pts = lax.axis_size("grp"), lax.axis_size("pts")
    devices = 2 * grp * pts
    total_points = local_field.shape[0] * grp * pts
    columns = samples // grp
    place = lax.axis_index("grp")
    side = lax.axis_index("side").astype(jnp.int32).reshape(1)

    def part(member):
        return lax.dynamic_slice_in_dim(local_field, (member % grp) * columns, columns, 1)

    weighted = modes0 * weight
    blocks, weights, starts = [part(place)], [weight], [weighted]
    for k in range(1, grp):
        blocks.append(shifted(part(place - k), k))
        weights.append(shifted(weight, k))
        starts.append(shifted(weighted, k))
    field = jnp.concatenate(blocks, axis=0)
    weight = jnp.concatenate(weights, axis=1)
    start = jnp.concatenate(starts, axis=1)
    points = weight.shape[1]

    def reduced(recv, has_gram):
        shapes = [(devices, ROWS, LANES)] + [(ROWS, LANES)] * has_gram
        kernel = lambda *refs: reduce_kernel(*refs, grp=grp, pts=pts)
        return call(kernel, shapes, side, recv)

    factor = None
    send = call(first_kernel, (devices, ROWS, LANES), start, field)
    for iteration in range(ITERS):
        has_gram = iteration > 0
        out = reduced(exchange(send), has_gram)
        gathered = exchange(out[0])
        if has_gram:
            kernel = lambda *refs: factor_kernel(*refs, modes=modes, points=total_points)
            factor = call(kernel, (modes, LANES), out[1])
        own = call(back_kernel, (modes, points), gathered, field)
        others = [shifted(own, k) for k in range(1, grp)]
        last = iteration == ITERS - 1
        kernel = lambda *refs: map_kernel(
            *refs, samples=samples, others=grp - 1, has_factor=has_gram, last=last
        )
        given = [own, *others, *([factor] if has_gram else []), weight]
        if last:
            shapes = [(modes, points // grp), (devices, ROWS, LANES)]
            mapped, send = call(kernel, shapes, *given)
        else:
            send = call(kernel, (devices, 2 * ROWS, LANES), *given, field)
    kernel = lambda *refs: finish_kernel(*refs, grp=grp, pts=pts, points=total_points)
    return call(kernel, (modes, points // grp), side, exchange(send), mapped)[None]


def body_sums(fields, point_weight, start_modes):
    local_field, weight, mode_rows = fields[0], point_weight[0], start_modes[0]
    samples = local_field.shape[1]
    total_points = local_field.shape[0] * lax.axis_size("grp") * lax.axis_size("pts")
    for _ in range(ITERS):
        weighted = (mode_rows * weight[None, :]).astype(BF16)
        partial = jnp.dot(weighted, local_field, preferred_element_type=F32)
        coeffs = lax.psum(partial, ("grp", "pts")).astype(BF16)
        partner = lax.ppermute(coeffs, "side", [(0, 1), (1, 0)])
        mapped = lax.dot_general(
            partner, local_field, (((1,), (1,)), ((), ())), preferred_element_type=F32
        )
        mapped = mapped * weight[None, :] / samples
        gram = jnp.dot(mapped, mapped.T, precision=HIGHEST, preferred_element_type=F32)
        gram = lax.psum(gram, ("grp", "pts")) / total_points
        factor = jnp.linalg.cholesky(gram)
        mode_rows = lax.linalg.triangular_solve(factor, mapped, left_side=True, lower=True)
    return mode_rows[None]


def solution(mesh):
    grp, pts = mesh.shape["grp"], mesh.shape["pts"]

    def run(fields, point_weight, start_modes):
        modes, samples = start_modes.shape[1], fields.shape[2]
        tiles = (modes // ROWS) * (samples // (LANES * grp))
        fits = tiles == 2 * grp * pts and 4 * modes == LANES
        placed = (
            P("side", ("grp", "pts"), None),
            P("side", ("grp", "pts")),
            P("side", None, ("grp", "pts")),
        )
        return jax.shard_map(
            body_tiles if fits else body_sums,
            mesh=mesh,
            in_specs=placed,
            out_specs=P("side", None, ("grp", "pts")),
            check_vma=False,
        )(fields, point_weight, start_modes)

    return run
```

time: 806 us -> 239 us (0.30)
  blocking collectives: 718 us -> 135 us
  Pallas kernels: 0 us -> 64.9 us
  other arithmetic: 40.1 us -> 1.69 us
    psum x12 -> x0, blocking collectives: 718 us -> none  [the longest x6 367 us: body(): coeffs = lax.psum(partial_value, ('grp', 'pts')).astype(jnp.bfloat16)]
    all_to_all x0 -> x11, blocking collectives: none -> 135 us  [exchange(): return lax.all_to_all(value, ALL, 0, 0)]
    pallas_call x0 -> x25, Pallas kernels: none -> 64.9 us  [call(): pl.pallas_call(kernel, out_shape=[jax.ShapeDtypeStruct(o, F32) for o in o...]
    another operation x30 -> x0, other arithmetic: 40.1 us -> none  [the longest x18 21.6 us: body(): factor = jnp.linalg.cholesky(gram_sum)]
    ppermute x6 -> x9, waiting for transfers between devices: 23.3 us -> 2.83 us  [shifted(): lax.ppermute(value, 'grp', [((i + shift) % grp, i) for i in range(grp)])]
    all_to_all x0 -> x2, waiting for transfers between devices: none -> 15.4 us  [exchange(): return lax.all_to_all(value, ALL, 0, 0)]
    all_to_all x0 -> x2, starting transfers between devices: none -> 9.77 us  [exchange(): return lax.all_to_all(value, ALL, 0, 0)]
  transfers between devices with their start and end apart: 6 -> 11, of which waited for: 6 -> 4; matrix products, arithmetic and copies ran while one was open for 0% -> 0% of each run, Pallas kernels for 0% -> 9%
where the time goes in v1:
time: 239 us; the launch traced here: 238 us
  blocking collectives  135 us (56%)
  Pallas kernels  64.9 us (27%)
  waiting for transfers between devices  18.3 us (8%)
  starting transfers between devices  11.3 us (5%)
  local copies, waits for them, and re-layouts  6.34 us (3%)
    all_to_all x11, blocking collectives, exchange(): return lax.all_to_all(value, ALL, 0, 0)  135 us
    pallas_call x25, Pallas kernels, call(): pl.pallas_call(kernel, out_shape=[jax.ShapeDtypeStruct(o, F32) for o in o...  64.9 us
    all_to_all x2, waiting for transfers between devices, exchange(): return lax.all_to_all(value, ALL, 0, 0)  15.4 us
    all_to_all x2, starting transfers between devices, exchange(): return lax.all_to_all(value, ALL, 0, 0)  9.77 us
    unnamed x23, local copies, waits for them, and re-layouts  5.06 us
  transfers between devices with their start and end apart: 11, of which 4 were waited for; matrix products, arithmetic and copies ran while one was open for 0% of the time, Pallas kernels for 9%

profile of v1, /device:TPU:0, one launch (start us, length us, event | category | flops | bytes accessed | tf_op | source)
XLA Modules:
  0.0 237.5 jit_solution(693482038453186543)
XLA Ops:
  7.3 7.2 %all-to-all-start = ((f32[32,8,128]{2,1,0:T(8,128)}), f32[32,8,128]{2,1,0:T(8,128)S(1)}, u32[]{:S(2)}, u32[]{:S(2)}) async-start(f32[32,8,128]{2,1,0:T(8,128)} %shard_map.37), calls=%async_computation | async-start | bytes 262144 | tf_op jit(solution)/shard_map/all_to_all | solution.py:165
  14.6 7.8 %all-to-all-done.refs_1_ = f32[32,8,128]{2,1,0:T(8,128)S(1)} async-done(((f32[32,8,128]{2,1,0:T(8,128)}), f32[32,8,128]{2,1,0:T(8,128)S(1)}, u32[]{:S(2)}, u32[]{:S(2)}) %all-to-all-start) | async-done | bytes 131104 | tf_op jit(solution)/shard_map/all_to_all | solution.py:165
  27.3 7.6 %all-to-all-done.1.recv_ref = f32[32,8,128]{2,1,0:T(8,128)S(1)} async-done(((f32[32,8,128]{2,1,0:T(8,128)}), f32[32,8,128]{2,1,0:T(8,128)S(1)}, u32[]{:S(2)}, u32[]{:S(2)}) %all-to-all-start.1) | async-done | bytes 131104 | tf_op jit(solution)/shard_map/all_to_all | solution.py:165
  42.5 13.7 %all_to_all.65.refs_1_ = f32[32,16,128]{2,1,0:T(8,128)} all-to-all(f32[32,16,128]{2,1,0:T(8,128)} %shard_map.40), channel_id=1, replica_groups=mesh['side'=2,'grp'=2,'pts'=8] {'side','grp','pts'}, dimensions={0} | all-to-all | bytes 524288 | tf_op jit(solution)/shard_map/all_to_all | solution.py:165
  57.8 11.1 %all_to_all.66.recv_ref = f32[32,8,128]{2,1,0:T(8,128)} all-to-all(f32[32,8,128]{2,1,0:T(8,128)} %get-tuple-element.17), channel_id=1, replica_groups=mesh['side'=2,'grp'=2,'pts'=8] {'side','grp','pts'}, dimensions={0} | all-to-all | bytes 262144 | tf_op jit(solution)/shard_map/all_to_all | solution.py:165
  71.4 3.9 %shard_map.43.refs_2_ = f32[32,128]{1,0:T(8,128)} custom-call(f32[8,128]{1,0:T(8,128)} %get-tuple-element.18.refs_0_), custom_call_target="tpu_custom_call" | custom-call | tf_op jit(solution)/shard_map/pallas_call | solution.py:155
  75.9 2.6 %shard_map.44 = f32[32,16,128]{2,1,0:T(8,128)} custom-call(f32[32,512]{1,0:T(8,128)} %shard_map.42.refs_0_, f32[32,512]{1,0:T(8,128)} %copy-done.4, f32[32,128]{1,0:T(8,128)} %shard_map.43.refs_2_, f32[1,512]{1,0:T(1,128)} %copy-done.2, bf16[512,1024]{1,0:T(8,128)(2,1)} %pad_maximum_fusion.field_ref.refs_3_.refs_4_), custom_call_target="tpu_custom_call" | custom-call | tf_op jit(solution)/shard_map/pallas_call | solution.py:155
  78.5 13.7 %all_to_all.67.refs_1_ = f32[32,16,128]{2,1,0:T(8,128)} all-to-all(f32[32,16,128]{2,1,0:T(8,128)} %shard_map.44), channel_id=1, replica_groups=mesh['side'=2,'grp'=2,'pts'=8] {'side','grp','pts'}, dimensions={0} | all-to-all | bytes 524288 | tf_op jit(solution)/shard_map/all_to_all | solution.py:165
  93.9 11.1 %all_to_all.68.recv_ref = f32[32,8,128]{2,1,0:T(8,128)} all-to-all(f32[32,8,128]{2,1,0:T(8,128)} %get-tuple-element.19), channel_id=1, replica_groups=mesh['side'=2,'grp'=2,'pts'=8] {'side','grp','pts'}, dimensions={0} | all-to-all | bytes 262144 | tf_op jit(solution)/shard_map/all_to_all | solution.py:165
  107.4 3.9 %shard_map.47.refs_2_ = f32[32,128]{1,0:T(8,128)} custom-call(f32[8,128]{1,0:T(8,128)} %get-tuple-element.20.refs_0_), custom_call_target="tpu_custom_call" | custom-call | tf_op jit(solution)/shard_map/pallas_call | solution.py:155
  112.0 2.6 %shard_map.48 = f32[32,16,128]{2,1,0:T(8,128)} custom-call(f32[32,512]{1,0:T(8,128)} %shard_map.46.refs_0_, f32[32,512]{1,0:T(8,128)} %copy-done.5, f32[32,128]{1,0:T(8,128)} %shard_map.47.refs_2_, f32[1,512]{1,0:T(1,128)} %copy-done.2, bf16[512,1024]{1,0:T(8,128)(2,1)} %pad_maximum_fusion.field_ref.refs_3_.refs_4_), custom_call_target="tpu_custom_call" | custom-call | tf_op jit(solution)/shard_map/pallas_call | solution.py:155
  114.6 13.7 %all_to_all.69.refs_1_ = f32[32,16,128]{2,1,0:T(8,128)} all-to-all(f32[32,16,128]{2,1,0:T(8,128)} %shard_map.48), channel_id=1, replica_groups=mesh['side'=2,'grp'=2,'pts'=8] {'side','grp','pts'}, dimensions={0} | all-to-all | bytes 524288 | tf_op jit(solution)/shard_map/all_to_all | solution.py:165
  129.9 11.1 %all_to_all.70.recv_ref = f32[32,8,128]{2,1,0:T(8,128)} all-to-all(f32[32,8,128]{2,1,0:T(8,128)} %get-tuple-element.21), channel_id=1, replica_groups=mesh['side'=2,'grp'=2,'pts'=8] {'side','grp','pts'}, dimensions={0} | all-to-all | bytes 262144 | tf_op jit(solution)/shard_map/all_to_all | solution.py:165
  143.5 3.9 %shard_map.51.refs_2_ = f32[32,128]{1,0:T(8,128)} custom-call(f32[8,128]{1,0:T(8,128)} %get-tuple-element.22.refs_0_), custom_call_target="tpu_custom_call" | custom-call | tf_op jit(solution)/shard_map/pallas_call | solution.py:155
  148.1 2.6 %shard_map.52 = f32[32,16,128]{2,1,0:T(8,128)} custom-call(f32[32,512]{1,0:T(8,128)} %shard_map.50.refs_0_, f32[32,512]{1,0:T(8,128)} %copy-done.6, f32[32,128]{1,0:T(8,128)} %shard_map.51.refs_2_, f32[1,512]{1,0:T(1,128)} %copy-done.2, bf16[512,1024]{1,0:T(8,128)(2,1)} %pad_maximum_fusion.field_ref.refs_3_.refs_4_), custom_call_target="tpu_custom_call" | custom-call | tf_op jit(solution)/shard_map/pallas_call | solution.py:155
  150.7 13.7 %all_to_all.71.refs_1_ = f32[32,16,128]{2,1,0:T(8,128)} all-to-all(f32[32,16,128]{2,1,0:T(8,128)} %shard_map.52), channel_id=1, replica_groups=mesh['side'=2,'grp'=2,'pts'=8] {'side','grp','pts'}, dimensions={0} | all-to-all | bytes 524288 | tf_op jit(solution)/shard_map/all_to_all | solution.py:165
  166.0 11.1 %all_to_all.72.recv_ref = f32[32,8,128]{2,1,0:T(8,128)} all-to-all(f32[32,8,128]{2,1,0:T(8,128)} %get-tuple-element.23), channel_id=1, replica_groups=mesh['side'=2,'grp'=2,'pts'=8] {'side','grp','pts'}, dimensions={0} | all-to-all | bytes 262144 | tf_op jit(solution)/shard_map/all_to_all | solution.py:165
  179.6 3.9 %shard_map.55.refs_2_ = f32[32,128]{1,0:T(8,128)} custom-call(f32[8,128]{1,0:T(8,128)} %get-tuple-element.24.refs_0_), custom_call_target="tpu_custom_call" | custom-call | tf_op jit(solution)/shard_map/pallas_call | solution.py:155
  184.1 2.6 %shard_map.56 = f32[32,16,128]{2,1,0:T(8,128)} custom-call(f32[32,512]{1,0:T(8,128)} %shard_map.54.refs_0_, f32[32,512]{1,0:T(8,128)} %copy-done.7, f32[32,128]{1,0:T(8,128)} %shard_map.55.refs_2_, f32[1,512]{1,0:T(1,128)} %copy-done.2, bf16[512,1024]{1,0:T(8,128)(2,1)} %pad_maximum_fusion.field_ref.refs_3_.refs_4_), custom_call_target="tpu_custom_call" | custom-call | tf_op jit(solution)/shard_map/pallas_call | solution.py:155
  186.7 13.7 %all_to_all.73.refs_1_ = f32[32,16,128]{2,1,0:T(8,128)} all-to-all(f32[32,16,128]{2,1,0:T(8,128)} %shard_map.56), channel_id=1, replica_groups=mesh['side'=2,'grp'=2,'pts'=8] {'side','grp','pts'}, dimensions={0} | all-to-all | bytes 524288 | tf_op jit(solution)/shard_map/all_to_all | solution.py:165
  202.1 11.1 %all_to_all.74.recv_ref = f32[32,8,128]{2,1,0:T(8,128)} all-to-all(f32[32,8,128]{2,1,0:T(8,128)} %get-tuple-element.25), channel_id=1, replica_groups=mesh['side'=2,'grp'=2,'pts'=8] {'side','grp','pts'}, dimensions={0} | all-to-all | bytes 262144 | tf_op jit(solution)/shard_map/all_to_all | solution.py:165
  215.6 3.9 %shard_map.59.refs_2_ = f32[32,128]{1,0:T(8,128)} custom-call(f32[8,128]{1,0:T(8,128)} %get-tuple-element.26.refs_0_), custom_call_target="tpu_custom_call" | custom-call | tf_op jit(solution)/shard_map/pallas_call | solution.py:155
  222.2 11.1 %all_to_all.75.refs_1_ = f32[32,8,128]{2,1,0:T(8,128)} all-to-all(f32[32,8,128]{2,1,0:T(8,128)} %get-tuple-element.27), channel_id=1, replica_groups=mesh['side'=2,'grp'=2,'pts'=8] {'side','grp','pts'}, dimensions={0} | all-to-all | bytes 262144 | tf_op jit(solution)/shard_map/all_to_all | solution.py:165
  233.2 4.3 %shard_map.61 = f32[32,256]{1,0:T(8,128)} custom-call(s32[1]{0:T(128)} %bitcast.refs_0_, f32[32,8,128]{2,1,0:T(8,128)} %all_to_all.75.refs_1_, f32[32,256]{1,0:T(8,128)} %get-tuple-element.28.refs_2_), custom_call_target="tpu_custom_call" | custom-call | tf_op jit(solution)/shard_map/pallas_call | solution.py:155
  (62 shorter events, 45.5 us)
Async XLA Ops:
  0.0 1.8 copy-start.9
  0.0 1.8 copy-start.10
  1.3 2.8 %collective-permute-start.1 = (bf16[256,1024]{1,0:T(8,128)(2,1)S(1)}, bf16[256,1024]{1,0:T(8,128)(2,1)S(1)}, u32[]{:S(2)}, u32[]{:S(2)}) collective-permute-start(bf16[256,1024]{1,0:T(8,128)(2,1)S(1)} %get-tuple-element.30), channel_id=1, source_target_pairs={{8,0},{0,8},{9,1},{1,9},{10,2},{2,10},{11,3},{3,11},{12,4},{4,12},... | collective-permute-start | bytes 1572872 | tf_op jit(solution)/shard_map/ppermute | solution.py:170
  1.9 1.6 collective-permute-start
  7.3 15.0 %all-to-all-start = ((f32[32,8,128]{2,1,0:T(8,128)}), f32[32,8,128]{2,1,0:T(8,128)S(1)}, u32[]{:S(2)}, u32[]{:S(2)}) async-start(f32[32,8,128]{2,1,0:T(8,128)} %shard_map.37), calls=%async_computation | async-start | bytes 262144 | tf_op jit(solution)/shard_map/all_to_all | solution.py:165
  22.4 0.7 copy-start.1
  24.6 10.4 %all-to-all-start.1 = ((f32[32,8,128]{2,1,0:T(8,128)}), f32[32,8,128]{2,1,0:T(8,128)S(1)}, u32[]{:S(2)}, u32[]{:S(2)}) async-start(f32[32,8,128]{2,1,0:T(8,128)} %shard_map.38), calls=%async_computation.1 | async-start | bytes 262144 | tf_op jit(solution)/shard_map/all_to_all | solution.py:165
  27.2 11.0 %collective-permute-start.3 = (f32[1,256]{1,0:T(1,128)S(1)}, f32[1,256]{1,0:T(1,128)S(1)}, u32[]{:S(2)}, u32[]{:S(2)}) collective-permute-start(f32[1,256]{1,0:T(1,128)S(1)} %copy-done.10), channel_id=1, source_target_pairs={{8,0},{0,8},{9,1},{1,9},{10,2},{2,10},{11,3},{3,11},{12,4},{4,12},... | collective-permute-start | bytes 3080 | tf_op jit(solution)/shard_map/ppermute | solution.py:170
  35.0 0.7 copy-start
  38.0 1.5 collective-permute-start.2
  38.1 1.3 copy-start.2
  39.5 0.6 copy-start.3
  71.3 4.0 %collective-permute-start.4 = (f32[32,512]{1,0:T(8,128)}, f32[32,512]{1,0:T(8,128)S(1)}, u32[]{:S(2)}, u32[]{:S(2)}) collective-permute-start(f32[32,512]{1,0:T(8,128)} %shard_map.42.refs_0_), channel_id=1, source_target_pairs={{8,0},{0,8},{9,1},{1,9},{10,2},{2,10},{11,3},{3,11},{12,4},{4,12},... | collective-permute-start | bytes 196616 | tf_op jit(solution)/shard_map/ppermute | solution.py:170
  75.3 0.6 copy-start.4
  107.3 4.0 %collective-permute-start.5 = (f32[32,512]{1,0:T(8,128)}, f32[32,512]{1,0:T(8,128)S(1)}, u32[]{:S(2)}, u32[]{:S(2)}) collective-permute-start(f32[32,512]{1,0:T(8,128)} %shard_map.46.refs_0_), channel_id=1, source_target_pairs={{8,0},{0,8},{9,1},{1,9},{10,2},{2,10},{11,3},{3,11},{12,4},{4,12},... | collective-permute-start | bytes 196616 | tf_op jit(solution)/shard_map/ppermute | solution.py:170
  111.4 0.6 copy-start.5
  143.4 4.0 %collective-permute-start.6 = (f32[32,512]{1,0:T(8,128)}, f32[32,512]{1,0:T(8,128)S(1)}, u32[]{:S(2)}, u32[]{:S(2)}) collective-permute-start(f32[32,512]{1,0:T(8,128)} %shard_map.50.refs_0_), channel_id=1, source_target_pairs={{8,0},{0,8},{9,1},{1,9},{10,2},{2,10},{11,3},{3,11},{12,4},{4,12},... | collective-permute-start | bytes 196616 | tf_op jit(solution)/shard_map/ppermute | solution.py:170
  147.4 0.6 copy-start.6
  179.5 4.0 %collective-permute-start.7 = (f32[32,512]{1,0:T(8,128)}, f32[32,512]{1,0:T(8,128)S(1)}, u32[]{:S(2)}, u32[]{:S(2)}) collective-permute-start(f32[32,512]{1,0:T(8,128)} %shard_map.54.refs_0_), channel_id=1, source_target_pairs={{8,0},{0,8},{9,1},{1,9},{10,2},{2,10},{11,3},{3,11},{12,4},{4,12},... | collective-permute-start | bytes 196616 | tf_op jit(solution)/shard_map/ppermute | solution.py:170
  183.5 0.6 copy-start.7
  215.5 4.0 %collective-permute-start.8 = (f32[32,512]{1,0:T(8,128)}, f32[32,512]{1,0:T(8,128)S(1)}, u32[]{:S(2)}, u32[]{:S(2)}) collective-permute-start(f32[32,512]{1,0:T(8,128)} %shard_map.58.refs_0_), channel_id=1, source_target_pairs={{8,0},{0,8},{9,1},{1,9},{10,2},{2,10},{11,3},{3,11},{12,4},{4,12},... | collective-permute-start | bytes 196616 | tf_op jit(solution)/shard_map/ppermute | solution.py:170
  219.5 0.6 copy-start.8

commit v2 on v1

--- a/solution.py
+++ b/solution.py
@@ -120,7 +120,7 @@
     weight = refs.pop(0)[...]
     if has_factor:
         mapped = jnp.dot(factor, mapped, precision=HIGHEST, preferred_element_type=F32)
-    mapped = mapped * weight / samples
+    mapped = mapped * weight if has_factor else mapped * weight / samples
     padded = jnp.concatenate([mapped, jnp.zeros((LANES - modes, points), F32)], axis=0)
     gram = lax.dot_general(
         mapped, padded, (((1,), (1,)), ((), ())), precision=HIGHEST, preferred_element_type=F32
@@ -149,15 +149,19 @@
     out_ref[...] = jnp.dot(factor, mapped, precision=HIGHEST, preferred_element_type=F32)
 
 
-def call(kernel, outs, *args):
+def call(kernel, outs, *args, cost=None):
     specs = [SMEM if a.dtype == jnp.int32 else VMEM for a in args]
+    args = [
+        a if a.dtype == jnp.int32 else pltpu.with_memory_space_constraint(a, pltpu.VMEM)
+        for a in args
+    ]
     many = isinstance(outs, list)
     return pl.pallas_call(
         kernel,
-        out_shape=[jax.ShapeDtypeStruct(o, F32) for o in outs] if many
-        else jax.ShapeDtypeStruct(outs, F32),
+        out_shape=[pltpu.VMEM(o, F32) for o in outs] if many else pltpu.VMEM(outs, F32),
         in_specs=specs,
         out_specs=[VMEM for _ in outs] if many else VMEM,
+        cost_estimate=cost,
     )(*args)
 
 
@@ -207,7 +211,8 @@
         gathered = exchange(out[0])
         if has_gram:
             kernel = lambda *refs: factor_kernel(*refs, modes=modes, points=total_points)
-            factor = call(kernel, (modes, LANES), out[1])
+            cost = pl.CostEstimate(flops=modes**3 << 10, bytes_accessed=ROWS * LANES * 4, transcendentals=0)
+            factor = call(kernel, (modes, LANES), out[1], cost=cost) / samples
         own = call(back_kernel, (modes, points), gathered, field)
         others = [shifted(own, k) for k in range(1, grp)]
         last = iteration == ITERS - 1

time: 239 us -> 176 us (0.74)
  blocking collectives: 135 us -> 72.7 us
  Pallas kernels: 64.9 us -> 26.6 us
  waiting for transfers between devices: 18.3 us -> 49.5 us
  starting transfers between devices: 11.3 us -> 24.3 us
  local copies, waits for them, and re-layouts: 6.34 us -> 1.91 us
    all_to_all x11 -> x6, blocking collectives: 135 us -> 72.7 us  [exchange(): return lax.all_to_all(value, ALL, 0, 0)]
    pallas_call x25, Pallas kernels: 64.9 us -> 26.6 us  [call(): pl.pallas_call(kernel, out_shape=[pltpu.VMEM(o, F32) for o in outs] if ma...]
    all_to_all x2 -> x7, waiting for transfers between devices: 15.4 us -> 41.2 us  [exchange(): return lax.all_to_all(value, ALL, 0, 0)]
    all_to_all x2 -> x7, starting transfers between devices: 9.77 us -> 22.6 us  [exchange(): return lax.all_to_all(value, ALL, 0, 0)]
    ppermute x9, waiting for transfers between devices: 2.83 us -> 8.3 us  [shifted(): lax.ppermute(value, 'grp', [((i + shift) % grp, i) for i in range(grp)])]
    unnamed x23 -> x6, local copies, waits for them, and re-layouts: 5.06 us -> 0.63 us
  transfers between devices with their start and end apart: 11 -> 16, of which waited for: 4 -> 14; matrix products, arithmetic and copies ran while one was open for 0% -> 0% of each run, Pallas kernels for 9% -> 8%
where the time goes in v2:
time: 176 us; the launch traced here: 175 us
  blocking collectives  72.7 us (41%)
  waiting for transfers between devices  49.5 us (28%)
  Pallas kernels  26.6 us (15%)
  starting transfers between devices  24.3 us (14%)
  local copies, waits for them, and re-layouts  1.91 us (1%)
    all_to_all x6, blocking collectives, exchange(): return lax.all_to_all(value, ALL, 0, 0)  72.7 us
    all_to_all x7, waiting for transfers between devices, exchange(): return lax.all_to_all(value, ALL, 0, 0)  41.2 us
    pallas_call x25, Pallas kernels, call(): pl.pallas_call(kernel, out_shape=[pltpu.VMEM(o, F32) for o in outs] if ma...  26.6 us
    all_to_all x7, starting transfers between devices, exchange(): return lax.all_to_all(value, ALL, 0, 0)  22.6 us
    ppermute x9, waiting for transfers between devices, shifted(): lax.ppermute(value, 'grp', [((i + shift) % grp, i) for i in range(grp)])  8.3 us
  transfers between devices with their start and end apart: 16, of which 14 were waited for; matrix products, arithmetic and copies ran while one was open for 0% of the time, Pallas kernels for 8%

profile of v2, /device:TPU:0, one launch (start us, length us, event | category | flops | bytes accessed | tf_op | source)
XLA Modules:
  0.0 175.3 jit_solution(13293640523738330937)
XLA Ops:
  4.5 7.2 %all-to-all-start = ((f32[32,8,128]{2,1,0:T(8,128)}), f32[32,8,128]{2,1,0:T(8,128)S(1)}, u32[]{:S(2)}, u32[]{:S(2)}) async-start(f32[32,8,128]{2,1,0:T(8,128)} %shard_map.37), calls=%async_computation | async-start | bytes 262144 | tf_op jit(solution)/shard_map/all_to_all | solution.py:169
  11.7 7.8 %all-to-all-done.refs_1_ = f32[32,8,128]{2,1,0:T(8,128)S(1)} async-done(((f32[32,8,128]{2,1,0:T(8,128)}), f32[32,8,128]{2,1,0:T(8,128)S(1)}, u32[]{:S(2)}, u32[]{:S(2)}) %all-to-all-start) | async-done | bytes 131104 | tf_op jit(solution)/shard_map/all_to_all | solution.py:169
  20.2 2.6 %all-to-all-start.1 = ((f32[32,8,128]{2,1,0:T(8,128)}), f32[32,8,128]{2,1,0:T(8,128)S(1)}, u32[]{:S(2)}, u32[]{:S(2)}) async-start(f32[32,8,128]{2,1,0:T(8,128)} %shard_map.38), calls=%async_computation.1 | async-start | bytes 262144 | tf_op jit(solution)/shard_map/all_to_all | solution.py:169
  22.9 7.6 %all-to-all-done.1.recv_ref = f32[32,8,128]{2,1,0:T(8,128)S(1)} async-done(((f32[32,8,128]{2,1,0:T(8,128)}), f32[32,8,128]{2,1,0:T(8,128)S(1)}, u32[]{:S(2)}, u32[]{:S(2)}) %all-to-all-start.1) | async-done | bytes 131104 | tf_op jit(solution)/shard_map/all_to_all | solution.py:169
  32.6 12.5 %all_to_all.65.refs_1_ = f32[32,16,128]{2,1,0:T(8,128)S(1)} all-to-all(f32[32,16,128]{2,1,0:T(8,128)S(1)} %shard_map.40), channel_id=1, replica_groups=mesh['side'=2,'grp'=2,'pts'=8] {'side','grp','pts'}, dimensions={0} | all-to-all | bytes 524288 | tf_op jit(solution)/shard_map/all_to_all | solution.py:169
  45.8 2.6 %all-to-all-start.3 = ((f32[32,8,128]{2,1,0:T(8,128)}), f32[32,8,128]{2,1,0:T(8,128)S(1)}, u32[]{:S(2)}, u32[]{:S(2)}) async-start(f32[32,8,128]{2,1,0:T(8,128)} %get-tuple-element.17), calls=%async_computation.3 | async-start | bytes 262144 | tf_op jit(solution)/shard_map/all_to_all | solution.py:169
  48.4 2.6 %shard_map.43 = f32[32,128]{1,0:T(8,128)S(1)} custom-call(f32[8,128]{1,0:T(8,128)S(1)} %get-tuple-element.18.refs_0_), custom_call_target="tpu_custom_call" | custom-call | flops 33554432 | bytes 4096 | tf_op jit(solution)/shard_map/pallas_call | solution.py:159
  51.0 5.2 %all-to-all-done.3.recv_ref = f32[32,8,128]{2,1,0:T(8,128)S(1)} async-done(((f32[32,8,128]{2,1,0:T(8,128)}), f32[32,8,128]{2,1,0:T(8,128)S(1)}, u32[]{:S(2)}, u32[]{:S(2)}) %all-to-all-start.3) | async-done | bytes 131104 | tf_op jit(solution)/shard_map/all_to_all | solution.py:169
  58.5 12.6 %all_to_all.66.refs_1_ = f32[32,16,128]{2,1,0:T(8,128)S(1)} all-to-all(f32[32,16,128]{2,1,0:T(8,128)S(1)} %shard_map.44), channel_id=1, replica_groups=mesh['side'=2,'grp'=2,'pts'=8] {'side','grp','pts'}, dimensions={0} | all-to-all | bytes 524288 | tf_op jit(solution)/shard_map/all_to_all | solution.py:169
  71.7 2.6 %all-to-all-start.5 = ((f32[32,8,128]{2,1,0:T(8,128)}), f32[32,8,128]{2,1,0:T(8,128)S(1)}, u32[]{:S(2)}, u32[]{:S(2)}) async-start(f32[32,8,128]{2,1,0:T(8,128)} %get-tuple-element.19), calls=%async_computation.5 | async-start | bytes 262144 | tf_op jit(solution)/shard_map/all_to_all | solution.py:169
  74.3 2.6 %shard_map.47 = f32[32,128]{1,0:T(8,128)S(1)} custom-call(f32[8,128]{1,0:T(8,128)S(1)} %get-tuple-element.20.refs_0_), custom_call_target="tpu_custom_call" | custom-call | flops 33554432 | bytes 4096 | tf_op jit(solution)/shard_map/pallas_call | solution.py:159
  76.9 5.2 %all-to-all-done.5.recv_ref = f32[32,8,128]{2,1,0:T(8,128)S(1)} async-done(((f32[32,8,128]{2,1,0:T(8,128)}), f32[32,8,128]{2,1,0:T(8,128)S(1)}, u32[]{:S(2)}, u32[]{:S(2)}) %all-to-all-start.5) | async-done | bytes 131104 | tf_op jit(solution)/shard_map/all_to_all | solution.py:169
  84.4 12.6 %all_to_all.67.refs_1_ = f32[32,16,128]{2,1,0:T(8,128)S(1)} all-to-all(f32[32,16,128]{2,1,0:T(8,128)S(1)} %shard_map.48), channel_id=1, replica_groups=mesh['side'=2,'grp'=2,'pts'=8] {'side','grp','pts'}, dimensions={0} | all-to-all | bytes 524288 | tf_op jit(solution)/shard_map/all_to_all | solution.py:169
  97.6 2.6 %all-to-all-start.7 = ((f32[32,8,128]{2,1,0:T(8,128)}), f32[32,8,128]{2,1,0:T(8,128)S(1)}, u32[]{:S(2)}, u32[]{:S(2)}) async-start(f32[32,8,128]{2,1,0:T(8,128)} %get-tuple-element.21), calls=%async_computation.7 | async-start | bytes 262144 | tf_op jit(solution)/shard_map/all_to_all | solution.py:169
  100.2 2.6 %shard_map.51 = f32[32,128]{1,0:T(8,128)S(1)} custom-call(f32[8,128]{1,0:T(8,128)S(1)} %get-tuple-element.22.refs_0_), custom_call_target="tpu_custom_call" | custom-call | flops 33554432 | bytes 4096 | tf_op jit(solution)/shard_map/pallas_call | solution.py:159
  102.8 5.2 %all-to-all-done.7.recv_ref = f32[32,8,128]{2,1,0:T(8,128)S(1)} async-done(((f32[32,8,128]{2,1,0:T(8,128)}), f32[32,8,128]{2,1,0:T(8,128)S(1)}, u32[]{:S(2)}, u32[]{:S(2)}) %all-to-all-start.7) | async-done | bytes 131104 | tf_op jit(solution)/shard_map/all_to_all | solution.py:169
  110.2 12.6 %all_to_all.68.refs_1_ = f32[32,16,128]{2,1,0:T(8,128)S(1)} all-to-all(f32[32,16,128]{2,1,0:T(8,128)S(1)} %shard_map.52), channel_id=1, replica_groups=mesh['side'=2,'grp'=2,'pts'=8] {'side','grp','pts'}, dimensions={0} | all-to-all | bytes 524288 | tf_op jit(solution)/shard_map/all_to_all | solution.py:169
  126.1 2.6 %shard_map.55 = f32[32,128]{1,0:T(8,128)S(1)} custom-call(f32[8,128]{1,0:T(8,128)S(1)} %get-tuple-element.24.refs_0_), custom_call_target="tpu_custom_call" | custom-call | flops 33554432 | bytes 4096 | tf_op jit(solution)/shard_map/pallas_call | solution.py:159
  128.7 5.2 %all-to-all-done.9.recv_ref = f32[32,8,128]{2,1,0:T(8,128)S(1)} async-done(((f32[32,8,128]{2,1,0:T(8,128)}), f32[32,8,128]{2,1,0:T(8,128)S(1)}, u32[]{:S(2)}, u32[]{:S(2)}) %all-to-all-start.9) | async-done | bytes 131104 | tf_op jit(solution)/shard_map/all_to_all | solution.py:169
  136.1 12.6 %all_to_all.69.refs_1_ = f32[32,16,128]{2,1,0:T(8,128)S(1)} all-to-all(f32[32,16,128]{2,1,0:T(8,128)S(1)} %shard_map.56), channel_id=1, replica_groups=mesh['side'=2,'grp'=2,'pts'=8] {'side','grp','pts'}, dimensions={0} | all-to-all | bytes 524288 | tf_op jit(solution)/shard_map/all_to_all | solution.py:169
  151.9 2.6 %shard_map.59 = f32[32,128]{1,0:T(8,128)S(1)} custom-call(f32[8,128]{1,0:T(8,128)S(1)} %get-tuple-element.26.refs_0_), custom_call_target="tpu_custom_call" | custom-call | flops 33554432 | bytes 4096 | tf_op jit(solution)/shard_map/pallas_call | solution.py:159
  154.6 5.2 %all-to-all-done.11.recv_ref = f32[32,8,128]{2,1,0:T(8,128)S(1)} async-done(((f32[32,8,128]{2,1,0:T(8,128)}), f32[32,8,128]{2,1,0:T(8,128)S(1)}, u32[]{:S(2)}, u32[]{:S(2)}) %all-to-all-start.11) | async-done | bytes 131104 | tf_op jit(solution)/shard_map/all_to_all | solution.py:169
  161.9 9.9 %all_to_all.70.refs_1_ = f32[32,8,128]{2,1,0:T(8,128)S(1)} all-to-all(f32[32,8,128]{2,1,0:T(8,128)S(1)} %get-tuple-element.27), channel_id=1, replica_groups=mesh['side'=2,'grp'=2,'pts'=8] {'side','grp','pts'}, dimensions={0} | all-to-all | bytes 262144 | tf_op jit(solution)/shard_map/all_to_all | solution.py:169
  171.9 2.8 %shard_map.61 = f32[32,256]{1,0:T(8,128)S(1)} custom-call(s32[1]{0:T(128)} %bitcast.refs_0_, f32[32,8,128]{2,1,0:T(8,128)S(1)} %all_to_all.70.refs_1_, f32[32,256]{1,0:T(8,128)S(1)} %get-tuple-element.28.refs_2_), custom_call_target="tpu_custom_call" | custom-call | tf_op jit(solution)/shard_map/pallas_call | solution.py:159
  (55 shorter events, 27.7 us)
Async XLA Ops:
  0.0 1.8 %copy-start = (f32[1,32,256]{2,1,0:T(8,128)S(1)}, f32[1,32,256]{2,1,0:T(8,128)}, u32[]{:S(2)}) copy-start(f32[1,32,256]{2,1,0:T(8,128)} %param.5) | copy-start | bytes 98308
  0.0 1.8 %copy-start.1 = (f32[1,256]{1,0:T(1,128)S(1)}, f32[1,256]{1,0:T(1,128)}, u32[]{:S(2)}) copy-start(f32[1,256]{1,0:T(1,128)} %param.4) | copy-start | bytes 3076
  1.3 2.2 %collective-permute-start.1 = (bf16[256,1024]{1,0:T(8,128)(2,1)S(1)}, bf16[256,1024]{1,0:T(8,128)(2,1)S(1)}, u32[]{:S(2)}, u32[]{:S(2)}) collective-permute-start(bf16[256,1024]{1,0:T(8,128)(2,1)S(1)} %get-tuple-element.30), channel_id=1, source_target_pairs={{8,0},{0,8},{9,1},{1,9},{10,2},{2,10},{11,3},{3,11},{12,4},{4,12},... | collective-permute-start | bytes 1572872 | tf_op jit(solution)/shard_map/ppermute | solution.py:174
  1.9 1.6 collective-permute-start
  4.5 15.0 %all-to-all-start = ((f32[32,8,128]{2,1,0:T(8,128)}), f32[32,8,128]{2,1,0:T(8,128)S(1)}, u32[]{:S(2)}, u32[]{:S(2)}) async-start(f32[32,8,128]{2,1,0:T(8,128)} %shard_map.37), calls=%async_computation | async-start | bytes 262144 | tf_op jit(solution)/shard_map/all_to_all | solution.py:169
  20.2 10.4 %all-to-all-start.1 = ((f32[32,8,128]{2,1,0:T(8,128)}), f32[32,8,128]{2,1,0:T(8,128)S(1)}, u32[]{:S(2)}, u32[]{:S(2)}) async-start(f32[32,8,128]{2,1,0:T(8,128)} %shard_map.38), calls=%async_computation.1 | async-start | bytes 262144 | tf_op jit(solution)/shard_map/all_to_all | solution.py:169
  22.7 8.4 %collective-permute-start.3 = (f32[1,256]{1,0:T(1,128)S(1)}, f32[1,256]{1,0:T(1,128)S(1)}, u32[]{:S(2)}, u32[]{:S(2)}) collective-permute-start(f32[1,256]{1,0:T(1,128)S(1)} %copy-done.1), channel_id=1, source_target_pairs={{8,0},{0,8},{9,1},{1,9},{10,2},{2,10},{11,3},{3,11},{12,4},{4,12},... | collective-permute-start | bytes 3080 | tf_op jit(solution)/shard_map/ppermute | solution.py:174
  31.0 1.3 collective-permute-start.2
  45.8 10.4 %all-to-all-start.3 = ((f32[32,8,128]{2,1,0:T(8,128)}), f32[32,8,128]{2,1,0:T(8,128)S(1)}, u32[]{:S(2)}, u32[]{:S(2)}) async-start(f32[32,8,128]{2,1,0:T(8,128)} %get-tuple-element.17), calls=%async_computation.3 | async-start | bytes 262144 | tf_op jit(solution)/shard_map/all_to_all | solution.py:169
  56.6 1.3 collective-permute-start.4
  71.7 10.4 %all-to-all-start.5 = ((f32[32,8,128]{2,1,0:T(8,128)}), f32[32,8,128]{2,1,0:T(8,128)S(1)}, u32[]{:S(2)}, u32[]{:S(2)}) async-start(f32[32,8,128]{2,1,0:T(8,128)} %get-tuple-element.19), calls=%async_computation.5 | async-start | bytes 262144 | tf_op jit(solution)/shard_map/all_to_all | solution.py:169
  82.5 1.3 collective-permute-start.5
  97.6 10.4 %all-to-all-start.7 = ((f32[32,8,128]{2,1,0:T(8,128)}), f32[32,8,128]{2,1,0:T(8,128)S(1)}, u32[]{:S(2)}, u32[]{:S(2)}) async-start(f32[32,8,128]{2,1,0:T(8,128)} %get-tuple-element.21), calls=%async_computation.7 | async-start | bytes 262144 | tf_op jit(solution)/shard_map/all_to_all | solution.py:169
  108.4 1.3 collective-permute-start.6
  123.5 10.4 %all-to-all-start.9 = ((f32[32,8,128]{2,1,0:T(8,128)}), f32[32,8,128]{2,1,0:T(8,128)S(1)}, u32[]{:S(2)}, u32[]{:S(2)}) async-start(f32[32,8,128]{2,1,0:T(8,128)} %get-tuple-element.23), calls=%async_computation.9 | async-start | bytes 262144 | tf_op jit(solution)/shard_map/all_to_all | solution.py:169
  134.3 1.3 collective-permute-start.7
  149.4 10.4 %all-to-all-start.11 = ((f32[32,8,128]{2,1,0:T(8,128)}), f32[32,8,128]{2,1,0:T(8,128)S(1)}, u32[]{:S(2)}, u32[]{:S(2)}) async-start(f32[32,8,128]{2,1,0:T(8,128)} %get-tuple-element.25), calls=%async_computation.11 | async-start | bytes 262144 | tf_op jit(solution)/shard_map/all_to_all | solution.py:169
  160.2 1.3 collective-permute-start.8

commit v3 on v2

--- a/solution.py
+++ b/solution.py
@@ -63,9 +63,30 @@
     columns = projected.shape[1] // LANES
     for d in range(send_ref.shape[0]):
         h, j = divmod(d, columns)
-        send_ref[d, :ROWS, :] = projected[
-            h * ROWS : (h + 1) * ROWS, j * LANES : (j + 1) * LANES
-        ]
+        tile = projected[h * ROWS : (h + 1) * ROWS, j * LANES : (j + 1) * LANES]
+        if send_ref.ndim == 3:
+            send_ref[d] = tile
+            continue
+        slab = send_ref.shape[2]
+        for k in range(ROWS // slab):
+            send_ref[d, k] = tile[k * slab : (k + 1) * slab]
+
+
+def own_slab(tile, place, grp):
+    slab = ROWS // grp
+    return sum(
+        jnp.where(place == c, tile[c * slab : (c + 1) * slab], 0.0) for c in range(grp)
+    )
+
+
+def whole_tile(read, first, grp, pts):
+    slabs = []
+    for c in range(grp):
+        total = read(first + c * pts)
+        for p in range(1, pts):
+            total = total + read(first + c * pts + p)
+        slabs.append(total)
+    return jnp.concatenate(slabs, axis=0)
 
 
 def first_kernel(weighted_ref, field_ref, send_ref):
@@ -73,21 +94,21 @@
 
 
 def reduce_kernel(side_ref, recv_ref, send_ref, *gram_ref, grp, pts):
-    side = side_ref[0]
     for s in range(2):
         for c in range(grp):
             first = (s * grp + c) * pts
-            total = recv_ref[first, :ROWS, :]
-            for p in range(1, pts):
-                total = total + recv_ref[first + p, :ROWS, :]
+            slabs = []
+            for k in range(grp) if gram_ref else [...]:
+                total = recv_ref[first, k]
+                for p in range(1, pts):
+                    total = total + recv_ref[first + p, k]
+                slabs.append(total)
+            total = jnp.concatenate(slabs, axis=0) if gram_ref else slabs[0]
             for p in range(pts):
                 send_ref[((1 - s) * grp + c) * pts + p] = total
     if gram_ref:
-        first = (1 - side) * (grp * pts)
-        total = recv_ref[first, ROWS:, :]
-        for p in range(1, pts):
-            total = total + recv_ref[first + p, ROWS:, :]
-        gram_ref[0][...] = total
+        first = (1 - side_ref[0]) * (grp * pts)
+        gram_ref[0][...] = whole_tile(lambda d: recv_ref[d, grp], first, grp, pts)
 
 
 def factor_kernel(gram_ref, out_ref, *, modes, points):
@@ -109,9 +130,10 @@
 
 def map_kernel(*refs, samples, others, has_factor, last):
     refs = list(refs)
+    place, grp = refs.pop(0)[0], others + 1
     mapped = refs.pop(0)[...]
     modes, points = mapped.shape
-    block = points // (others + 1)
+    block = points // grp
     for k in range(others):
         other = refs.pop(0)[...]
         cut = (others - k) * block
@@ -125,24 +147,21 @@
     gram = lax.dot_general(
         mapped, padded, (((1,), (1,)), ((), ())), precision=HIGHEST, preferred_element_type=F32
     )
-    tile = fold(gram, modes)
+    slab = own_slab(fold(gram, modes), place, grp)
     if last:
         out_ref, send_ref = refs
         out_ref[...] = mapped[:, :block]
         for d in range(send_ref.shape[0]):
-            send_ref[d] = tile
+            send_ref[d] = slab
         return
     field_ref, send_ref = refs
     store_tiles(send_ref, dot_wide(mapped * weight, field_ref[...], 0))
     for d in range(send_ref.shape[0]):
-        send_ref[d, ROWS:, :] = tile
+        send_ref[d, grp] = slab
 
 
 def finish_kernel(side_ref, recv_ref, mapped_ref, out_ref, *, grp, pts, points):
-    first = side_ref[0] * (grp * pts)
-    total = recv_ref[first]
-    for p in range(1, pts):
-        total = total + recv_ref[first + p]
+    total = whole_tile(lambda d: recv_ref[d], side_ref[0] * (grp * pts), grp, pts)
     mapped = mapped_ref[...]
     modes = mapped.shape[0]
     factor = inverse_factor(unfold(total, modes) / points, modes)[:, :modes]
@@ -181,10 +200,11 @@
     devices = 2 * grp * pts
     total_points = local_field.shape[0] * grp * pts
     columns = samples // grp
-    place = lax.axis_index("grp")
+    place = lax.axis_index("grp").astype(jnp.int32).reshape(1)
     side = lax.axis_index("side").astype(jnp.int32).reshape(1)
 
     def part(member):
+        member = member[0]
         return lax.dynamic_slice_in_dim(local_field, (member % grp) * columns, columns, 1)
 
     weighted = modes0 * weight
@@ -219,12 +239,12 @@
         kernel = lambda *refs: map_kernel(
             *refs, samples=samples, others=grp - 1, has_factor=has_gram, last=last
         )
-        given = [own, *others, *([factor] if has_gram else []), weight]
+        given = [place, own, *others, *([factor] if has_gram else []), weight]
         if last:
-            shapes = [(modes, points // grp), (devices, ROWS, LANES)]
+            shapes = [(modes, points // grp), (devices, ROWS // grp, LANES)]
             mapped, send = call(kernel, shapes, *given)
         else:
-            send = call(kernel, (devices, 2 * ROWS, LANES), *given, field)
+            send = call(kernel, (devices, grp + 1, ROWS // grp, LANES), *given, field)
     kernel = lambda *refs: finish_kernel(*refs, grp=grp, pts=pts, points=total_points)
     return call(kernel, (modes, points // grp), side, exchange(send), mapped)[None]
 
@@ -255,7 +275,7 @@
     def run(fields, point_weight, start_modes):
         modes, samples = start_modes.shape[1], fields.shape[2]
         tiles = (modes // ROWS) * (samples // (LANES * grp))
-        fits = tiles == 2 * grp * pts and 4 * modes == LANES
+        fits = tiles == 2 * grp * pts and 4 * modes == LANES and ROWS % grp == 0
         placed = (
             P("side", ("grp", "pts"), None),
             P("side", ("grp", "pts")),

time: 176 us -> 168 us (0.955)
  blocking collectives: 72.7 us -> 61.3 us
  starting transfers between devices: 24.3 us -> 28.1 us
    all_to_all x6, blocking collectives: 72.7 us -> 61.3 us  [exchange(): return lax.all_to_all(value, ALL, 0, 0)]
    all_to_all x7, starting transfers between devices: 22.6 us -> 26.4 us  [exchange(): return lax.all_to_all(value, ALL, 0, 0)]
where the time goes in v3:
time: 168 us
  blocking collectives  61.3 us (36%)
  waiting for transfers between devices  49.5 us (29%)
  starting transfers between devices  28.1 us (17%)
  Pallas kernels  26.7 us (16%)
  local copies, waits for them, and re-layouts  1.91 us (1%)
    all_to_all x6, blocking collectives, exchange(): return lax.all_to_all(value, ALL, 0, 0)  61.3 us
    all_to_all x7, waiting for transfers between devices, exchange(): return lax.all_to_all(value, ALL, 0, 0)  41.2 us
    pallas_call x25, Pallas kernels, call(): pl.pallas_call(kernel, out_shape=[pltpu.VMEM(o, F32) for o in outs] if ma...  26.7 us
    all_to_all x7, starting transfers between devices, exchange(): return lax.all_to_all(value, ALL, 0, 0)  26.4 us
    ppermute x9, waiting for transfers between devices, shifted(): lax.ppermute(value, 'grp', [((i + shift) % grp, i) for i in range(grp)])  8.31 us
  transfers between devices with their start and end apart: 16, of which 14 were waited for; matrix products, arithmetic and copies ran while one was open for 0% of the time, Pallas kernels for 8%

profile of v3, /device:TPU:0, one launch (start us, length us, event | category | flops | bytes accessed | tf_op | source)
XLA Modules:
  0.0 167.8 jit_solution(10210761353257531695)
XLA Ops:
  4.5 7.2 %all-to-all-start = ((f32[32,8,128]{2,1,0:T(8,128)}), f32[32,8,128]{2,1,0:T(8,128)S(1)}, u32[]{:S(2)}, u32[]{:S(2)}) async-start(f32[32,8,128]{2,1,0:T(8,128)} %shard_map.37), calls=%async_computation | async-start | bytes 262144 | tf_op jit(solution)/shard_map/all_to_all | solution.py:188
  11.7 7.8 %all-to-all-done.refs_1_ = f32[32,8,128]{2,1,0:T(8,128)S(1)} async-done(((f32[32,8,128]{2,1,0:T(8,128)}), f32[32,8,128]{2,1,0:T(8,128)S(1)}, u32[]{:S(2)}, u32[]{:S(2)}) %all-to-all-start) | async-done | bytes 131104 | tf_op jit(solution)/shard_map/all_to_all | solution.py:188
  22.9 7.6 %all-to-all-done.1.recv_ref = f32[32,8,128]{2,1,0:T(8,128)S(1)} async-done(((f32[32,8,128]{2,1,0:T(8,128)}), f32[32,8,128]{2,1,0:T(8,128)S(1)}, u32[]{:S(2)}, u32[]{:S(2)}) %all-to-all-start.1) | async-done | bytes 131104 | tf_op jit(solution)/shard_map/all_to_all | solution.py:188
  32.6 10.3 %all_to_all.65.refs_1_ = f32[32,3,4,128]{3,2,1,0:T(4,128)S(1)} all-to-all(f32[32,3,4,128]{3,2,1,0:T(4,128)S(1)} %shard_map.40), channel_id=1, replica_groups=mesh['side'=2,'grp'=2,'pts'=8] {'side','grp','pts'}, dimensions={0} | all-to-all | bytes 393216 | tf_op jit(solution)/shard_map/all_to_all | solution.py:188
  43.6 3.3 %all-to-all-start.3 = ((f32[32,8,128]{2,1,0:T(8,128)}), f32[32,8,128]{2,1,0:T(8,128)S(1)}, u32[]{:S(2)}, u32[]{:S(2)}) async-start(f32[32,8,128]{2,1,0:T(8,128)} %get-tuple-element.17), calls=%async_computation.3 | async-start | bytes 262144 | tf_op jit(solution)/shard_map/all_to_all | solution.py:188
  47.0 2.6 %shard_map.43 = f32[32,128]{1,0:T(8,128)S(1)} custom-call(f32[8,128]{1,0:T(8,128)S(1)} %get-tuple-element.18.refs_0_), custom_call_target="tpu_custom_call" | custom-call | flops 33554432 | bytes 4096 | tf_op jit(solution)/shard_map/pallas_call | solution.py:178
  49.6 5.2 %all-to-all-done.3.recv_ref = f32[32,8,128]{2,1,0:T(8,128)S(1)} async-done(((f32[32,8,128]{2,1,0:T(8,128)}), f32[32,8,128]{2,1,0:T(8,128)S(1)}, u32[]{:S(2)}, u32[]{:S(2)}) %all-to-all-start.3) | async-done | bytes 131104 | tf_op jit(solution)/shard_map/all_to_all | solution.py:188
  57.0 10.4 %all_to_all.66.refs_1_ = f32[32,3,4,128]{3,2,1,0:T(4,128)S(1)} all-to-all(f32[32,3,4,128]{3,2,1,0:T(4,128)S(1)} %shard_map.44), channel_id=1, replica_groups=mesh['side'=2,'grp'=2,'pts'=8] {'side','grp','pts'}, dimensions={0} | all-to-all | bytes 393216 | tf_op jit(solution)/shard_map/all_to_all | solution.py:188
  68.1 3.3 %all-to-all-start.5 = ((f32[32,8,128]{2,1,0:T(8,128)}), f32[32,8,128]{2,1,0:T(8,128)S(1)}, u32[]{:S(2)}, u32[]{:S(2)}) async-start(f32[32,8,128]{2,1,0:T(8,128)} %get-tuple-element.19), calls=%async_computation.5 | async-start | bytes 262144 | tf_op jit(solution)/shard_map/all_to_all | solution.py:188
  74.1 5.2 %all-to-all-done.5.recv_ref = f32[32,8,128]{2,1,0:T(8,128)S(1)} async-done(((f32[32,8,128]{2,1,0:T(8,128)}), f32[32,8,128]{2,1,0:T(8,128)S(1)}, u32[]{:S(2)}, u32[]{:S(2)}) %all-to-all-start.5) | async-done | bytes 131104 | tf_op jit(solution)/shard_map/all_to_all | solution.py:188
  81.5 10.4 %all_to_all.67.refs_1_ = f32[32,3,4,128]{3,2,1,0:T(4,128)S(1)} all-to-all(f32[32,3,4,128]{3,2,1,0:T(4,128)S(1)} %shard_map.48), channel_id=1, replica_groups=mesh['side'=2,'grp'=2,'pts'=8] {'side','grp','pts'}, dimensions={0} | all-to-all | bytes 393216 | tf_op jit(solution)/shard_map/all_to_all | solution.py:188
  92.6 3.3 %all-to-all-start.7 = ((f32[32,8,128]{2,1,0:T(8,128)}), f32[32,8,128]{2,1,0:T(8,128)S(1)}, u32[]{:S(2)}, u32[]{:S(2)}) async-start(f32[32,8,128]{2,1,0:T(8,128)} %get-tuple-element.21), calls=%async_computation.7 | async-start | bytes 262144 | tf_op jit(solution)/shard_map/all_to_all | solution.py:188
  95.9 2.6 %shard_map.51 = f32[32,128]{1,0:T(8,128)S(1)} custom-call(f32[8,128]{1,0:T(8,128)S(1)} %get-tuple-element.22.refs_0_), custom_call_target="tpu_custom_call" | custom-call | flops 33554432 | bytes 4096 | tf_op jit(solution)/shard_map/pallas_call | solution.py:178
  98.6 5.2 %all-to-all-done.7.recv_ref = f32[32,8,128]{2,1,0:T(8,128)S(1)} async-done(((f32[32,8,128]{2,1,0:T(8,128)}), f32[32,8,128]{2,1,0:T(8,128)S(1)}, u32[]{:S(2)}, u32[]{:S(2)}) %all-to-all-start.7) | async-done | bytes 131104 | tf_op jit(solution)/shard_map/all_to_all | solution.py:188
  106.0 10.4 %all_to_all.68.refs_1_ = f32[32,3,4,128]{3,2,1,0:T(4,128)S(1)} all-to-all(f32[32,3,4,128]{3,2,1,0:T(4,128)S(1)} %shard_map.52), channel_id=1, replica_groups=mesh['side'=2,'grp'=2,'pts'=8] {'side','grp','pts'}, dimensions={0} | all-to-all | bytes 393216 | tf_op jit(solution)/shard_map/all_to_all | solution.py:188
  117.1 3.3 %all-to-all-start.9 = ((f32[32,8,128]{2,1,0:T(8,128)}), f32[32,8,128]{2,1,0:T(8,128)S(1)}, u32[]{:S(2)}, u32[]{:S(2)}) async-start(f32[32,8,128]{2,1,0:T(8,128)} %get-tuple-element.23), calls=%async_computation.9 | async-start | bytes 262144 | tf_op jit(solution)/shard_map/all_to_all | solution.py:188
  120.4 2.6 %shard_map.55 = f32[32,128]{1,0:T(8,128)S(1)} custom-call(f32[8,128]{1,0:T(8,128)S(1)} %get-tuple-element.24.refs_0_), custom_call_target="tpu_custom_call" | custom-call | flops 33554432 | bytes 4096 | tf_op jit(solution)/shard_map/pallas_call | solution.py:178
  123.1 5.2 %all-to-all-done.9.recv_ref = f32[32,8,128]{2,1,0:T(8,128)S(1)} async-done(((f32[32,8,128]{2,1,0:T(8,128)}), f32[32,8,128]{2,1,0:T(8,128)S(1)}, u32[]{:S(2)}, u32[]{:S(2)}) %all-to-all-start.9) | async-done | bytes 131104 | tf_op jit(solution)/shard_map/all_to_all | solution.py:188
  130.5 10.4 %all_to_all.69.refs_1_ = f32[32,3,4,128]{3,2,1,0:T(4,128)S(1)} all-to-all(f32[32,3,4,128]{3,2,1,0:T(4,128)S(1)} %shard_map.56), channel_id=1, replica_groups=mesh['side'=2,'grp'=2,'pts'=8] {'side','grp','pts'}, dimensions={0} | all-to-all | bytes 393216 | tf_op jit(solution)/shard_map/all_to_all | solution.py:188
  141.6 3.3 %all-to-all-start.11 = ((f32[32,8,128]{2,1,0:T(8,128)}), f32[32,8,128]{2,1,0:T(8,128)S(1)}, u32[]{:S(2)}, u32[]{:S(2)}) async-start(f32[32,8,128]{2,1,0:T(8,128)} %get-tuple-element.25), calls=%async_computation.11 | async-start | bytes 262144 | tf_op jit(solution)/shard_map/all_to_all | solution.py:188
  144.9 2.6 %shard_map.59 = f32[32,128]{1,0:T(8,128)S(1)} custom-call(f32[8,128]{1,0:T(8,128)S(1)} %get-tuple-element.26.refs_0_), custom_call_target="tpu_custom_call" | custom-call | flops 33554432 | bytes 4096 | tf_op jit(solution)/shard_map/pallas_call | solution.py:178
  147.6 5.2 %all-to-all-done.11.recv_ref = f32[32,8,128]{2,1,0:T(8,128)S(1)} async-done(((f32[32,8,128]{2,1,0:T(8,128)}), f32[32,8,128]{2,1,0:T(8,128)S(1)}, u32[]{:S(2)}, u32[]{:S(2)}) %all-to-all-start.11) | async-done | bytes 131104 | tf_op jit(solution)/shard_map/all_to_all | solution.py:188
  154.9 9.4 %all_to_all.70.refs_1_ = f32[32,4,128]{2,1,0:T(4,128)S(1)} all-to-all(f32[32,4,128]{2,1,0:T(4,128)S(1)} %get-tuple-element.27), channel_id=1, replica_groups=mesh['side'=2,'grp'=2,'pts'=8] {'side','grp','pts'}, dimensions={0} | all-to-all | bytes 131072 | tf_op jit(solution)/shard_map/all_to_all | solution.py:188
  164.4 2.8 %shard_map.61 = f32[32,256]{1,0:T(8,128)S(1)} custom-call(s32[1]{0:T(128)} %bitcast.refs_0_, f32[32,4,128]{2,1,0:T(4,128)S(1)} %all_to_all.70.refs_1_, f32[32,256]{1,0:T(8,128)S(1)} %get-tuple-element.28.refs_2_), custom_call_target="tpu_custom_call" | custom-call | tf_op jit(solution)/shard_map/pallas_call | solution.py:178
  (55 shorter events, 27.8 us)
Async XLA Ops:
  0.0 1.8 %copy-start = (f32[1,32,256]{2,1,0:T(8,128)S(1)}, f32[1,32,256]{2,1,0:T(8,128)}, u32[]{:S(2)}) copy-start(f32[1,32,256]{2,1,0:T(8,128)} %param.5) | copy-start | bytes 98308
  0.0 1.8 %copy-start.1 = (f32[1,256]{1,0:T(1,128)S(1)}, f32[1,256]{1,0:T(1,128)}, u32[]{:S(2)}) copy-start(f32[1,256]{1,0:T(1,128)} %param.4) | copy-start | bytes 3076
  1.3 2.2 %collective-permute-start.1 = (bf16[256,1024]{1,0:T(8,128)(2,1)S(1)}, bf16[256,1024]{1,0:T(8,128)(2,1)S(1)}, u32[]{:S(2)}, u32[]{:S(2)}) collective-permute-start(bf16[256,1024]{1,0:T(8,128)(2,1)S(1)} %get-tuple-element.30), channel_id=1, source_target_pairs={{8,0},{0,8},{9,1},{1,9},{10,2},{2,10},{11,3},{3,11},{12,4},{4,12},... | collective-permute-start | bytes 1572872 | tf_op jit(solution)/shard_map/ppermute | solution.py:193
  1.9 1.6 collective-permute-start
  4.5 15.0 %all-to-all-start = ((f32[32,8,128]{2,1,0:T(8,128)}), f32[32,8,128]{2,1,0:T(8,128)S(1)}, u32[]{:S(2)}, u32[]{:S(2)}) async-start(f32[32,8,128]{2,1,0:T(8,128)} %shard_map.37), calls=%async_computation | async-start | bytes 262144 | tf_op jit(solution)/shard_map/all_to_all | solution.py:188
  20.2 10.4 %all-to-all-start.1 = ((f32[32,8,128]{2,1,0:T(8,128)}), f32[32,8,128]{2,1,0:T(8,128)S(1)}, u32[]{:S(2)}, u32[]{:S(2)}) async-start(f32[32,8,128]{2,1,0:T(8,128)} %shard_map.38), calls=%async_computation.1 | async-start | bytes 262144 | tf_op jit(solution)/shard_map/all_to_all | solution.py:188
  22.7 8.4 %collective-permute-start.3 = (f32[1,256]{1,0:T(1,128)S(1)}, f32[1,256]{1,0:T(1,128)S(1)}, u32[]{:S(2)}, u32[]{:S(2)}) collective-permute-start(f32[1,256]{1,0:T(1,128)S(1)} %copy-done.1), channel_id=1, source_target_pairs={{8,0},{0,8},{9,1},{1,9},{10,2},{2,10},{11,3},{3,11},{12,4},{4,12},... | collective-permute-start | bytes 3080 | tf_op jit(solution)/shard_map/ppermute | solution.py:193
  31.0 1.3 collective-permute-start.2
  43.6 11.1 %all-to-all-start.3 = ((f32[32,8,128]{2,1,0:T(8,128)}), f32[32,8,128]{2,1,0:T(8,128)S(1)}, u32[]{:S(2)}, u32[]{:S(2)}) async-start(f32[32,8,128]{2,1,0:T(8,128)} %get-tuple-element.17), calls=%async_computation.3 | async-start | bytes 262144 | tf_op jit(solution)/shard_map/all_to_all | solution.py:188
  55.2 1.3 collective-permute-start.4
  68.1 11.1 %all-to-all-start.5 = ((f32[32,8,128]{2,1,0:T(8,128)}), f32[32,8,128]{2,1,0:T(8,128)S(1)}, u32[]{:S(2)}, u32[]{:S(2)}) async-start(f32[32,8,128]{2,1,0:T(8,128)} %get-tuple-element.19), calls=%async_computation.5 | async-start | bytes 262144 | tf_op jit(solution)/shard_map/all_to_all | solution.py:188
  79.7 1.3 collective-permute-start.5
  92.6 11.1 %all-to-all-start.7 = ((f32[32,8,128]{2,1,0:T(8,128)}), f32[32,8,128]{2,1,0:T(8,128)S(1)}, u32[]{:S(2)}, u32[]{:S(2)}) async-start(f32[32,8,128]{2,1,0:T(8,128)} %get-tuple-element.21), calls=%async_computation.7 | async-start | bytes 262144 | tf_op jit(solution)/shard_map/all_to_all | solution.py:188
  104.2 1.3 collective-permute-start.6
  117.1 11.1 %all-to-all-start.9 = ((f32[32,8,128]{2,1,0:T(8,128)}), f32[32,8,128]{2,1,0:T(8,128)S(1)}, u32[]{:S(2)}, u32[]{:S(2)}) async-start(f32[32,8,128]{2,1,0:T(8,128)} %get-tuple-element.23), calls=%async_computation.9 | async-start | bytes 262144 | tf_op jit(solution)/shard_map/all_to_all | solution.py:188
  128.7 1.3 collective-permute-start.7
  141.6 11.1 %all-to-all-start.11 = ((f32[32,8,128]{2,1,0:T(8,128)}), f32[32,8,128]{2,1,0:T(8,128)S(1)}, u32[]{:S(2)}, u32[]{:S(2)}) async-start(f32[32,8,128]{2,1,0:T(8,128)} %get-tuple-element.25), calls=%async_computation.11 | async-start | bytes 262144 | tf_op jit(solution)/shard_map/all_to_all | solution.py:188
  153.2 1.3 collective-permute-start.8

commit v4 on v3

--- a/solution.py
+++ b/solution.py
@@ -49,11 +49,29 @@
     row = lax.broadcasted_iota(jnp.int32, (modes, LANES), 0)
     lane = lax.broadcasted_iota(jnp.int32, (modes, LANES), 1)
     work = gram + jnp.where(lane == row + modes, 1.0, 0.0)
-    for k in range(modes):
-        top = work[k : k + 1]
-        pivot = top[:, k : k + 1]
-        factor = jnp.where(row > k, work[:, k : k + 1] / pivot, 0.0)
-        work = work - factor * top
+    for k in range(0, modes, ROWS):
+        rows = [work[k + j : k + j + 1] for j in range(ROWS)]
+        columns = [
+            jnp.broadcast_to(work[:, k + j : k + j + 1], (modes, LANES)) for j in range(ROWS)
+        ]
+        block = {
+            (i, j): jnp.broadcast_to(rows[i][:, k + j : k + j + 1], (1, LANES))
+            for i in range(ROWS)
+            for j in range(i, ROWS)
+        }
+        factors = []
+        for j in range(ROWS):
+            inverse = 1.0 / block[j, j]
+            factor = jnp.where(row > k + j, columns[j] * inverse, 0.0)
+            factors.append(factor)
+            for i in range(j + 1, ROWS):
+                columns[i] = columns[i] - factor * block[j, i]
+                ratio = block[j, i] * inverse
+                for c in range(i, ROWS):
+                    block[i, c] = block[i, c] - ratio * block[j, c]
+                rows[i] = rows[i] - ratio * rows[j]
+        for j in range(ROWS):
+            work = work - factors[j] * rows[j]
     pivots = jnp.sum(jnp.where(lane == row, work, 0.0), axis=1, keepdims=True)
     inverse = pltpu.roll(work, LANES - modes, 1) / jnp.sqrt(pivots)
     return jnp.where(lane < modes, inverse, 0.0)
@@ -89,8 +107,31 @@
     return jnp.concatenate(slabs, axis=0)
 
 
-def first_kernel(weighted_ref, field_ref, send_ref):
-    store_tiles(send_ref, dot_wide(weighted_ref[...], field_ref[...], 0))
+def setup_kernel(place_ref, fields_ref, weight_ref, modes_ref, pack_ref, *rest):
+    *block_refs, sems = rest
+    grp, columns = len(block_refs), block_refs[0].shape[1]
+    copies = []
+    for k in reversed(range(grp)):
+        start = pl.multiple_of(lax.rem(place_ref[0] + grp - k, grp) * columns, LANES)
+        copies.append(
+            pltpu.make_async_copy(
+                fields_ref.at[0, :, pl.ds(start, columns)], block_refs[k], sems.at[k]
+            )
+        )
+        copies[-1].start()
+    modes = modes_ref.shape[1]
+    pack_ref[:modes] = modes_ref[0]
+    pack_ref[modes:] = jnp.broadcast_to(weight_ref[...], (ROWS, weight_ref.shape[1]))
+    for copy in copies:
+        copy.wait()
+
+
+def first_kernel(*refs):
+    *pack_refs, field_ref, send_ref, weight_ref = refs
+    pack = jnp.concatenate([ref[...] for ref in pack_refs], axis=1)
+    weight = pack[-ROWS:]
+    weight_ref[...] = weight
+    store_tiles(send_ref, dot_wide(pack[:-ROWS] * weight[:1], field_ref[...], 0))
 
 
 def reduce_kernel(side_ref, recv_ref, send_ref, *gram_ref, grp, pts):
@@ -105,7 +146,7 @@
                 slabs.append(total)
             total = jnp.concatenate(slabs, axis=0) if gram_ref else slabs[0]
             for p in range(pts):
-                send_ref[((1 - s) * grp + c) * pts + p] = total
+                send_ref[((1 - s) * grp + c) * pts + p] = total.astype(send_ref.dtype)
     if gram_ref:
         first = (1 - side_ref[0]) * (grp * pts)
         gram_ref[0][...] = whole_tile(lambda d: recv_ref[d, grp], first, grp, pts)
@@ -125,7 +166,12 @@
         ],
         axis=0,
     )
-    out_ref[...] = dot_wide(coeffs, field_ref[...], 1)
+    if coeffs.dtype == BF16:
+        out_ref[...] = lax.dot_general(
+            coeffs, field_ref[...], (((1,), (1,)), ((), ())), preferred_element_type=F32
+        )
+    else:
+        out_ref[...] = dot_wide(coeffs, field_ref[...], 1)
 
 
 def map_kernel(*refs, samples, others, has_factor, last):
@@ -139,10 +185,10 @@
         cut = (others - k) * block
         mapped = mapped + jnp.concatenate([other[:, cut:], other[:, :cut]], axis=1)
     factor = refs.pop(0)[...][:, :modes] if has_factor else None
-    weight = refs.pop(0)[...]
+    weight = refs.pop(0)[:1]
     if has_factor:
         mapped = jnp.dot(factor, mapped, precision=HIGHEST, preferred_element_type=F32)
-    mapped = mapped * weight if has_factor else mapped * weight / samples
+    mapped = mapped * weight / samples
     padded = jnp.concatenate([mapped, jnp.zeros((LANES - modes, points), F32)], axis=0)
     gram = lax.dot_general(
         mapped, padded, (((1,), (1,)), ((), ())), precision=HIGHEST, preferred_element_type=F32
@@ -168,20 +214,31 @@
     out_ref[...] = jnp.dot(factor, mapped, precision=HIGHEST, preferred_element_type=F32)
 
 
-def call(kernel, outs, *args, cost=None):
+def call(kernel, outs, *args):
     specs = [SMEM if a.dtype == jnp.int32 else VMEM for a in args]
     args = [
         a if a.dtype == jnp.int32 else pltpu.with_memory_space_constraint(a, pltpu.VMEM)
         for a in args
     ]
-    many = isinstance(outs, list)
+    out = [o if isinstance(o, jax.ShapeDtypeStruct) else pltpu.VMEM(*o) for o in outs]
+    result = pl.pallas_call(
+        kernel, out_shape=out, in_specs=specs, out_specs=[VMEM for _ in out]
+    )(*args)
+    return result if len(out) > 1 else result[0]
+
+
+def cut(place, fields, weight, modes, grp):
+    _, points, samples = fields.shape
+    out = [pltpu.VMEM((modes.shape[1] + ROWS, points), F32)]
+    out += [pltpu.VMEM((points, samples // grp), fields.dtype) for _ in range(grp)]
+    anywhere = pl.BlockSpec(memory_space=pl.ANY)
     return pl.pallas_call(
-        kernel,
-        out_shape=[pltpu.VMEM(o, F32) for o in outs] if many else pltpu.VMEM(outs, F32),
-        in_specs=specs,
-        out_specs=[VMEM for _ in outs] if many else VMEM,
-        cost_estimate=cost,
-    )(*args)
+        setup_kernel,
+        out_shape=out,
+        in_specs=[SMEM, anywhere, VMEM, VMEM],
+        out_specs=[VMEM for _ in out],
+        scratch_shapes=[pltpu.SemaphoreType.DMA((grp,))],
+    )(place, fields, weight, modes)
 
 
 def exchange(value):
@@ -194,59 +251,49 @@
 
 
 def body_tiles(fields, point_weight, start_modes):
-    local_field, weight, modes0 = fields[0], point_weight, start_modes[0]
-    modes, samples = modes0.shape[0], local_field.shape[1]
+    modes, samples = start_modes.shape[1], fields.shape[2]
     grp, pts = lax.axis_size("grp"), lax.axis_size("pts")
     devices = 2 * grp * pts
-    total_points = local_field.shape[0] * grp * pts
-    columns = samples // grp
+    total_points = fields.shape[1] * grp * pts
+    points = fields.shape[1] * grp
     place = lax.axis_index("grp").astype(jnp.int32).reshape(1)
     side = lax.axis_index("side").astype(jnp.int32).reshape(1)
 
-    def part(member):
-        member = member[0]
-        return lax.dynamic_slice_in_dim(local_field, (member % grp) * columns, columns, 1)
-
-    weighted = modes0 * weight
-    blocks, weights, starts = [part(place)], [weight], [weighted]
-    for k in range(1, grp):
-        blocks.append(shifted(part(place - k), k))
-        weights.append(shifted(weight, k))
-        starts.append(shifted(weighted, k))
-    field = jnp.concatenate(blocks, axis=0)
-    weight = jnp.concatenate(weights, axis=1)
-    start = jnp.concatenate(starts, axis=1)
-    points = weight.shape[1]
-
-    def reduced(recv, has_gram):
-        shapes = [(devices, ROWS, LANES)] + [(ROWS, LANES)] * has_gram
+    pack, *blocks = cut(place, fields, point_weight, start_modes, grp)
+    packs = [pack] + [shifted(pack, k) for k in range(1, grp)]
+    field = jnp.concatenate(
+        [blocks[0]] + [shifted(blocks[k], k) for k in range(1, grp)], axis=0
+    )
+    tile = (devices, ROWS, LANES)
+    slabs = (devices, grp + 1, ROWS // grp, LANES)
+
+    factor = None
+    send, weight = call(first_kernel, [(tile, F32), ((ROWS, points), F32)], *packs, field)
+    for iteration in range(ITERS):
+        has_gram, last = iteration > 0, iteration == ITERS - 1
         kernel = lambda *refs: reduce_kernel(*refs, grp=grp, pts=pts)
-        return call(kernel, shapes, side, recv)
-
-    factor = None
-    send = call(first_kernel, (devices, ROWS, LANES), start, field)
-    for iteration in range(ITERS):
-        has_gram = iteration > 0
-        out = reduced(exchange(send), has_gram)
-        gathered = exchange(out[0])
+        if has_gram:
+            outs = [(tile, F32), ((ROWS, LANES), F32)]
+            summed, gram = call(kernel, outs, side, exchange(send))
+        else:
+            summed = call(kernel, [(tile, BF16)], side, exchange(send))
+        own = call(back_kernel, [((modes, points), F32)], exchange(summed), field)
+        others = [shifted(own, k) for k in range(1, grp)]
         if has_gram:
             kernel = lambda *refs: factor_kernel(*refs, modes=modes, points=total_points)
-            cost = pl.CostEstimate(flops=modes**3 << 10, bytes_accessed=ROWS * LANES * 4, transcendentals=0)
-            factor = call(kernel, (modes, LANES), out[1], cost=cost) / samples
-        own = call(back_kernel, (modes, points), gathered, field)
-        others = [shifted(own, k) for k in range(1, grp)]
-        last = iteration == ITERS - 1
+            factor = call(kernel, [((modes, LANES), F32)], gram)
         kernel = lambda *refs: map_kernel(
             *refs, samples=samples, others=grp - 1, has_factor=has_gram, last=last
         )
         given = [place, own, *others, *([factor] if has_gram else []), weight]
         if last:
-            shapes = [(modes, points // grp), (devices, ROWS // grp, LANES)]
-            mapped, send = call(kernel, shapes, *given)
+            outs = [((modes, points // grp), F32), ((devices, ROWS // grp, LANES), F32)]
+            mapped, send = call(kernel, outs, *given)
         else:
-            send = call(kernel, (devices, grp + 1, ROWS // grp, LANES), *given, field)
+            send = call(kernel, [(slabs, F32)], *given, field)
     kernel = lambda *refs: finish_kernel(*refs, grp=grp, pts=pts, points=total_points)
-    return call(kernel, (modes, points // grp), side, exchange(send), mapped)[None]
+    out = jax.ShapeDtypeStruct((modes, points // grp), F32)
+    return call(kernel, [out], side, exchange(send), mapped)[None]
 
 
 def body_sums(fields, point_weight, start_modes):

time: 168 us -> 161 us (0.958)
  blocking collectives: 61.3 us -> 125 us
  waiting for transfers between devices: 49.5 us -> 12 us
  starting transfers between devices: 28.1 us -> 8.66 us
  Pallas kernels: 26.7 us -> 14.4 us
  local copies, waits for them, and re-layouts: 1.91 us -> 0.07 us
    all_to_all x6 -> x12, blocking collectives: 61.3 us -> 125 us  [exchange(): return lax.all_to_all(value, ALL, 0, 0)]
    all_to_all x7 -> x1, waiting for transfers between devices: 41.2 us -> 7.8 us  [exchange(): return lax.all_to_all(value, ALL, 0, 0)]
    all_to_all x7 -> x1, starting transfers between devices: 26.4 us -> 7.21 us  [exchange(): return lax.all_to_all(value, ALL, 0, 0)]
    pallas_call x25 -> x26, Pallas kernels: 26.7 us -> 14.4 us  [the longest x25 12.4 us: call(): pl.pallas_call(kernel, out_shape=out, in_specs=specs, out_specs=[VMEM for...]
    ppermute x9 -> x8, waiting for transfers between devices: 8.31 us -> 4.21 us  [shifted(): lax.ppermute(value, 'grp', [((i + shift) % grp, i) for i in range(grp)])]
  transfers between devices with their start and end apart: 16 -> 9, of which waited for: 14 -> 8; matrix products, arithmetic and copies ran while one was open for 0% -> 0% of each run, Pallas kernels for 8% -> 3%
where the time goes in v4:
time: 161 us; the launch traced here: 160 us
  blocking collectives  125 us (78%)
  Pallas kernels  14.4 us (9%)
  waiting for transfers between devices  12 us (7%)
  starting transfers between devices  8.66 us (5%)
    all_to_all x12, blocking collectives, exchange(): return lax.all_to_all(value, ALL, 0, 0)  125 us
    pallas_call x25, Pallas kernels, call(): pl.pallas_call(kernel, out_shape=out, in_specs=specs, out_specs=[VMEM for...  12.4 us
    all_to_all x1, waiting for transfers between devices, exchange(): return lax.all_to_all(value, ALL, 0, 0)  7.8 us
    all_to_all x1, starting transfers between devices, exchange(): return lax.all_to_all(value, ALL, 0, 0)  7.21 us
    ppermute x8, waiting for transfers between devices, shifted(): lax.ppermute(value, 'grp', [((i + shift) % grp, i) for i in range(grp)])  4.21 us
  transfers between devices with their start and end apart: 9, of which 8 were waited for; matrix products, arithmetic and copies ran while one was open for 0% of the time, Pallas kernels for 3%

profile of v4, /device:TPU:0, one launch (start us, length us, event | category | flops | bytes accessed | tf_op | source)
XLA Modules:
  0.0 160.3 jit_solution(11859019489104355804)
XLA Ops:
  0.0 2.0 %shard_map.37 = (f32[40,256]{1,0:T(8,128)S(1)}, bf16[256,1024]{1,0:T(8,128)(2,1)S(1)}, bf16[256,1024]{1,0:T(8,128)(2,1)S(1)}) custom-call(s32[1]{0:T(128)} %bitcast.1.place_ref.refs_0_, bf16[1,256,2048]{2,1,0:T(8,128)(2,1)} %fields_ref.1, f32[1,256]{1,0:T(1,128)} %weight_ref.1, f32[1,32,256]{2,1,0:T(8,128)} %modes_ref.1), custom_call_target="tpu_custom_call" | custom-call | tf_op jit(solution)/shard_map/pallas_call | solution.py:235
  2.7 1.4 collective-permute-done.1
  4.2 1.0 shard_map.38
  5.1 7.2 %all-to-all-start = ((f32[32,8,128]{2,1,0:T(8,128)}), f32[32,8,128]{2,1,0:T(8,128)S(1)}, u32[]{:S(2)}, u32[]{:S(2)}) async-start(f32[32,8,128]{2,1,0:T(8,128)} %get-tuple-element.25), calls=%async_computation | async-start | bytes 262144 | tf_op jit(solution)/shard_map/all_to_all | solution.py:245
  12.3 7.8 %all-to-all-done.refs_1_ = f32[32,8,128]{2,1,0:T(8,128)S(1)} async-done(((f32[32,8,128]{2,1,0:T(8,128)}), f32[32,8,128]{2,1,0:T(8,128)S(1)}, u32[]{:S(2)}, u32[]{:S(2)}) %all-to-all-start) | async-done | bytes 131104 | tf_op jit(solution)/shard_map/all_to_all | solution.py:245
  20.2 9.4 %all_to_all.65.recv_ref = bf16[32,8,128]{2,1,0:T(8,128)(2,1)S(1)} all-to-all(bf16[32,8,128]{2,1,0:T(8,128)(2,1)S(1)} %shard_map.39), channel_id=1, replica_groups=mesh['side'=2,'grp'=2,'pts'=8] {'side','grp','pts'}, dimensions={0} | all-to-all | bytes 131072 | tf_op jit(solution)/shard_map/all_to_all | solution.py:245
  30.1 1.1 collective-permute-done.2.refs_2_
  31.6 9.9 %all_to_all.66.refs_1_ = f32[32,3,4,128]{3,2,1,0:T(4,128)S(1)} all-to-all(f32[32,3,4,128]{3,2,1,0:T(4,128)S(1)} %shard_map.41), channel_id=1, replica_groups=mesh['side'=2,'grp'=2,'pts'=8] {'side','grp','pts'}, dimensions={0} | all-to-all | bytes 393216 | tf_op jit(solution)/shard_map/all_to_all | solution.py:245
  41.6 10.8 %all_to_all.67.recv_ref = f32[32,8,128]{2,1,0:T(8,128)S(1)} all-to-all(f32[32,8,128]{2,1,0:T(8,128)S(1)} %get-tuple-element.27), channel_id=1, replica_groups=mesh['side'=2,'grp'=2,'pts'=8] {'side','grp','pts'}, dimensions={0} | all-to-all | bytes 262144 | tf_op jit(solution)/shard_map/all_to_all | solution.py:245
  53.0 0.8 shard_map.44.refs_3_
  54.7 10.4 %all_to_all.68.refs_1_ = f32[32,3,4,128]{3,2,1,0:T(4,128)S(1)} all-to-all(f32[32,3,4,128]{3,2,1,0:T(4,128)S(1)} %shard_map.45), channel_id=1, replica_groups=mesh['side'=2,'grp'=2,'pts'=8] {'side','grp','pts'}, dimensions={0} | all-to-all | bytes 393216 | tf_op jit(solution)/shard_map/all_to_all | solution.py:245
  65.2 10.9 %all_to_all.69.recv_ref = f32[32,8,128]{2,1,0:T(8,128)S(1)} all-to-all(f32[32,8,128]{2,1,0:T(8,128)S(1)} %get-tuple-element.29), channel_id=1, replica_groups=mesh['side'=2,'grp'=2,'pts'=8] {'side','grp','pts'}, dimensions={0} | all-to-all | bytes 262144 | tf_op jit(solution)/shard_map/all_to_all | solution.py:245
  76.7 0.8 shard_map.48.refs_3_
  78.4 10.4 %all_to_all.70.refs_1_ = f32[32,3,4,128]{3,2,1,0:T(4,128)S(1)} all-to-all(f32[32,3,4,128]{3,2,1,0:T(4,128)S(1)} %shard_map.49), channel_id=1, replica_groups=mesh['side'=2,'grp'=2,'pts'=8] {'side','grp','pts'}, dimensions={0} | all-to-all | bytes 393216 | tf_op jit(solution)/shard_map/all_to_all | solution.py:245
  88.8 10.9 %all_to_all.71.recv_ref = f32[32,8,128]{2,1,0:T(8,128)S(1)} all-to-all(f32[32,8,128]{2,1,0:T(8,128)S(1)} %get-tuple-element.31), channel_id=1, replica_groups=mesh['side'=2,'grp'=2,'pts'=8] {'side','grp','pts'}, dimensions={0} | all-to-all | bytes 262144 | tf_op jit(solution)/shard_map/all_to_all | solution.py:245
  100.3 0.8 shard_map.52.refs_3_
  102.0 10.4 %all_to_all.72.refs_1_ = f32[32,3,4,128]{3,2,1,0:T(4,128)S(1)} all-to-all(f32[32,3,4,128]{3,2,1,0:T(4,128)S(1)} %shard_map.53), channel_id=1, replica_groups=mesh['side'=2,'grp'=2,'pts'=8] {'side','grp','pts'}, dimensions={0} | all-to-all | bytes 393216 | tf_op jit(solution)/shard_map/all_to_all | solution.py:245
  112.4 10.9 %all_to_all.73.recv_ref = f32[32,8,128]{2,1,0:T(8,128)S(1)} all-to-all(f32[32,8,128]{2,1,0:T(8,128)S(1)} %get-tuple-element.33), channel_id=1, replica_groups=mesh['side'=2,'grp'=2,'pts'=8] {'side','grp','pts'}, dimensions={0} | all-to-all | bytes 262144 | tf_op jit(solution)/shard_map/all_to_all | solution.py:245
  124.0 0.8 shard_map.56.refs_3_
  125.7 10.4 %all_to_all.74.refs_1_ = f32[32,3,4,128]{3,2,1,0:T(4,128)S(1)} all-to-all(f32[32,3,4,128]{3,2,1,0:T(4,128)S(1)} %shard_map.57), channel_id=1, replica_groups=mesh['side'=2,'grp'=2,'pts'=8] {'side','grp','pts'}, dimensions={0} | all-to-all | bytes 393216 | tf_op jit(solution)/shard_map/all_to_all | solution.py:245
  136.1 10.9 %all_to_all.75.recv_ref = f32[32,8,128]{2,1,0:T(8,128)S(1)} all-to-all(f32[32,8,128]{2,1,0:T(8,128)S(1)} %get-tuple-element.35), channel_id=1, replica_groups=mesh['side'=2,'grp'=2,'pts'=8] {'side','grp','pts'}, dimensions={0} | all-to-all | bytes 262144 | tf_op jit(solution)/shard_map/all_to_all | solution.py:245
  147.6 0.8 shard_map.60.refs_3_
  149.2 9.4 %all_to_all.76.refs_1_ = f32[32,4,128]{2,1,0:T(4,128)S(1)} all-to-all(f32[32,4,128]{2,1,0:T(4,128)S(1)} %get-tuple-element.37), channel_id=1, replica_groups=mesh['side'=2,'grp'=2,'pts'=8] {'side','grp','pts'}, dimensions={0} | all-to-all | bytes 131072 | tf_op jit(solution)/shard_map/all_to_all | solution.py:245
  158.7 1.6 shard_map.62
  (34 shorter events, 8.9 us)
Async XLA Ops:
  2.0 2.1 %collective-permute-start.1 = (bf16[256,1024]{1,0:T(8,128)(2,1)S(1)}, bf16[256,1024]{1,0:T(8,128)(2,1)S(1)}, u32[]{:S(2)}, u32[]{:S(2)}) collective-permute-start(bf16[256,1024]{1,0:T(8,128)(2,1)S(1)} %get-tuple-element.24), channel_id=1, source_target_pairs={{8,0},{0,8},{9,1},{1,9},{10,2},{2,10},{11,3},{3,11},{12,4},{4,12},... | collective-permute-start | bytes 1572872 | tf_op jit(solution)/shard_map/ppermute | solution.py:250
  2.6 1.6 collective-permute-start
  5.1 15.0 %all-to-all-start = ((f32[32,8,128]{2,1,0:T(8,128)}), f32[32,8,128]{2,1,0:T(8,128)S(1)}, u32[]{:S(2)}, u32[]{:S(2)}) async-start(f32[32,8,128]{2,1,0:T(8,128)} %get-tuple-element.25), calls=%async_computation | async-start | bytes 262144 | tf_op jit(solution)/shard_map/all_to_all | solution.py:245
  30.0 1.3 collective-permute-start.2
  52.9 1.3 collective-permute-start.3
  76.5 1.3 collective-permute-start.4
  100.2 1.3 collective-permute-start.5
  123.8 1.3 collective-permute-start.6
  147.5 1.3 collective-permute-start.7

commit v5 on v4

--- a/solution.py
+++ b/solution.py
@@ -77,17 +77,13 @@
     return jnp.where(lane < modes, inverse, 0.0)
 
 
-def store_tiles(send_ref, projected):
+def store_tiles(send_ref, projected, pitch):
     columns = projected.shape[1] // LANES
-    for d in range(send_ref.shape[0]):
+    for d in range(send_ref.shape[0] // pitch):
         h, j = divmod(d, columns)
-        tile = projected[h * ROWS : (h + 1) * ROWS, j * LANES : (j + 1) * LANES]
-        if send_ref.ndim == 3:
-            send_ref[d] = tile
-            continue
-        slab = send_ref.shape[2]
-        for k in range(ROWS // slab):
-            send_ref[d, k] = tile[k * slab : (k + 1) * slab]
+        send_ref[d * pitch : d * pitch + ROWS] = projected[
+            h * ROWS : (h + 1) * ROWS, j * LANES : (j + 1) * LANES
+        ]
 
 
 def own_slab(tile, place, grp):
@@ -108,21 +104,22 @@
 
 
 def setup_kernel(place_ref, fields_ref, weight_ref, modes_ref, pack_ref, *rest):
-    *block_refs, sems = rest
+    *block_refs, row_ref, sems = rest
     grp, columns = len(block_refs), block_refs[0].shape[1]
-    copies = []
+    modes = modes_ref.shape[1]
+    pairs = [(weight_ref, row_ref), (modes_ref.at[0], pack_ref.at[:modes])]
     for k in reversed(range(grp)):
         start = pl.multiple_of(lax.rem(place_ref[0] + grp - k, grp) * columns, LANES)
-        copies.append(
-            pltpu.make_async_copy(
-                fields_ref.at[0, :, pl.ds(start, columns)], block_refs[k], sems.at[k]
-            )
-        )
-        copies[-1].start()
-    modes = modes_ref.shape[1]
-    pack_ref[:modes] = modes_ref[0]
-    pack_ref[modes:] = jnp.broadcast_to(weight_ref[...], (ROWS, weight_ref.shape[1]))
+        pairs.append((fields_ref.at[0, :, pl.ds(start, columns)], block_refs[k]))
+    copies = [
+        pltpu.make_async_copy(source, target, sems.at[i])
+        for i, (source, target) in enumerate(pairs)
+    ]
     for copy in copies:
+        copy.start()
+    copies[0].wait()
+    pack_ref[modes:] = jnp.broadcast_to(row_ref[...], (ROWS, row_ref.shape[1]))
+    for copy in copies[1:]:
         copy.wait()
 
 
@@ -131,37 +128,45 @@
     pack = jnp.concatenate([ref[...] for ref in pack_refs], axis=1)
     weight = pack[-ROWS:]
     weight_ref[...] = weight
-    store_tiles(send_ref, dot_wide(pack[:-ROWS] * weight[:1], field_ref[...], 0))
-
-
-def reduce_kernel(side_ref, recv_ref, send_ref, *gram_ref, grp, pts):
+    store_tiles(send_ref, dot_wide(pack[:-ROWS] * weight[:1], field_ref[...], 0), ROWS)
+
+
+def reduce_kernel(recv_ref, send_ref, *, grp, pts, pitch):
+    def total(first, rows):
+        parts = [recv_ref[d * pitch + rows.start : d * pitch + rows.stop] for d in
+                 range(first, first + pts)]
+        return sum(parts[1:], parts[0])
+
     for s in range(2):
+        gram = total(s * grp * pts, slice(ROWS, pitch)) if pitch > ROWS else None
         for c in range(grp):
-            first = (s * grp + c) * pts
-            slabs = []
-            for k in range(grp) if gram_ref else [...]:
-                total = recv_ref[first, k]
-                for p in range(1, pts):
-                    total = total + recv_ref[first + p, k]
-                slabs.append(total)
-            total = jnp.concatenate(slabs, axis=0) if gram_ref else slabs[0]
+            tile = total((s * grp + c) * pts, slice(0, ROWS)).astype(send_ref.dtype)
             for p in range(pts):
-                send_ref[((1 - s) * grp + c) * pts + p] = total.astype(send_ref.dtype)
-    if gram_ref:
-        first = (1 - side_ref[0]) * (grp * pts)
-        gram_ref[0][...] = whole_tile(lambda d: recv_ref[d, grp], first, grp, pts)
-
-
-def factor_kernel(gram_ref, out_ref, *, modes, points):
-    out_ref[...] = inverse_factor(unfold(gram_ref[...], modes) / points, modes)
-
-
-def back_kernel(recv_ref, field_ref, out_ref):
+                first = (((1 - s) * grp + c) * pts + p) * pitch
+                send_ref[first : first + ROWS] = tile
+                if pitch > ROWS:
+                    send_ref[first + ROWS : first + pitch] = gram
+
+
+def factor_kernel(recv_ref, out_ref, *, modes, points, pitch):
+    gram = jnp.concatenate(
+        [recv_ref[r * pitch + ROWS : (r + 1) * pitch] for r in range(ROWS)], axis=0
+    )
+    out_ref[...] = inverse_factor(unfold(gram, modes) / points, modes)
+
+
+def back_kernel(recv_ref, field_ref, out_ref, *, pitch):
     columns = field_ref.shape[1] // LANES
-    count = recv_ref.shape[0] // columns
+    count = recv_ref.shape[0] // (pitch * columns)
     coeffs = jnp.concatenate(
         [
-            jnp.concatenate([recv_ref[h * columns + j] for j in range(columns)], axis=1)
+            jnp.concatenate(
+                [
+                    recv_ref[(h * columns + j) * pitch : (h * columns + j) * pitch + ROWS]
+                    for j in range(columns)
+                ],
+                axis=1,
+            )
             for h in range(count)
         ],
         axis=0,
@@ -193,17 +198,19 @@
     gram = lax.dot_general(
         mapped, padded, (((1,), (1,)), ((), ())), precision=HIGHEST, preferred_element_type=F32
     )
-    slab = own_slab(fold(gram, modes), place, grp)
+    tile = fold(gram, modes)
     if last:
         out_ref, send_ref = refs
         out_ref[...] = mapped[:, :block]
+        slab = own_slab(tile, place, grp)
         for d in range(send_ref.shape[0]):
             send_ref[d] = slab
         return
     field_ref, send_ref = refs
-    store_tiles(send_ref, dot_wide(mapped * weight, field_ref[...], 0))
-    for d in range(send_ref.shape[0]):
-        send_ref[d, grp] = slab
+    pitch = ROWS + 1
+    store_tiles(send_ref, dot_wide(mapped * weight, field_ref[...], 0), pitch)
+    for d in range(send_ref.shape[0] // pitch):
+        send_ref[d * pitch + ROWS : (d + 1) * pitch] = tile[d % ROWS : d % ROWS + 1]
 
 
 def finish_kernel(side_ref, recv_ref, mapped_ref, out_ref, *, grp, pts, points):
@@ -235,14 +242,19 @@
     return pl.pallas_call(
         setup_kernel,
         out_shape=out,
-        in_specs=[SMEM, anywhere, VMEM, VMEM],
+        in_specs=[SMEM, anywhere, anywhere, anywhere],
         out_specs=[VMEM for _ in out],
-        scratch_shapes=[pltpu.SemaphoreType.DMA((grp,))],
+        scratch_shapes=[pltpu.VMEM((1, points), F32), pltpu.SemaphoreType.DMA((grp + 2,))],
     )(place, fields, weight, modes)
 
 
-def exchange(value):
-    return lax.all_to_all(value, ALL, 0, 0)
+def exchange(value, pitch=None):
+    if pitch is None:
+        return lax.all_to_all(value, ALL, 0, 0)
+    chunks = value.shape[0] // pitch
+    unit = ROWS if pitch == ROWS else 1
+    split = value.reshape(chunks, pitch // unit, unit, LANES)
+    return lax.all_to_all(split, ALL, 0, 0).reshape(value.shape)
 
 
 def shifted(value, shift):
@@ -264,24 +276,24 @@
     field = jnp.concatenate(
         [blocks[0]] + [shifted(blocks[k], k) for k in range(1, grp)], axis=0
     )
-    tile = (devices, ROWS, LANES)
-    slabs = (devices, grp + 1, ROWS // grp, LANES)
-
-    factor = None
-    send, weight = call(first_kernel, [(tile, F32), ((ROWS, points), F32)], *packs, field)
+    factor, pitch = None, ROWS
+    outs = [((devices * ROWS, LANES), F32), ((ROWS, points), F32)]
+    send, weight = call(first_kernel, outs, *packs, field)
     for iteration in range(ITERS):
         has_gram, last = iteration > 0, iteration == ITERS - 1
-        kernel = lambda *refs: reduce_kernel(*refs, grp=grp, pts=pts)
-        if has_gram:
-            outs = [(tile, F32), ((ROWS, LANES), F32)]
-            summed, gram = call(kernel, outs, side, exchange(send))
-        else:
-            summed = call(kernel, [(tile, BF16)], side, exchange(send))
-        own = call(back_kernel, [((modes, points), F32)], exchange(summed), field)
+        kernel = lambda *refs: reduce_kernel(*refs, grp=grp, pts=pts, pitch=pitch)
+        dtype = F32 if has_gram else BF16
+        summed = call(kernel, [((devices * pitch, LANES), dtype)], exchange(send, pitch))
+        gathered = exchange(summed, pitch)
+        kernel = lambda *refs: back_kernel(*refs, pitch=pitch)
+        own = call(kernel, [((modes, points), F32)], gathered, field)
         others = [shifted(own, k) for k in range(1, grp)]
         if has_gram:
-            kernel = lambda *refs: factor_kernel(*refs, modes=modes, points=total_points)
-            factor = call(kernel, [((modes, LANES), F32)], gram)
+            kernel = lambda *refs: factor_kernel(
+                *refs, modes=modes, points=total_points, pitch=pitch
+            )
+            factor = call(kernel, [((modes, LANES), F32)], gathered)
+        pitch = ROWS + 1
         kernel = lambda *refs: map_kernel(
             *refs, samples=samples, others=grp - 1, has_factor=has_gram, last=last
         )
@@ -290,7 +302,7 @@
             outs = [((modes, points // grp), F32), ((devices, ROWS // grp, LANES), F32)]
             mapped, send = call(kernel, outs, *given)
         else:
-            send = call(kernel, [(slabs, F32)], *given, field)
+            send = call(kernel, [((devices * pitch, LANES), F32)], *given, field)
     kernel = lambda *refs: finish_kernel(*refs, grp=grp, pts=pts, points=total_points)
     out = jax.ShapeDtypeStruct((modes, points // grp), F32)
     return call(kernel, [out], side, exchange(send), mapped)[None]

time: 161 us -> 156 us (0.969)
  starting transfers between devices: 8.66 us -> 4.11 us
  blocking collectives: 125 us -> 127 us
    all_to_all x1, starting transfers between devices: 7.21 us -> 2.62 us  [exchange(): return lax.all_to_all(value, ALL, 0, 0)]
    all_to_all x12, blocking collectives: 125 us -> 127 us  [exchange(): return lax.all_to_all(split, ALL, 0, 0).reshape(value.shape)]
where the time goes in v5:
time: 156 us
  blocking collectives  127 us (81%)
  Pallas kernels  13.6 us (9%)
  waiting for transfers between devices  11.4 us (7%)
  starting transfers between devices  4.11 us (3%)
    all_to_all x12, blocking collectives, exchange(): return lax.all_to_all(split, ALL, 0, 0).reshape(value.shape)  127 us
    pallas_call x25, Pallas kernels, call(): pl.pallas_call(kernel, out_shape=out, in_specs=specs, out_specs=[VMEM for...  12.4 us
    all_to_all x1, waiting for transfers between devices, exchange(): return lax.all_to_all(value, ALL, 0, 0)  7.27 us
    ppermute x8, waiting for transfers between devices, shifted(): lax.ppermute(value, 'grp', [((i + shift) % grp, i) for i in range(grp)])  4.15 us
  transfers between devices with their start and end apart: 9, of which 8 were waited for; matrix products, arithmetic and copies ran while one was open for 0% of the time, Pallas kernels for 3%

profile of v5, /device:TPU:0, one launch (start us, length us, event | category | flops | bytes accessed | tf_op | source)
XLA Modules:
  0.0 156.0 jit_solution(5762154393404260852)
XLA Ops:
  0.0 1.3 shard_map.37
  2.0 1.4 collective-permute-done.1
  3.7 14.8 %all_to_all.65 = f32[32,1,8,128]{3,2,1,0:T(8,128)S(1)} all-to-all(f32[32,1,8,128]{3,2,1,0:T(8,128)S(1)} %bitcast.59), channel_id=1, replica_groups=mesh['side'=2,'grp'=2,'pts'=8] {'side','grp','pts'}, dimensions={0} | all-to-all | bytes 262144 | tf_op jit(solution)/shard_map/all_to_all | solution.py:257
  18.6 9.4 %all_to_all.66 = bf16[32,1,8,128]{3,2,1,0:T(8,128)(2,1)S(1)} all-to-all(bf16[32,1,8,128]{3,2,1,0:T(8,128)(2,1)S(1)} %bitcast.57), channel_id=1, replica_groups=mesh['side'=2,'grp'=2,'pts'=8] {'side','grp','pts'}, dimensions={0} | all-to-all | bytes 131072 | tf_op jit(solution)/shard_map/all_to_all | solution.py:257
  28.5 1.1 collective-permute-done.2.refs_2_
  30.0 9.6 %all_to_all.67 = f32[32,9,1,128]{3,2,1,0:T(1,128)S(1)} all-to-all(f32[32,9,1,128]{3,2,1,0:T(1,128)S(1)} %bitcast.45), channel_id=1, replica_groups=mesh['side'=2,'grp'=2,'pts'=8] {'side','grp','pts'}, dimensions={0} | all-to-all | bytes 294912 | tf_op jit(solution)/shard_map/all_to_all | solution.py:257
  39.7 10.2 %all_to_all.68 = f32[32,9,1,128]{3,2,1,0:T(1,128)S(1)} all-to-all(f32[32,9,1,128]{3,2,1,0:T(1,128)S(1)} %bitcast.47), channel_id=1, replica_groups=mesh['side'=2,'grp'=2,'pts'=8] {'side','grp','pts'}, dimensions={0} | all-to-all | bytes 294912 | tf_op jit(solution)/shard_map/all_to_all | solution.py:257
  50.5 0.8 shard_map.44.refs_3_
  52.2 10.3 %all_to_all.69 = f32[32,9,1,128]{3,2,1,0:T(1,128)S(1)} all-to-all(f32[32,9,1,128]{3,2,1,0:T(1,128)S(1)} %bitcast.41), channel_id=1, replica_groups=mesh['side'=2,'grp'=2,'pts'=8] {'side','grp','pts'}, dimensions={0} | all-to-all | bytes 294912 | tf_op jit(solution)/shard_map/all_to_all | solution.py:257
  62.5 10.3 %all_to_all.70 = f32[32,9,1,128]{3,2,1,0:T(1,128)S(1)} all-to-all(f32[32,9,1,128]{3,2,1,0:T(1,128)S(1)} %bitcast.49), channel_id=1, replica_groups=mesh['side'=2,'grp'=2,'pts'=8] {'side','grp','pts'}, dimensions={0} | all-to-all | bytes 294912 | tf_op jit(solution)/shard_map/all_to_all | solution.py:257
  73.4 0.8 shard_map.48.refs_3_
  75.1 10.3 %all_to_all.71 = f32[32,9,1,128]{3,2,1,0:T(1,128)S(1)} all-to-all(f32[32,9,1,128]{3,2,1,0:T(1,128)S(1)} %bitcast.42), channel_id=1, replica_groups=mesh['side'=2,'grp'=2,'pts'=8] {'side','grp','pts'}, dimensions={0} | all-to-all | bytes 294912 | tf_op jit(solution)/shard_map/all_to_all | solution.py:257
  85.5 10.3 %all_to_all.72 = f32[32,9,1,128]{3,2,1,0:T(1,128)S(1)} all-to-all(f32[32,9,1,128]{3,2,1,0:T(1,128)S(1)} %bitcast.51), channel_id=1, replica_groups=mesh['side'=2,'grp'=2,'pts'=8] {'side','grp','pts'}, dimensions={0} | all-to-all | bytes 294912 | tf_op jit(solution)/shard_map/all_to_all | solution.py:257
  96.4 0.8 shard_map.52.refs_3_
  98.1 10.3 %all_to_all.73 = f32[32,9,1,128]{3,2,1,0:T(1,128)S(1)} all-to-all(f32[32,9,1,128]{3,2,1,0:T(1,128)S(1)} %bitcast.43), channel_id=1, replica_groups=mesh['side'=2,'grp'=2,'pts'=8] {'side','grp','pts'}, dimensions={0} | all-to-all | bytes 294912 | tf_op jit(solution)/shard_map/all_to_all | solution.py:257
  108.4 10.3 %all_to_all.74 = f32[32,9,1,128]{3,2,1,0:T(1,128)S(1)} all-to-all(f32[32,9,1,128]{3,2,1,0:T(1,128)S(1)} %bitcast.53), channel_id=1, replica_groups=mesh['side'=2,'grp'=2,'pts'=8] {'side','grp','pts'}, dimensions={0} | all-to-all | bytes 294912 | tf_op jit(solution)/shard_map/all_to_all | solution.py:257
  119.3 0.8 shard_map.56.refs_3_
  121.0 10.3 %all_to_all.75 = f32[32,9,1,128]{3,2,1,0:T(1,128)S(1)} all-to-all(f32[32,9,1,128]{3,2,1,0:T(1,128)S(1)} %bitcast.44), channel_id=1, replica_groups=mesh['side'=2,'grp'=2,'pts'=8] {'side','grp','pts'}, dimensions={0} | all-to-all | bytes 294912 | tf_op jit(solution)/shard_map/all_to_all | solution.py:257
  131.4 10.3 %all_to_all.76 = f32[32,9,1,128]{3,2,1,0:T(1,128)S(1)} all-to-all(f32[32,9,1,128]{3,2,1,0:T(1,128)S(1)} %bitcast.55), channel_id=1, replica_groups=mesh['side'=2,'grp'=2,'pts'=8] {'side','grp','pts'}, dimensions={0} | all-to-all | bytes 294912 | tf_op jit(solution)/shard_map/all_to_all | solution.py:257
  142.3 0.8 shard_map.60.refs_3_
  143.4 1.1 shard_map.61
  144.5 2.6 %all-to-all-start.12 = ((f32[32,4,128]{2,1,0:T(4,128)}), f32[32,4,128]{2,1,0:T(4,128)S(1)}, u32[]{:S(2)}, u32[]{:S(2)}) async-start(f32[32,4,128]{2,1,0:T(4,128)} %get-tuple-element.17), calls=%async_computation.12 | async-start | bytes 131072 | tf_op jit(solution)/shard_map/all_to_all | solution.py:253
  147.1 7.3 %all-to-all-done.12.refs_1_ = f32[32,4,128]{2,1,0:T(4,128)S(1)} async-done(((f32[32,4,128]{2,1,0:T(4,128)}), f32[32,4,128]{2,1,0:T(4,128)S(1)}, u32[]{:S(2)}, u32[]{:S(2)}) %all-to-all-start.12) | async-done | bytes 65568 | tf_op jit(solution)/shard_map/all_to_all | solution.py:253
  154.4 1.6 %shard_map.62 = f32[32,256]{1,0:T(8,128)} custom-call(s32[1]{0:T(128)} %bitcast.refs_0_, f32[32,4,128]{2,1,0:T(4,128)S(1)} %all-to-all-done.12.refs_1_, f32[32,256]{1,0:T(8,128)S(1)} %get-tuple-element.18.refs_2_), custom_call_target="tpu_custom_call" | custom-call | tf_op jit(solution)/shard_map/pallas_call | solution.py:231
  (34 shorter events, 8.7 us)
Async XLA Ops:
  1.3 2.1 %collective-permute-start.1 = (bf16[256,1024]{1,0:T(8,128)(2,1)S(1)}, bf16[256,1024]{1,0:T(8,128)(2,1)S(1)}, u32[]{:S(2)}, u32[]{:S(2)}) collective-permute-start(bf16[256,1024]{1,0:T(8,128)(2,1)S(1)} %get-tuple-element.14), channel_id=1, source_target_pairs={{8,0},{0,8},{9,1},{1,9},{10,2},{2,10},{11,3},{3,11},{12,4},{4,12},... | collective-permute-start | bytes 1572872 | tf_op jit(solution)/shard_map/ppermute | solution.py:262
  1.8 1.6 %collective-permute-start = (f32[40,256]{1,0:T(8,128)S(1)}, f32[40,256]{1,0:T(8,128)S(1)}, u32[]{:S(2)}, u32[]{:S(2)}) collective-permute-start(f32[40,256]{1,0:T(8,128)S(1)} %get-tuple-element.12.refs_0_), channel_id=1, source_target_pairs={{8,0},{0,8},{9,1},{1,9},{10,2},{2,10},{11,3},{3,11},{12,4},{4,12},... | collective-permute-start | bytes 122888 | tf_op jit(solution)/shard_map/ppermute | solution.py:262
  28.4 1.3 collective-permute-start.2
  50.3 1.3 collective-permute-start.3
  73.3 1.3 collective-permute-start.4
  96.2 1.3 collective-permute-start.5
  119.2 1.3 collective-permute-start.6
  142.1 1.3 collective-permute-start.7
  144.5 9.9 %all-to-all-start.12 = ((f32[32,4,128]{2,1,0:T(4,128)}), f32[32,4,128]{2,1,0:T(4,128)S(1)}, u32[]{:S(2)}, u32[]{:S(2)}) async-start(f32[32,4,128]{2,1,0:T(4,128)} %get-tuple-element.17), calls=%async_computation.12 | async-start | bytes 131072 | tf_op jit(solution)/shard_map/all_to_all | solution.py:253

commit v6 on v5

--- a/solution.py
+++ b/solution.py
@@ -22,11 +22,9 @@
     return jnp.concatenate([high, mid, low], axis=0)
 
 
-def dot_wide(x, field, contract):
+def dot_wide(x, field):
     count = x.shape[0]
-    out = lax.dot_general(
-        split3(x), field, (((1,), (contract,)), ((), ())), preferred_element_type=F32
-    )
+    out = jnp.dot(split3(x), field, preferred_element_type=F32)
     return out[2 * count :] + out[count : 2 * count] + out[:count]
 
 
@@ -128,7 +126,7 @@
     pack = jnp.concatenate([ref[...] for ref in pack_refs], axis=1)
     weight = pack[-ROWS:]
     weight_ref[...] = weight
-    store_tiles(send_ref, dot_wide(pack[:-ROWS] * weight[:1], field_ref[...], 0), ROWS)
+    store_tiles(send_ref, dot_wide(pack[:-ROWS] * weight[:1], field_ref[...]), ROWS)
 
 
 def reduce_kernel(recv_ref, send_ref, *, grp, pts, pitch):
@@ -155,8 +153,8 @@
     out_ref[...] = inverse_factor(unfold(gram, modes) / points, modes)
 
 
-def back_kernel(recv_ref, field_ref, out_ref, *, pitch):
-    columns = field_ref.shape[1] // LANES
+def back_kernel(recv_ref, field_ref, out_ref, *, pitch, samples):
+    columns = samples // LANES
     count = recv_ref.shape[0] // (pitch * columns)
     coeffs = jnp.concatenate(
         [
@@ -176,7 +174,11 @@
             coeffs, field_ref[...], (((1,), (1,)), ((), ())), preferred_element_type=F32
         )
     else:
-        out_ref[...] = dot_wide(coeffs, field_ref[...], 1)
+        out_ref[...] = dot_wide(coeffs, field_ref[...])
+
+
+def turn_kernel(_, field_ref, out_ref):
+    out_ref[...] = field_ref[...].T
 
 
 def map_kernel(*refs, samples, others, has_factor, last):
@@ -208,13 +210,13 @@
         return
     field_ref, send_ref = refs
     pitch = ROWS + 1
-    store_tiles(send_ref, dot_wide(mapped * weight, field_ref[...], 0), pitch)
+    store_tiles(send_ref, dot_wide(mapped * weight, field_ref[...]), pitch)
     for d in range(send_ref.shape[0] // pitch):
         send_ref[d * pitch + ROWS : (d + 1) * pitch] = tile[d % ROWS : d % ROWS + 1]
 
 
-def finish_kernel(side_ref, recv_ref, mapped_ref, out_ref, *, grp, pts, points):
-    total = whole_tile(lambda d: recv_ref[d], side_ref[0] * (grp * pts), grp, pts)
+def finish_kernel(place_ref, recv_ref, mapped_ref, out_ref, *, grp, pts, points):
+    total = whole_tile(lambda d: recv_ref[d], place_ref[1] * (grp * pts), grp, pts)
     mapped = mapped_ref[...]
     modes = mapped.shape[0]
     factor = inverse_factor(unfold(total, modes) / points, modes)[:, :modes]
@@ -268,8 +270,7 @@
     devices = 2 * grp * pts
     total_points = fields.shape[1] * grp * pts
     points = fields.shape[1] * grp
-    place = lax.axis_index("grp").astype(jnp.int32).reshape(1)
-    side = lax.axis_index("side").astype(jnp.int32).reshape(1)
+    place = jnp.stack([lax.axis_index("grp"), lax.axis_index("side")]).astype(jnp.int32)
 
     pack, *blocks = cut(place, fields, point_weight, start_modes, grp)
     packs = [pack] + [shifted(pack, k) for k in range(1, grp)]
@@ -285,8 +286,13 @@
         dtype = F32 if has_gram else BF16
         summed = call(kernel, [((devices * pitch, LANES), dtype)], exchange(send, pitch))
         gathered = exchange(summed, pitch)
-        kernel = lambda *refs: back_kernel(*refs, pitch=pitch)
-        own = call(kernel, [((modes, points), F32)], gathered, field)
+        kernel = lambda *refs: back_kernel(*refs, pitch=pitch, samples=samples // grp)
+        own = call(
+            kernel, [((modes, points), F32)], gathered, turned if has_gram else field
+        )
+        if not has_gram:
+            shape = (field.shape[1], points)
+            turned = call(turn_kernel, [(shape, field.dtype)], own, field)
         others = [shifted(own, k) for k in range(1, grp)]
         if has_gram:
             kernel = lambda *refs: factor_kernel(
@@ -305,7 +311,7 @@
             send = call(kernel, [((devices * pitch, LANES), F32)], *given, field)
     kernel = lambda *refs: finish_kernel(*refs, grp=grp, pts=pts, points=total_points)
     out = jax.ShapeDtypeStruct((modes, points // grp), F32)
-    return call(kernel, [out], side, exchange(send), mapped)[None]
+    return call(kernel, [out], place, exchange(send), mapped)[None]
 
 
 def body_sums(fields, point_weight, start_modes):

time: 156 us -> 168 us (1.077)
  local copies, waits for them, and re-layouts: 0.07 us -> 5.99 us
  Pallas kernels: 13.6 us -> 18.5 us
    all_to_all x12 -> x11, blocking collectives: 127 us -> 116 us  [exchange(): return lax.all_to_all(split, ALL, 0, 0).reshape(value.shape)]
    all_to_all x0 -> x1, blocking collectives: none -> 9.71 us  [exchange(): return lax.all_to_all(value, ALL, 0, 0)]
    unnamed x1 -> x11, local copies, waits for them, and re-layouts: 0.03 us -> 5.95 us
    pallas_call x25 -> x26, Pallas kernels: 12.4 us -> 16.6 us  [call(): pl.pallas_call(kernel, out_shape=out, in_specs=specs, out_specs=[VMEM for...]
where the time goes in v6:
time: 168 us; the launch traced here: 167 us
  blocking collectives  126 us (75%)
  Pallas kernels  18.5 us (11%)
  waiting for transfers between devices  11.7 us (7%)
  local copies, waits for them, and re-layouts  5.99 us (4%)
  starting transfers between devices  4.04 us (2%)
    all_to_all x11, blocking collectives, exchange(): return lax.all_to_all(split, ALL, 0, 0).reshape(value.shape)  116 us
    pallas_call x26, Pallas kernels, call(): pl.pallas_call(kernel, out_shape=out, in_specs=specs, out_specs=[VMEM for...  16.6 us
    all_to_all x1, blocking collectives, exchange(): return lax.all_to_all(value, ALL, 0, 0)  9.71 us
    all_to_all x1, waiting for transfers between devices, exchange(): return lax.all_to_all(split, ALL, 0, 0).reshape(value.shape)  7.57 us
    unnamed x11, local copies, waits for them, and re-layouts  5.95 us
    ppermute x8, waiting for transfers between devices, shifted(): lax.ppermute(value, 'grp', [((i + shift) % grp, i) for i in range(grp)])  4.16 us
  transfers between devices with their start and end apart: 9, of which 8 were waited for; matrix products, arithmetic and copies ran while one was open for 0% of the time, Pallas kernels for 3%

profile of v6, /device:TPU:0, one launch (start us, length us, event | category | flops | bytes accessed | tf_op | source)
XLA Modules:
  0.0 167.1 jit_solution(5403201625268142290)
XLA Ops:
  0.7 1.9 %shard_map.37 = (f32[40,256]{1,0:T(8,128)S(1)}, bf16[256,1024]{1,0:T(8,128)(2,1)S(1)}, bf16[256,1024]{1,0:T(8,128)(2,1)S(1)}) custom-call(s32[2]{0:T(128)} %pad_add_fusion.place_ref.refs_0_, bf16[1,256,2048]{2,1,0:T(8,128)(2,1)} %fields_ref.1, f32[1,256]{1,0:T(1,128)} %weight_ref.1, f32[1,32,256]{2,1,0:T(8,128)} %modes_ref.1), custom_call_target="tpu_custom_call" | custom-call | tf_op jit(solution)/shard_map/pallas_call | solution.py:244
  3.3 1.4 collective-permute-done.1
  5.0 14.8 %all_to_all.65 = f32[32,1,8,128]{3,2,1,0:T(8,128)S(1)} all-to-all(f32[32,1,8,128]{3,2,1,0:T(8,128)S(1)} %bitcast.58), channel_id=1, replica_groups=mesh['side'=2,'grp'=2,'pts'=8] {'side','grp','pts'}, dimensions={0} | all-to-all | bytes 262144 | tf_op jit(solution)/shard_map/all_to_all | solution.py:259
  19.9 9.4 %all_to_all.66 = bf16[32,1,8,128]{3,2,1,0:T(8,128)(2,1)S(1)} all-to-all(bf16[32,1,8,128]{3,2,1,0:T(8,128)(2,1)S(1)} %bitcast.56), channel_id=1, replica_groups=mesh['side'=2,'grp'=2,'pts'=8] {'side','grp','pts'}, dimensions={0} | all-to-all | bytes 131072 | tf_op jit(solution)/shard_map/all_to_all | solution.py:259
  32.0 9.6 %all_to_all.67 = f32[32,9,1,128]{3,2,1,0:T(1,128)S(1)} all-to-all(f32[32,9,1,128]{3,2,1,0:T(1,128)S(1)} %bitcast.45), channel_id=1, replica_groups=mesh['side'=2,'grp'=2,'pts'=8] {'side','grp','pts'}, dimensions={0} | all-to-all | bytes 294912 | tf_op jit(solution)/shard_map/all_to_all | solution.py:259
  42.3 2.6 %all-to-all-start.3 = ((f32[32,9,1,128]{3,2,1,0:T(1,128)}), f32[32,9,1,128]{3,2,1,0:T(1,128)S(1)}, u32[]{:S(2)}, u32[]{:S(2)}) async-start(f32[32,9,1,128]{3,2,1,0:T(1,128)} %bitcast.10), calls=%async_computation.3 | async-start | bytes 294912 | tf_op jit(solution)/shard_map/all_to_all | solution.py:259
  45.2 7.6 %all-to-all-done.3 = f32[32,9,1,128]{3,2,1,0:T(1,128)S(1)} async-done(((f32[32,9,1,128]{3,2,1,0:T(1,128)}), f32[32,9,1,128]{3,2,1,0:T(1,128)S(1)}, u32[]{:S(2)}, u32[]{:S(2)}) %all-to-all-start.3) | async-done | bytes 147488 | tf_op jit(solution)/shard_map/all_to_all | solution.py:259
  55.4 1.2 shard_map.46
  56.6 10.3 %all_to_all.68 = f32[32,9,1,128]{3,2,1,0:T(1,128)S(1)} all-to-all(f32[32,9,1,128]{3,2,1,0:T(1,128)S(1)} %bitcast.42), channel_id=1, replica_groups=mesh['side'=2,'grp'=2,'pts'=8] {'side','grp','pts'}, dimensions={0} | all-to-all | bytes 294912 | tf_op jit(solution)/shard_map/all_to_all | solution.py:259
  66.9 10.3 %all_to_all.69 = f32[32,9,1,128]{3,2,1,0:T(1,128)S(1)} all-to-all(f32[32,9,1,128]{3,2,1,0:T(1,128)S(1)} %bitcast.48), channel_id=1, replica_groups=mesh['side'=2,'grp'=2,'pts'=8] {'side','grp','pts'}, dimensions={0} | all-to-all | bytes 294912 | tf_op jit(solution)/shard_map/all_to_all | solution.py:259
  77.2 1.2 copy-done.1
  80.0 1.2 shard_map.50
  81.2 10.3 %all_to_all.70 = f32[32,9,1,128]{3,2,1,0:T(1,128)S(1)} all-to-all(f32[32,9,1,128]{3,2,1,0:T(1,128)S(1)} %bitcast.43), channel_id=1, replica_groups=mesh['side'=2,'grp'=2,'pts'=8] {'side','grp','pts'}, dimensions={0} | all-to-all | bytes 294912 | tf_op jit(solution)/shard_map/all_to_all | solution.py:259
  91.6 10.3 %all_to_all.71 = f32[32,9,1,128]{3,2,1,0:T(1,128)S(1)} all-to-all(f32[32,9,1,128]{3,2,1,0:T(1,128)S(1)} %bitcast.50), channel_id=1, replica_groups=mesh['side'=2,'grp'=2,'pts'=8] {'side','grp','pts'}, dimensions={0} | all-to-all | bytes 294912 | tf_op jit(solution)/shard_map/all_to_all | solution.py:259
  101.9 1.2 copy-done.2
  104.7 1.2 shard_map.54
  105.9 10.3 %all_to_all.72 = f32[32,9,1,128]{3,2,1,0:T(1,128)S(1)} all-to-all(f32[32,9,1,128]{3,2,1,0:T(1,128)S(1)} %bitcast.44), channel_id=1, replica_groups=mesh['side'=2,'grp'=2,'pts'=8] {'side','grp','pts'}, dimensions={0} | all-to-all | bytes 294912 | tf_op jit(solution)/shard_map/all_to_all | solution.py:259
  116.2 10.3 %all_to_all.73 = f32[32,9,1,128]{3,2,1,0:T(1,128)S(1)} all-to-all(f32[32,9,1,128]{3,2,1,0:T(1,128)S(1)} %bitcast.52), channel_id=1, replica_groups=mesh['side'=2,'grp'=2,'pts'=8] {'side','grp','pts'}, dimensions={0} | all-to-all | bytes 294912 | tf_op jit(solution)/shard_map/all_to_all | solution.py:259
  126.6 1.2 copy-done.3
  130.6 10.3 %all_to_all.74 = f32[32,9,1,128]{3,2,1,0:T(1,128)S(1)} all-to-all(f32[32,9,1,128]{3,2,1,0:T(1,128)S(1)} %bitcast.41), channel_id=1, replica_groups=mesh['side'=2,'grp'=2,'pts'=8] {'side','grp','pts'}, dimensions={0} | all-to-all | bytes 294912 | tf_op jit(solution)/shard_map/all_to_all | solution.py:259
  140.9 10.3 %all_to_all.75 = f32[32,9,1,128]{3,2,1,0:T(1,128)S(1)} all-to-all(f32[32,9,1,128]{3,2,1,0:T(1,128)S(1)} %bitcast.54), channel_id=1, replica_groups=mesh['side'=2,'grp'=2,'pts'=8] {'side','grp','pts'}, dimensions={0} | all-to-all | bytes 294912 | tf_op jit(solution)/shard_map/all_to_all | solution.py:259
  151.2 1.2 copy-done.4
  155.2 9.7 %all_to_all.76.refs_1_ = f32[32,4,128]{2,1,0:T(4,128)S(1)} all-to-all(f32[32,4,128]{2,1,0:T(4,128)S(1)} %get-tuple-element.17), channel_id=1, replica_groups=mesh['side'=2,'grp'=2,'pts'=8] {'side','grp','pts'}, dimensions={0} | all-to-all | bytes 131072 | tf_op jit(solution)/shard_map/all_to_all | solution.py:255
  164.9 2.3 %shard_map.63 = f32[32,256]{1,0:T(8,128)} custom-call(s32[2]{0:T(128)} %pad_add_fusion.place_ref.refs_0_, f32[32,4,128]{2,1,0:T(4,128)S(1)} %all_to_all.76.refs_1_, f32[32,256]{1,0:T(8,128)S(1)} %get-tuple-element.18.refs_2_), custom_call_target="tpu_custom_call" | custom-call | tf_op jit(solution)/shard_map/pallas_call | solution.py:233
  (46 shorter events, 16.6 us)
Async XLA Ops:
  2.6 2.1 %collective-permute-start.1 = (bf16[256,1024]{1,0:T(8,128)(2,1)S(1)}, bf16[256,1024]{1,0:T(8,128)(2,1)S(1)}, u32[]{:S(2)}, u32[]{:S(2)}) collective-permute-start(bf16[256,1024]{1,0:T(8,128)(2,1)S(1)} %get-tuple-element.14), channel_id=1, source_target_pairs={{8,0},{0,8},{9,1},{1,9},{10,2},{2,10},{11,3},{3,11},{12,4},{4,12},... | collective-permute-start | bytes 1572872 | tf_op jit(solution)/shard_map/ppermute | solution.py:264
  3.1 1.6 collective-permute-start
  29.7 1.3 collective-permute-start.2
  42.3 10.5 %all-to-all-start.3 = ((f32[32,9,1,128]{3,2,1,0:T(1,128)}), f32[32,9,1,128]{3,2,1,0:T(1,128)S(1)}, u32[]{:S(2)}, u32[]{:S(2)}) async-start(f32[32,9,1,128]{3,2,1,0:T(1,128)} %bitcast.10), calls=%async_computation.3 | async-start | bytes 294912 | tf_op jit(solution)/shard_map/all_to_all | solution.py:259
  53.1 1.0 copy-start
  54.1 1.3 collective-permute-start.3
  77.2 1.2 copy-start.1
  78.7 1.3 collective-permute-start.4
  101.9 1.2 copy-start.2
  103.4 1.3 collective-permute-start.5
  126.6 1.2 copy-start.3
  128.1 1.3 collective-permute-start.6
  151.2 1.2 copy-start.4
  152.7 1.3 collective-permute-start.7

commit v7 on v6

--- a/solution.py
+++ b/solution.py
@@ -12,6 +12,7 @@
 HIGHEST = lax.Precision.HIGHEST
 VMEM = pl.BlockSpec(memory_space=pltpu.VMEM)
 SMEM = pl.BlockSpec(memory_space=pltpu.SMEM)
+GRANT = pltpu.CompilerParams(vmem_limit_bytes=8 << 20)
 
 
 def split3(x):
@@ -101,7 +102,7 @@
     return jnp.concatenate(slabs, axis=0)
 
 
-def setup_kernel(place_ref, fields_ref, weight_ref, modes_ref, pack_ref, *rest):
+def setup_kernel(place_ref, _, fields_ref, weight_ref, modes_ref, pack_ref, *rest):
     *block_refs, row_ref, sems = rest
     grp, columns = len(block_refs), block_refs[0].shape[1]
     modes = modes_ref.shape[1]
@@ -191,7 +192,7 @@
         other = refs.pop(0)[...]
         cut = (others - k) * block
         mapped = mapped + jnp.concatenate([other[:, cut:], other[:, :cut]], axis=1)
-    factor = refs.pop(0)[...][:, :modes] if has_factor else None
+    factor = refs.pop(0)[...][:, :modes]
     weight = refs.pop(0)[:1]
     if has_factor:
         mapped = jnp.dot(factor, mapped, precision=HIGHEST, preferred_element_type=F32)
@@ -215,8 +216,8 @@
         send_ref[d * pitch + ROWS : (d + 1) * pitch] = tile[d % ROWS : d % ROWS + 1]
 
 
-def finish_kernel(place_ref, recv_ref, mapped_ref, out_ref, *, grp, pts, points):
-    total = whole_tile(lambda d: recv_ref[d], place_ref[1] * (grp * pts), grp, pts)
+def finish_kernel(side_ref, recv_ref, mapped_ref, out_ref, *, grp, pts, points):
+    total = whole_tile(lambda d: recv_ref[d], side_ref[0] * (grp * pts), grp, pts)
     mapped = mapped_ref[...]
     modes = mapped.shape[0]
     factor = inverse_factor(unfold(total, modes) / points, modes)[:, :modes]
@@ -231,23 +232,28 @@
     ]
     out = [o if isinstance(o, jax.ShapeDtypeStruct) else pltpu.VMEM(*o) for o in outs]
     result = pl.pallas_call(
-        kernel, out_shape=out, in_specs=specs, out_specs=[VMEM for _ in out]
+        kernel,
+        out_shape=out,
+        in_specs=specs,
+        out_specs=[VMEM for _ in out],
+        compiler_params=GRANT,
     )(*args)
     return result if len(out) > 1 else result[0]
 
 
-def cut(place, fields, weight, modes, grp):
+def cut(place, side, fields, weight, modes, grp):
     _, points, samples = fields.shape
     out = [pltpu.VMEM((modes.shape[1] + ROWS, points), F32)]
     out += [pltpu.VMEM((points, samples // grp), fields.dtype) for _ in range(grp)]
-    anywhere = pl.BlockSpec(memory_space=pl.ANY)
+    anywhere = pl.BlockSpec(memory_space=pltpu.HBM)
     return pl.pallas_call(
         setup_kernel,
         out_shape=out,
-        in_specs=[SMEM, anywhere, anywhere, anywhere],
+        in_specs=[SMEM, SMEM, anywhere, anywhere, anywhere],
         out_specs=[VMEM for _ in out],
+        compiler_params=GRANT,
         scratch_shapes=[pltpu.VMEM((1, points), F32), pltpu.SemaphoreType.DMA((grp + 2,))],
-    )(place, fields, weight, modes)
+    )(place, side, *(pltpu.with_memory_space_constraint(a, pltpu.HBM) for a in (fields, weight, modes)))
 
 
 def exchange(value, pitch=None):
@@ -270,9 +276,10 @@
     devices = 2 * grp * pts
     total_points = fields.shape[1] * grp * pts
     points = fields.shape[1] * grp
-    place = jnp.stack([lax.axis_index("grp"), lax.axis_index("side")]).astype(jnp.int32)
-
-    pack, *blocks = cut(place, fields, point_weight, start_modes, grp)
+    place = lax.axis_index("grp").astype(jnp.int32).reshape(1)
+    side = lax.axis_index("side").astype(jnp.int32).reshape(1)
+
+    pack, *blocks = cut(place, side, fields, point_weight, start_modes, grp)
     packs = [pack] + [shifted(pack, k) for k in range(1, grp)]
     field = jnp.concatenate(
         [blocks[0]] + [shifted(blocks[k], k) for k in range(1, grp)], axis=0
@@ -303,7 +310,7 @@
         kernel = lambda *refs: map_kernel(
             *refs, samples=samples, others=grp - 1, has_factor=has_gram, last=last
         )
-        given = [place, own, *others, *([factor] if has_gram else []), weight]
+        given = [place, own, *others, factor if has_gram else turned, weight]
         if last:
             outs = [((modes, points // grp), F32), ((devices, ROWS // grp, LANES), F32)]
             mapped, send = call(kernel, outs, *given)
@@ -311,7 +318,7 @@
             send = call(kernel, [((devices * pitch, LANES), F32)], *given, field)
     kernel = lambda *refs: finish_kernel(*refs, grp=grp, pts=pts, points=total_points)
     out = jax.ShapeDtypeStruct((modes, points // grp), F32)
-    return call(kernel, [out], place, exchange(send), mapped)[None]
+    return call(kernel, [out], side, exchange(send), mapped)[None]
 
 
 def body_sums(fields, point_weight, start_modes):

time: 168 us -> 155 us (0.923)
  blocking collectives: 126 us -> 136 us
  waiting for transfers between devices: 11.7 us -> 3.83 us
  Pallas kernels: 18.5 us -> 12.5 us
  local copies, waits for them, and re-layouts: 5.99 us -> 0.07 us
  starting transfers between devices: 4.04 us -> 1.5 us
    all_to_all x11 -> x12, blocking collectives: 116 us -> 127 us  [exchange(): return lax.all_to_all(split, ALL, 0, 0).reshape(value.shape)]
    all_to_all x1 -> x0, waiting for transfers between devices: 7.57 us -> none  [exchange(): return lax.all_to_all(split, ALL, 0, 0).reshape(value.shape)]
    unnamed x11 -> x1, local copies, waits for them, and re-layouts: 5.95 us -> 0.03 us
    pallas_call x26, Pallas kernels: 16.6 us -> 11.2 us  [call(): pl.pallas_call(kernel, out_shape=out, in_specs=specs, out_specs=[VMEM for...]
    all_to_all x1 -> x0, starting transfers between devices: 2.57 us -> none  [exchange(): return lax.all_to_all(split, ALL, 0, 0).reshape(value.shape)]
  transfers between devices with their start and end apart: 9 -> 8, of which waited for: 8 -> 7; matrix products, arithmetic and copies ran while one was open for 0% -> 0% of each run, Pallas kernels for 3% -> 3%
where the time goes in v7:
time: 155 us; the launch traced here: 154 us
  blocking collectives  136 us (88%)
  Pallas kernels  12.5 us (8%)
  waiting for transfers between devices  3.83 us (2%)
    all_to_all x12, blocking collectives, exchange(): return lax.all_to_all(split, ALL, 0, 0).reshape(value.shape)  127 us
    pallas_call x26, Pallas kernels, call(): pl.pallas_call(kernel, out_shape=out, in_specs=specs, out_specs=[VMEM for...  11.2 us
    all_to_all x1, blocking collectives, exchange(): return lax.all_to_all(value, ALL, 0, 0)  9.7 us
    ppermute x8, waiting for transfers between devices, shifted(): lax.ppermute(value, 'grp', [((i + shift) % grp, i) for i in range(grp)])  3.83 us
  transfers between devices with their start and end apart: 8, of which 7 were waited for; matrix products, arithmetic and copies ran while one was open for 0% of the time, Pallas kernels for 3%

profile of v7, /device:TPU:0, one launch (start us, length us, event | category | flops | bytes accessed | tf_op | source)
XLA Modules:
  0.0 154.4 jit_solution(623407857237676772)
XLA Ops:
  0.0 1.3 shard_map.37
  1.3 0.6 collective-permute-start.1
  2.0 1.4 collective-permute-done.1
  3.7 14.8 %all_to_all.65 = f32[32,1,8,128]{3,2,1,0:T(8,128)S(1)} all-to-all(f32[32,1,8,128]{3,2,1,0:T(8,128)S(1)} %bitcast.59), channel_id=1, replica_groups=mesh['side'=2,'grp'=2,'pts'=8] {'side','grp','pts'}, dimensions={0} | all-to-all | bytes 262144 | tf_op jit(solution)/shard_map/all_to_all | solution.py:265
  18.6 9.4 %all_to_all.66 = bf16[32,1,8,128]{3,2,1,0:T(8,128)(2,1)S(1)} all-to-all(bf16[32,1,8,128]{3,2,1,0:T(8,128)(2,1)S(1)} %bitcast.57), channel_id=1, replica_groups=mesh['side'=2,'grp'=2,'pts'=8] {'side','grp','pts'}, dimensions={0} | all-to-all | bytes 131072 | tf_op jit(solution)/shard_map/all_to_all | solution.py:265
  28.9 0.8 collective-permute-done.2.refs_2_
  30.1 9.6 %all_to_all.67 = f32[32,9,1,128]{3,2,1,0:T(1,128)S(1)} all-to-all(f32[32,9,1,128]{3,2,1,0:T(1,128)S(1)} %bitcast.55), channel_id=1, replica_groups=mesh['side'=2,'grp'=2,'pts'=8] {'side','grp','pts'}, dimensions={0} | all-to-all | bytes 294912 | tf_op jit(solution)/shard_map/all_to_all | solution.py:265
  39.7 10.2 %all_to_all.68 = f32[32,9,1,128]{3,2,1,0:T(1,128)S(1)} all-to-all(f32[32,9,1,128]{3,2,1,0:T(1,128)S(1)} %bitcast.46), channel_id=1, replica_groups=mesh['side'=2,'grp'=2,'pts'=8] {'side','grp','pts'}, dimensions={0} | all-to-all | bytes 294912 | tf_op jit(solution)/shard_map/all_to_all | solution.py:265
  50.3 0.8 shard_map.45.refs_3_
  52.0 10.3 %all_to_all.69 = f32[32,9,1,128]{3,2,1,0:T(1,128)S(1)} all-to-all(f32[32,9,1,128]{3,2,1,0:T(1,128)S(1)} %bitcast.42), channel_id=1, replica_groups=mesh['side'=2,'grp'=2,'pts'=8] {'side','grp','pts'}, dimensions={0} | all-to-all | bytes 294912 | tf_op jit(solution)/shard_map/all_to_all | solution.py:265
  62.4 10.3 %all_to_all.70 = f32[32,9,1,128]{3,2,1,0:T(1,128)S(1)} all-to-all(f32[32,9,1,128]{3,2,1,0:T(1,128)S(1)} %bitcast.48), channel_id=1, replica_groups=mesh['side'=2,'grp'=2,'pts'=8] {'side','grp','pts'}, dimensions={0} | all-to-all | bytes 294912 | tf_op jit(solution)/shard_map/all_to_all | solution.py:265
  73.1 0.8 shard_map.49.refs_3_
  74.3 0.6 shard_map.50
  74.8 10.3 %all_to_all.71 = f32[32,9,1,128]{3,2,1,0:T(1,128)S(1)} all-to-all(f32[32,9,1,128]{3,2,1,0:T(1,128)S(1)} %bitcast.43), channel_id=1, replica_groups=mesh['side'=2,'grp'=2,'pts'=8] {'side','grp','pts'}, dimensions={0} | all-to-all | bytes 294912 | tf_op jit(solution)/shard_map/all_to_all | solution.py:265
  85.2 10.3 %all_to_all.72 = f32[32,9,1,128]{3,2,1,0:T(1,128)S(1)} all-to-all(f32[32,9,1,128]{3,2,1,0:T(1,128)S(1)} %bitcast.50), channel_id=1, replica_groups=mesh['side'=2,'grp'=2,'pts'=8] {'side','grp','pts'}, dimensions={0} | all-to-all | bytes 294912 | tf_op jit(solution)/shard_map/all_to_all | solution.py:265
  95.9 0.8 shard_map.53.refs_3_
  97.6 10.3 %all_to_all.73 = f32[32,9,1,128]{3,2,1,0:T(1,128)S(1)} all-to-all(f32[32,9,1,128]{3,2,1,0:T(1,128)S(1)} %bitcast.44), channel_id=1, replica_groups=mesh['side'=2,'grp'=2,'pts'=8] {'side','grp','pts'}, dimensions={0} | all-to-all | bytes 294912 | tf_op jit(solution)/shard_map/all_to_all | solution.py:265
  108.0 10.3 %all_to_all.74 = f32[32,9,1,128]{3,2,1,0:T(1,128)S(1)} all-to-all(f32[32,9,1,128]{3,2,1,0:T(1,128)S(1)} %bitcast.52), channel_id=1, replica_groups=mesh['side'=2,'grp'=2,'pts'=8] {'side','grp','pts'}, dimensions={0} | all-to-all | bytes 294912 | tf_op jit(solution)/shard_map/all_to_all | solution.py:265
  118.7 0.8 shard_map.57.refs_3_
  120.4 10.3 %all_to_all.75 = f32[32,9,1,128]{3,2,1,0:T(1,128)S(1)} all-to-all(f32[32,9,1,128]{3,2,1,0:T(1,128)S(1)} %bitcast.41), channel_id=1, replica_groups=mesh['side'=2,'grp'=2,'pts'=8] {'side','grp','pts'}, dimensions={0} | all-to-all | bytes 294912 | tf_op jit(solution)/shard_map/all_to_all | solution.py:265
  130.7 10.3 %all_to_all.76 = f32[32,9,1,128]{3,2,1,0:T(1,128)S(1)} all-to-all(f32[32,9,1,128]{3,2,1,0:T(1,128)S(1)} %bitcast.54), channel_id=1, replica_groups=mesh['side'=2,'grp'=2,'pts'=8] {'side','grp','pts'}, dimensions={0} | all-to-all | bytes 294912 | tf_op jit(solution)/shard_map/all_to_all | solution.py:265
  141.5 0.8 shard_map.61.refs_3_
  143.1 9.7 %all_to_all.77.refs_1_ = f32[32,4,128]{2,1,0:T(4,128)S(1)} all-to-all(f32[32,4,128]{2,1,0:T(4,128)S(1)} %get-tuple-element.17), channel_id=1, replica_groups=mesh['side'=2,'grp'=2,'pts'=8] {'side','grp','pts'}, dimensions={0} | all-to-all | bytes 131072 | tf_op jit(solution)/shard_map/all_to_all | solution.py:261
  152.8 1.6 %shard_map.63 = f32[32,256]{1,0:T(8,128)} custom-call(s32[1]{0:T(128)} %bitcast._.refs_0_, f32[32,4,128]{2,1,0:T(4,128)S(1)} %all_to_all.77.refs_1_, f32[32,256]{1,0:T(8,128)S(1)} %get-tuple-element.18.refs_2_), custom_call_target="tpu_custom_call" | custom-call | tf_op jit(solution)/shard_map/pallas_call | solution.py:234
  (34 shorter events, 7.6 us)
Async XLA Ops:
  1.3 2.1 %collective-permute-start.1 = (bf16[256,1024]{1,0:T(8,128)(2,1)S(1)}, bf16[256,1024]{1,0:T(8,128)(2,1)S(1)}, u32[]{:S(2)}, u32[]{:S(2)}) collective-permute-start(bf16[256,1024]{1,0:T(8,128)(2,1)S(1)} %get-tuple-element.14), channel_id=1, source_target_pairs={{8,0},{0,8},{9,1},{1,9},{10,2},{2,10},{11,3},{3,11},{12,4},{4,12},... | collective-permute-start | bytes 1572872 | tf_op jit(solution)/shard_map/ppermute | solution.py:270
  1.8 1.6 %collective-permute-start = (f32[40,256]{1,0:T(8,128)S(1)}, f32[40,256]{1,0:T(8,128)S(1)}, u32[]{:S(2)}, u32[]{:S(2)}) collective-permute-start(f32[40,256]{1,0:T(8,128)S(1)} %get-tuple-element.12.refs_0_), channel_id=1, source_target_pairs={{8,0},{0,8},{9,1},{1,9},{10,2},{2,10},{11,3},{3,11},{12,4},{4,12},... | collective-permute-start | bytes 122888 | tf_op jit(solution)/shard_map/ppermute | solution.py:270
  28.4 1.3 collective-permute-start.2
  50.2 1.3 collective-permute-start.3
  73.0 1.3 collective-permute-start.4
  95.8 1.3 collective-permute-start.5
  118.5 1.3 collective-permute-start.6
  141.3 1.3 collective-permute-start.7

commit v8 on v7

--- a/solution.py
+++ b/solution.py
@@ -102,12 +102,14 @@
     return jnp.concatenate(slabs, axis=0)
 
 
-def setup_kernel(place_ref, _, fields_ref, weight_ref, modes_ref, pack_ref, *rest):
-    *block_refs, row_ref, sems = rest
-    grp, columns = len(block_refs), block_refs[0].shape[1]
-    modes = modes_ref.shape[1]
-    pairs = [(weight_ref, row_ref), (modes_ref.at[0], pack_ref.at[:modes])]
-    for k in reversed(range(grp)):
+def start_kernel(place_ref, _, fields_ref, weight_ref, modes_ref, weights_ref, part_ref, *rest):
+    *out_refs, row_ref, modes_vmem, sems = rest
+    grp = (len(out_refs) + 1) // 2
+    part_refs, block_refs = [part_ref] + out_refs[: grp - 1], out_refs[grp - 1 :]
+    columns, modes = block_refs[0].shape[1], part_ref.shape[0]
+    pairs = [(weight_ref, row_ref), (modes_ref.at[0], modes_vmem)]
+    order = list(reversed(range(grp)))
+    for k in order:
         start = pl.multiple_of(lax.rem(place_ref[0] + grp - k, grp) * columns, LANES)
         pairs.append((fields_ref.at[0, :, pl.ds(start, columns)], block_refs[k]))
     copies = [
@@ -117,17 +119,29 @@
     for copy in copies:
         copy.start()
     copies[0].wait()
-    pack_ref[modes:] = jnp.broadcast_to(row_ref[...], (ROWS, row_ref.shape[1]))
-    for copy in copies[1:]:
+    copies[1].wait()
+    weights = jnp.broadcast_to(row_ref[...], weights_ref.shape)
+    weights_ref[...] = weights
+    weighted = modes_vmem[...] * row_ref[...]
+    for k, copy in zip(order, copies[2:]):
+        if k:
+            part_refs[k][modes:, : weights.shape[1]] = weights
+            part_refs[k][modes:, weights.shape[1] :] = jnp.zeros(
+                (ROWS, columns - weights.shape[1]), F32
+            )
         copy.wait()
-
-
-def first_kernel(*refs):
-    *pack_refs, field_ref, send_ref, weight_ref = refs
-    pack = jnp.concatenate([ref[...] for ref in pack_refs], axis=1)
-    weight = pack[-ROWS:]
-    weight_ref[...] = weight
-    store_tiles(send_ref, dot_wide(pack[:-ROWS] * weight[:1], field_ref[...]), ROWS)
+        part_refs[k][:modes] = dot_wide(weighted, block_refs[k][...])
+
+
+def first_kernel(weights_ref, part_ref, *refs):
+    *message_refs, send_ref, weight_ref = refs
+    modes, points = part_ref.shape[0], weights_ref.shape[1]
+    total, weights = part_ref[...], [weights_ref[...]]
+    for ref in message_refs:
+        total = total + ref[:modes]
+        weights.append(ref[modes:, :points])
+    store_tiles(send_ref, total, ROWS)
+    weight_ref[...] = jnp.concatenate(weights, axis=1)
 
 
 def reduce_kernel(recv_ref, send_ref, *, grp, pts, pitch):
@@ -154,10 +168,9 @@
     out_ref[...] = inverse_factor(unfold(gram, modes) / points, modes)
 
 
-def back_kernel(recv_ref, field_ref, out_ref, *, pitch, samples):
-    columns = samples // LANES
+def gathered_rows(recv_ref, columns, pitch):
     count = recv_ref.shape[0] // (pitch * columns)
-    coeffs = jnp.concatenate(
+    return jnp.concatenate(
         [
             jnp.concatenate(
                 [
@@ -170,16 +183,29 @@
         ],
         axis=0,
     )
-    if coeffs.dtype == BF16:
-        out_ref[...] = lax.dot_general(
-            coeffs, field_ref[...], (((1,), (1,)), ((), ())), preferred_element_type=F32
+
+
+def first_back_kernel(recv_ref, *refs):
+    *block_refs, out_ref = refs
+    coeffs = gathered_rows(recv_ref, block_refs[0].shape[1] // LANES, ROWS)
+    points = block_refs[0].shape[0]
+    for k, ref in enumerate(block_refs):
+        out_ref[:, k * points : (k + 1) * points] = lax.dot_general(
+            coeffs, ref[...], (((1,), (1,)), ((), ())), preferred_element_type=F32
         )
-    else:
-        out_ref[...] = dot_wide(coeffs, field_ref[...])
-
-
-def turn_kernel(_, field_ref, out_ref):
-    out_ref[...] = field_ref[...].T
+
+
+def back_kernel(recv_ref, turned_ref, out_ref, *, pitch):
+    coeffs = gathered_rows(recv_ref, turned_ref.shape[0] // LANES, pitch)
+    out_ref[...] = dot_wide(coeffs, turned_ref[...])
+
+
+def join_kernel(_, *refs):
+    *block_refs, field_ref, turned_ref = refs
+    points = block_refs[0].shape[0]
+    for k, ref in enumerate(block_refs):
+        field_ref[k * points : (k + 1) * points] = ref[...]
+        turned_ref[:, k * points : (k + 1) * points] = ref[...].T
 
 
 def map_kernel(*refs, samples, others, has_factor, last):
@@ -192,7 +218,7 @@
         other = refs.pop(0)[...]
         cut = (others - k) * block
         mapped = mapped + jnp.concatenate([other[:, cut:], other[:, :cut]], axis=1)
-    factor = refs.pop(0)[...][:, :modes]
+    factor = refs.pop(0)[...][:, :modes] if has_factor else None
     weight = refs.pop(0)[:1]
     if has_factor:
         mapped = jnp.dot(factor, mapped, precision=HIGHEST, preferred_element_type=F32)
@@ -241,19 +267,26 @@
     return result if len(out) > 1 else result[0]
 
 
-def cut(place, side, fields, weight, modes, grp):
+def begin(place, side, fields, weight, modes, grp):
     _, points, samples = fields.shape
-    out = [pltpu.VMEM((modes.shape[1] + ROWS, points), F32)]
-    out += [pltpu.VMEM((points, samples // grp), fields.dtype) for _ in range(grp)]
-    anywhere = pl.BlockSpec(memory_space=pltpu.HBM)
-    return pl.pallas_call(
-        setup_kernel,
+    columns, rows = samples // grp, modes.shape[1]
+    out = [pltpu.VMEM((ROWS, points), F32), pltpu.VMEM((rows, columns), F32)]
+    out += [pltpu.VMEM((rows + ROWS, columns), F32) for _ in range(1, grp)]
+    out += [pltpu.VMEM((points, columns), fields.dtype) for _ in range(grp)]
+    far = [pltpu.with_memory_space_constraint(a, pltpu.HBM) for a in (fields, weight, modes)]
+    weights, part, *rest = pl.pallas_call(
+        start_kernel,
         out_shape=out,
-        in_specs=[SMEM, SMEM, anywhere, anywhere, anywhere],
+        in_specs=[SMEM, SMEM] + [pl.BlockSpec(memory_space=pltpu.HBM)] * 3,
         out_specs=[VMEM for _ in out],
         compiler_params=GRANT,
-        scratch_shapes=[pltpu.VMEM((1, points), F32), pltpu.SemaphoreType.DMA((grp + 2,))],
-    )(place, side, *(pltpu.with_memory_space_constraint(a, pltpu.HBM) for a in (fields, weight, modes)))
+        scratch_shapes=[
+            pltpu.VMEM((1, points), F32),
+            pltpu.VMEM((rows, points), F32),
+            pltpu.SemaphoreType.DMA((grp + 2,)),
+        ],
+    )(place, side, *far)
+    return weights, part, rest[: grp - 1], rest[grp - 1 :]
 
 
 def exchange(value, pitch=None):
@@ -279,38 +312,40 @@
     place = lax.axis_index("grp").astype(jnp.int32).reshape(1)
     side = lax.axis_index("side").astype(jnp.int32).reshape(1)
 
-    pack, *blocks = cut(place, side, fields, point_weight, start_modes, grp)
-    packs = [pack] + [shifted(pack, k) for k in range(1, grp)]
-    field = jnp.concatenate(
-        [blocks[0]] + [shifted(blocks[k], k) for k in range(1, grp)], axis=0
-    )
-    factor, pitch = None, ROWS
+    weights, part, messages, blocks = begin(
+        place, side, fields, point_weight, start_modes, grp
+    )
+    messages = [shifted(m, k + 1) for k, m in enumerate(messages)]
+    *others, _ = lax.optimization_barrier((*blocks[1:], messages))
+    blocks = [blocks[0]] + [shifted(block, k + 1) for k, block in enumerate(others)]
+    pitch = ROWS
     outs = [((devices * ROWS, LANES), F32), ((ROWS, points), F32)]
-    send, weight = call(first_kernel, outs, *packs, field)
+    send, weight = call(first_kernel, outs, weights, part, *messages)
     for iteration in range(ITERS):
         has_gram, last = iteration > 0, iteration == ITERS - 1
         kernel = lambda *refs: reduce_kernel(*refs, grp=grp, pts=pts, pitch=pitch)
         dtype = F32 if has_gram else BF16
         summed = call(kernel, [((devices * pitch, LANES), dtype)], exchange(send, pitch))
         gathered = exchange(summed, pitch)
-        kernel = lambda *refs: back_kernel(*refs, pitch=pitch, samples=samples // grp)
-        own = call(
-            kernel, [((modes, points), F32)], gathered, turned if has_gram else field
-        )
-        if not has_gram:
-            shape = (field.shape[1], points)
-            turned = call(turn_kernel, [(shape, field.dtype)], own, field)
-        others = [shifted(own, k) for k in range(1, grp)]
+        outs = [((modes, points), F32)]
         if has_gram:
+            kernel = lambda *refs: back_kernel(*refs, pitch=pitch)
+            own = call(kernel, outs, gathered, turned)
             kernel = lambda *refs: factor_kernel(
                 *refs, modes=modes, points=total_points, pitch=pitch
             )
-            factor = call(kernel, [((modes, LANES), F32)], gathered)
+            factor = [call(kernel, [((modes, LANES), F32)], gathered)]
+        else:
+            own = call(first_back_kernel, outs, gathered, *blocks)
+            outs = [((points, samples // grp), BF16), ((samples // grp, points), BF16)]
+            field, turned = call(join_kernel, outs, own, *blocks)
+            factor = []
+        others = [shifted(own, k) for k in range(1, grp)]
         pitch = ROWS + 1
         kernel = lambda *refs: map_kernel(
             *refs, samples=samples, others=grp - 1, has_factor=has_gram, last=last
         )
-        given = [place, own, *others, factor if has_gram else turned, weight]
+        given = [place, own, *others, *factor, weight]
         if last:
             outs = [((modes, points // grp), F32), ((devices, ROWS // grp, LANES), F32)]
             mapped, send = call(kernel, outs, *given)
@@ -348,6 +383,7 @@
         modes, samples = start_modes.shape[1], fields.shape[2]
         tiles = (modes // ROWS) * (samples // (LANES * grp))
         fits = tiles == 2 * grp * pts and 4 * modes == LANES and ROWS % grp == 0
+        fits = fits and fields.shape[1] <= samples * pts
         placed = (
             P("side", ("grp", "pts"), None),
             P("side", ("grp", "pts")),

time: 155 us -> 154 us (level)
  no operation moved by 1% of the time
where the time goes in v8:
time: 154 us
  blocking collectives  136 us (88%)
  Pallas kernels  12.6 us (8%)
  waiting for transfers between devices  3.39 us (2%)
  starting transfers between devices  1.78 us (1%)
    all_to_all x12, blocking collectives, exchange(): return lax.all_to_all(split, ALL, 0, 0).reshape(value.shape)  126 us
    pallas_call x26, Pallas kernels, call(): pl.pallas_call(kernel, out_shape=out, in_specs=specs, out_specs=[VMEM for...  11 us
    all_to_all x1, blocking collectives, exchange(): return lax.all_to_all(value, ALL, 0, 0)  9.7 us
    ppermute x8, waiting for transfers between devices, shifted(): lax.ppermute(value, 'grp', [((i + shift) % grp, i) for i in range(grp)])  3.39 us
  transfers between devices with their start and end apart: 8, of which 7 were waited for; matrix products, arithmetic and copies ran while one was open for 0% of the time, Pallas kernels for 3%

profile of v8, /device:TPU:0, one launch (start us, length us, event | category | flops | bytes accessed | tf_op | source)
XLA Modules:
  0.0 154.0 jit_solution(14479932161845661570)
XLA Ops:
  0.0 1.6 %shard_map.37 = (f32[8,256]{1,0:T(8,128)S(1)}, f32[32,1024]{1,0:T(8,128)S(1)}, f32[40,1024]{1,0:T(8,128)S(1)}, bf16[256,1024]{1,0:T(8,128)(2,1)S(1)}, bf16[256,1024]{1,0:T(8,128)(2,1)S(1)}) custom-call(s32[1]{0:T(128)} %bitcast.1.place_ref.refs_0_, s32[1]{0:T(128)} %bitcast._.refs_0_, bf16[1,256,2048]{2,1,0:T(8,128)(2,1)} %fields_ref.1, ...), custom_call_target="tpu_custom_call" | custom-call | tf_op jit(solution)/shard_map/pallas_call | solution.py:277
  2.1 1.0 collective-permute-done.refs_0_
  3.5 14.6 %all_to_all.65 = f32[32,1,8,128]{3,2,1,0:T(8,128)S(1)} all-to-all(f32[32,1,8,128]{3,2,1,0:T(8,128)S(1)} %bitcast.59), channel_id=1, replica_groups=mesh['side'=2,'grp'=2,'pts'=8] {'side','grp','pts'}, dimensions={0} | all-to-all | bytes 262144 | tf_op jit(solution)/shard_map/all_to_all | solution.py:298
  18.2 9.4 %all_to_all.66 = bf16[32,1,8,128]{3,2,1,0:T(8,128)(2,1)S(1)} all-to-all(bf16[32,1,8,128]{3,2,1,0:T(8,128)(2,1)S(1)} %bitcast.58), channel_id=1, replica_groups=mesh['side'=2,'grp'=2,'pts'=8] {'side','grp','pts'}, dimensions={0} | all-to-all | bytes 131072 | tf_op jit(solution)/shard_map/all_to_all | solution.py:298
  28.5 0.8 collective-permute-done.2.refs_2_
  29.6 9.6 %all_to_all.67 = f32[32,9,1,128]{3,2,1,0:T(1,128)S(1)} all-to-all(f32[32,9,1,128]{3,2,1,0:T(1,128)S(1)} %bitcast.45), channel_id=1, replica_groups=mesh['side'=2,'grp'=2,'pts'=8] {'side','grp','pts'}, dimensions={0} | all-to-all | bytes 294912 | tf_op jit(solution)/shard_map/all_to_all | solution.py:298
  39.3 10.2 %all_to_all.68 = f32[32,9,1,128]{3,2,1,0:T(1,128)S(1)} all-to-all(f32[32,9,1,128]{3,2,1,0:T(1,128)S(1)} %bitcast.47), channel_id=1, replica_groups=mesh['side'=2,'grp'=2,'pts'=8] {'side','grp','pts'}, dimensions={0} | all-to-all | bytes 294912 | tf_op jit(solution)/shard_map/all_to_all | solution.py:298
  49.9 0.8 shard_map.45.refs_3_
  51.6 10.3 %all_to_all.69 = f32[32,9,1,128]{3,2,1,0:T(1,128)S(1)} all-to-all(f32[32,9,1,128]{3,2,1,0:T(1,128)S(1)} %bitcast.42), channel_id=1, replica_groups=mesh['side'=2,'grp'=2,'pts'=8] {'side','grp','pts'}, dimensions={0} | all-to-all | bytes 294912 | tf_op jit(solution)/shard_map/all_to_all | solution.py:298
  62.0 10.3 %all_to_all.70 = f32[32,9,1,128]{3,2,1,0:T(1,128)S(1)} all-to-all(f32[32,9,1,128]{3,2,1,0:T(1,128)S(1)} %bitcast.49), channel_id=1, replica_groups=mesh['side'=2,'grp'=2,'pts'=8] {'side','grp','pts'}, dimensions={0} | all-to-all | bytes 294912 | tf_op jit(solution)/shard_map/all_to_all | solution.py:298
  72.7 0.8 shard_map.49.refs_3_
  73.9 0.6 shard_map.50
  74.4 10.3 %all_to_all.71 = f32[32,9,1,128]{3,2,1,0:T(1,128)S(1)} all-to-all(f32[32,9,1,128]{3,2,1,0:T(1,128)S(1)} %bitcast.43), channel_id=1, replica_groups=mesh['side'=2,'grp'=2,'pts'=8] {'side','grp','pts'}, dimensions={0} | all-to-all | bytes 294912 | tf_op jit(solution)/shard_map/all_to_all | solution.py:298
  84.8 10.3 %all_to_all.72 = f32[32,9,1,128]{3,2,1,0:T(1,128)S(1)} all-to-all(f32[32,9,1,128]{3,2,1,0:T(1,128)S(1)} %bitcast.51), channel_id=1, replica_groups=mesh['side'=2,'grp'=2,'pts'=8] {'side','grp','pts'}, dimensions={0} | all-to-all | bytes 294912 | tf_op jit(solution)/shard_map/all_to_all | solution.py:298
  95.5 0.8 shard_map.53.refs_3_
  96.6 0.6 shard_map.54
  97.2 10.3 %all_to_all.73 = f32[32,9,1,128]{3,2,1,0:T(1,128)S(1)} all-to-all(f32[32,9,1,128]{3,2,1,0:T(1,128)S(1)} %bitcast.44), channel_id=1, replica_groups=mesh['side'=2,'grp'=2,'pts'=8] {'side','grp','pts'}, dimensions={0} | all-to-all | bytes 294912 | tf_op jit(solution)/shard_map/all_to_all | solution.py:298
  107.6 10.3 %all_to_all.74 = f32[32,9,1,128]{3,2,1,0:T(1,128)S(1)} all-to-all(f32[32,9,1,128]{3,2,1,0:T(1,128)S(1)} %bitcast.53), channel_id=1, replica_groups=mesh['side'=2,'grp'=2,'pts'=8] {'side','grp','pts'}, dimensions={0} | all-to-all | bytes 294912 | tf_op jit(solution)/shard_map/all_to_all | solution.py:298
  118.3 0.8 shard_map.57.refs_3_
  120.0 10.3 %all_to_all.75 = f32[32,9,1,128]{3,2,1,0:T(1,128)S(1)} all-to-all(f32[32,9,1,128]{3,2,1,0:T(1,128)S(1)} %bitcast.41), channel_id=1, replica_groups=mesh['side'=2,'grp'=2,'pts'=8] {'side','grp','pts'}, dimensions={0} | all-to-all | bytes 294912 | tf_op jit(solution)/shard_map/all_to_all | solution.py:298
  130.3 10.3 %all_to_all.76 = f32[32,9,1,128]{3,2,1,0:T(1,128)S(1)} all-to-all(f32[32,9,1,128]{3,2,1,0:T(1,128)S(1)} %bitcast.55), channel_id=1, replica_groups=mesh['side'=2,'grp'=2,'pts'=8] {'side','grp','pts'}, dimensions={0} | all-to-all | bytes 294912 | tf_op jit(solution)/shard_map/all_to_all | solution.py:298
  141.1 0.8 shard_map.61.refs_3_
  142.7 9.7 %all_to_all.77.refs_1_ = f32[32,4,128]{2,1,0:T(4,128)S(1)} all-to-all(f32[32,4,128]{2,1,0:T(4,128)S(1)} %get-tuple-element.27), channel_id=1, replica_groups=mesh['side'=2,'grp'=2,'pts'=8] {'side','grp','pts'}, dimensions={0} | all-to-all | bytes 131072 | tf_op jit(solution)/shard_map/all_to_all | solution.py:294
  152.4 1.6 %shard_map.63 = f32[32,256]{1,0:T(8,128)} custom-call(s32[1]{0:T(128)} %bitcast._.refs_0_, f32[32,4,128]{2,1,0:T(4,128)S(1)} %all_to_all.77.refs_1_, f32[32,256]{1,0:T(8,128)S(1)} %get-tuple-element.28.refs_2_), custom_call_target="tpu_custom_call" | custom-call | tf_op jit(solution)/shard_map/pallas_call | solution.py:260
  (32 shorter events, 7.6 us)
Async XLA Ops:
  1.6 1.6 %collective-permute-start = (f32[40,1024]{1,0:T(8,128)S(1)}, f32[40,1024]{1,0:T(8,128)S(1)}, u32[]{:S(2)}, u32[]{:S(2)}) collective-permute-start(f32[40,1024]{1,0:T(8,128)S(1)} %get-tuple-element.19), channel_id=1, source_target_pairs={{8,0},{0,8},{9,1},{1,9},{10,2},{2,10},{11,3},{3,11},{12,4},{4,12},... | collective-permute-start | bytes 491528 | tf_op jit(solution)/shard_map/ppermute | solution.py:303
  3.2 24.4 %collective-permute-start.1 = (bf16[256,1024]{1,0:T(8,128)(2,1)S(1)}, bf16[256,1024]{1,0:T(8,128)(2,1)S(1)}, u32[]{:S(2)}, u32[]{:S(2)}) collective-permute-start(bf16[256,1024]{1,0:T(8,128)(2,1)S(1)} %get-tuple-element.23), channel_id=1, source_target_pairs={{8,0},{0,8},{9,1},{1,9},{10,2},{2,10},{11,3},{3,11},{12,4},{4,12},... | collective-permute-start | bytes 1572872 | tf_op jit(solution)/shard_map/ppermute | solution.py:303
  28.0 1.3 collective-permute-start.2
  49.8 1.3 collective-permute-start.3
  72.6 1.3 collective-permute-start.4
  95.4 1.3 collective-permute-start.5
  118.2 1.3 collective-permute-start.6
  140.9 1.3 collective-permute-start.7

commit v9 on v8

--- a/solution.py
+++ b/solution.py
@@ -102,16 +102,20 @@
     return jnp.concatenate(slabs, axis=0)
 
 
-def start_kernel(place_ref, _, fields_ref, weight_ref, modes_ref, weights_ref, part_ref, *rest):
+def own_part(place_ref, fields_ref, back, columns, grp):
+    start = pl.multiple_of(lax.rem(place_ref[0] + grp - back, grp) * columns, LANES)
+    return fields_ref.at[0, :, pl.ds(start, columns)]
+
+
+def send_kernel(place_ref, _, fields_ref, weight_ref, modes_ref, weights_ref, weighted_ref, *rest):
     *out_refs, row_ref, modes_vmem, sems = rest
-    grp = (len(out_refs) + 1) // 2
-    part_refs, block_refs = [part_ref] + out_refs[: grp - 1], out_refs[grp - 1 :]
-    columns, modes = block_refs[0].shape[1], part_ref.shape[0]
+    others = len(out_refs) // 2
+    message_refs, block_refs = out_refs[:others], out_refs[others:]
+    modes = weighted_ref.shape[0]
     pairs = [(weight_ref, row_ref), (modes_ref.at[0], modes_vmem)]
-    order = list(reversed(range(grp)))
-    for k in order:
-        start = pl.multiple_of(lax.rem(place_ref[0] + grp - k, grp) * columns, LANES)
-        pairs.append((fields_ref.at[0, :, pl.ds(start, columns)], block_refs[k]))
+    for k, ref in enumerate(block_refs):
+        columns = ref.shape[1]
+        pairs.append((own_part(place_ref, fields_ref, k + 1, columns, others + 1), ref))
     copies = [
         pltpu.make_async_copy(source, target, sems.at[i])
         for i, (source, target) in enumerate(pairs)
@@ -123,14 +127,21 @@
     weights = jnp.broadcast_to(row_ref[...], weights_ref.shape)
     weights_ref[...] = weights
     weighted = modes_vmem[...] * row_ref[...]
-    for k, copy in zip(order, copies[2:]):
-        if k:
-            part_refs[k][modes:, : weights.shape[1]] = weights
-            part_refs[k][modes:, weights.shape[1] :] = jnp.zeros(
-                (ROWS, columns - weights.shape[1]), F32
-            )
+    weighted_ref[...] = weighted
+    points = weights.shape[1]
+    for message, block, copy in zip(message_refs, block_refs, copies[2:]):
+        message[modes:, :points] = weights
+        message[modes:, points:] = jnp.zeros((ROWS, message.shape[1] - points), F32)
         copy.wait()
-        part_refs[k][:modes] = dot_wide(weighted, block_refs[k][...])
+        message[:modes] = dot_wide(weighted, block[...])
+
+
+def keep_kernel(place_ref, weighted_ref, fields_ref, part_ref, block_ref, sem, *, grp):
+    source = own_part(place_ref, fields_ref, 0, block_ref.shape[1], grp)
+    copy = pltpu.make_async_copy(source, block_ref, sem)
+    copy.start()
+    copy.wait()
+    part_ref[...] = dot_wide(weighted_ref[...], block_ref[...])
 
 
 def first_kernel(weights_ref, part_ref, *refs):
@@ -269,24 +280,34 @@
 
 def begin(place, side, fields, weight, modes, grp):
     _, points, samples = fields.shape
-    columns, rows = samples // grp, modes.shape[1]
-    out = [pltpu.VMEM((ROWS, points), F32), pltpu.VMEM((rows, columns), F32)]
+    columns, rows, far = samples // grp, modes.shape[1], pl.BlockSpec(memory_space=pltpu.HBM)
+    fields, weight, modes = (
+        pltpu.with_memory_space_constraint(a, pltpu.HBM) for a in (fields, weight, modes)
+    )
+    out = [pltpu.VMEM((ROWS, points), F32), pltpu.VMEM((rows, points), F32)]
     out += [pltpu.VMEM((rows + ROWS, columns), F32) for _ in range(1, grp)]
-    out += [pltpu.VMEM((points, columns), fields.dtype) for _ in range(grp)]
-    far = [pltpu.with_memory_space_constraint(a, pltpu.HBM) for a in (fields, weight, modes)]
-    weights, part, *rest = pl.pallas_call(
-        start_kernel,
+    out += [pltpu.VMEM((points, columns), fields.dtype) for _ in range(1, grp)]
+    weights, weighted, *rest = pl.pallas_call(
+        send_kernel,
         out_shape=out,
-        in_specs=[SMEM, SMEM] + [pl.BlockSpec(memory_space=pltpu.HBM)] * 3,
+        in_specs=[SMEM, SMEM, far, far, far],
         out_specs=[VMEM for _ in out],
         compiler_params=GRANT,
         scratch_shapes=[
             pltpu.VMEM((1, points), F32),
             pltpu.VMEM((rows, points), F32),
-            pltpu.SemaphoreType.DMA((grp + 2,)),
+            pltpu.SemaphoreType.DMA((grp + 1,)),
         ],
-    )(place, side, *far)
-    return weights, part, rest[: grp - 1], rest[grp - 1 :]
+    )(place, side, fields, weight, modes)
+    part, block = pl.pallas_call(
+        lambda *refs: keep_kernel(*refs, grp=grp),
+        out_shape=[pltpu.VMEM((rows, columns), F32), pltpu.VMEM((points, columns), BF16)],
+        in_specs=[SMEM, VMEM, far],
+        out_specs=[VMEM, VMEM],
+        compiler_params=GRANT,
+        scratch_shapes=[pltpu.SemaphoreType.DMA],
+    )(place, pltpu.with_memory_space_constraint(weighted, pltpu.VMEM), fields)
+    return weights, part, rest[: grp - 1], [block] + rest[grp - 1 :]
 
 
 def exchange(value, pitch=None):
@@ -316,7 +337,7 @@
         place, side, fields, point_weight, start_modes, grp
     )
     messages = [shifted(m, k + 1) for k, m in enumerate(messages)]
-    *others, _ = lax.optimization_barrier((*blocks[1:], messages))
+    *others, part = lax.optimization_barrier((*blocks[1:], part))
     blocks = [blocks[0]] + [shifted(block, k + 1) for k, block in enumerate(others)]
     pitch = ROWS
     outs = [((devices * ROWS, LANES), F32), ((ROWS, points), F32)]
@@ -326,6 +347,8 @@
         kernel = lambda *refs: reduce_kernel(*refs, grp=grp, pts=pts, pitch=pitch)
         dtype = F32 if has_gram else BF16
         summed = call(kernel, [((devices * pitch, LANES), dtype)], exchange(send, pitch))
+        if not has_gram:
+            summed, *blocks = lax.optimization_barrier((summed, *blocks))
         gathered = exchange(summed, pitch)
         outs = [((modes, points), F32)]
         if has_gram:

time: 154 us -> 156 us (1.013)
  no operation moved by 1% of the time
where the time goes in v9:
time: 156 us
  blocking collectives  136 us (87%)
  Pallas kernels  13.7 us (9%)
  waiting for transfers between devices  4.06 us (3%)
    all_to_all x12, blocking collectives, exchange(): return lax.all_to_all(split, ALL, 0, 0).reshape(value.shape)  127 us
    pallas_call x26, Pallas kernels, call(): pl.pallas_call(kernel, out_shape=out, in_specs=specs, out_specs=[VMEM for...  11 us
    all_to_all x1, blocking collectives, exchange(): return lax.all_to_all(value, ALL, 0, 0)  9.7 us
    ppermute x8, waiting for transfers between devices, shifted(): lax.ppermute(value, 'grp', [((i + shift) % grp, i) for i in range(grp)])  4.06 us
  transfers between devices with their start and end apart: 8, of which 7 were waited for; matrix products, arithmetic and copies ran while one was open for 0% of the time, Pallas kernels for 3%

profile of v9, /device:TPU:0, one launch (start us, length us, event | category | flops | bytes accessed | tf_op | source)
XLA Modules:
  0.0 155.7 jit_solution(17494914748499103565)
XLA Ops:
  0.0 1.3 shard_map.37
  1.3 1.3 shard_map.38
  3.3 1.7 %collective-permute-done.refs_0_ = f32[40,1024]{1,0:T(8,128)S(1)} collective-permute-done((f32[40,1024]{1,0:T(8,128)S(1)}, f32[40,1024]{1,0:T(8,128)S(1)}, u32[]{:S(2)}, u32[]{:S(2)}) %collective-permute-start) | collective-permute-done | bytes 163872 | tf_op jit(solution)/shard_map/ppermute | solution.py:324
  5.0 14.8 %all_to_all.65 = f32[32,1,8,128]{3,2,1,0:T(8,128)S(1)} all-to-all(f32[32,1,8,128]{3,2,1,0:T(8,128)S(1)} %bitcast.59), channel_id=1, replica_groups=mesh['side'=2,'grp'=2,'pts'=8] {'side','grp','pts'}, dimensions={0} | all-to-all | bytes 262144 | tf_op jit(solution)/shard_map/all_to_all | solution.py:319
  19.8 9.4 %all_to_all.66 = bf16[32,1,8,128]{3,2,1,0:T(8,128)(2,1)S(1)} all-to-all(bf16[32,1,8,128]{3,2,1,0:T(8,128)(2,1)S(1)} %bitcast.57), channel_id=1, replica_groups=mesh['side'=2,'grp'=2,'pts'=8] {'side','grp','pts'}, dimensions={0} | all-to-all | bytes 131072 | tf_op jit(solution)/shard_map/all_to_all | solution.py:319
  30.2 0.8 collective-permute-done.2.refs_2_
  31.3 9.6 %all_to_all.67 = f32[32,9,1,128]{3,2,1,0:T(1,128)S(1)} all-to-all(f32[32,9,1,128]{3,2,1,0:T(1,128)S(1)} %bitcast.45), channel_id=1, replica_groups=mesh['side'=2,'grp'=2,'pts'=8] {'side','grp','pts'}, dimensions={0} | all-to-all | bytes 294912 | tf_op jit(solution)/shard_map/all_to_all | solution.py:319
  40.9 10.2 %all_to_all.68 = f32[32,9,1,128]{3,2,1,0:T(1,128)S(1)} all-to-all(f32[32,9,1,128]{3,2,1,0:T(1,128)S(1)} %bitcast.47), channel_id=1, replica_groups=mesh['side'=2,'grp'=2,'pts'=8] {'side','grp','pts'}, dimensions={0} | all-to-all | bytes 294912 | tf_op jit(solution)/shard_map/all_to_all | solution.py:319
  51.6 0.8 shard_map.46.refs_3_
  53.3 10.3 %all_to_all.69 = f32[32,9,1,128]{3,2,1,0:T(1,128)S(1)} all-to-all(f32[32,9,1,128]{3,2,1,0:T(1,128)S(1)} %bitcast.42), channel_id=1, replica_groups=mesh['side'=2,'grp'=2,'pts'=8] {'side','grp','pts'}, dimensions={0} | all-to-all | bytes 294912 | tf_op jit(solution)/shard_map/all_to_all | solution.py:319
  63.6 10.3 %all_to_all.70 = f32[32,9,1,128]{3,2,1,0:T(1,128)S(1)} all-to-all(f32[32,9,1,128]{3,2,1,0:T(1,128)S(1)} %bitcast.49), channel_id=1, replica_groups=mesh['side'=2,'grp'=2,'pts'=8] {'side','grp','pts'}, dimensions={0} | all-to-all | bytes 294912 | tf_op jit(solution)/shard_map/all_to_all | solution.py:319
  74.4 0.8 shard_map.50.refs_3_
  75.5 0.6 shard_map.51
  76.1 10.3 %all_to_all.71 = f32[32,9,1,128]{3,2,1,0:T(1,128)S(1)} all-to-all(f32[32,9,1,128]{3,2,1,0:T(1,128)S(1)} %bitcast.43), channel_id=1, replica_groups=mesh['side'=2,'grp'=2,'pts'=8] {'side','grp','pts'}, dimensions={0} | all-to-all | bytes 294912 | tf_op jit(solution)/shard_map/all_to_all | solution.py:319
  86.4 10.3 %all_to_all.72 = f32[32,9,1,128]{3,2,1,0:T(1,128)S(1)} all-to-all(f32[32,9,1,128]{3,2,1,0:T(1,128)S(1)} %bitcast.51), channel_id=1, replica_groups=mesh['side'=2,'grp'=2,'pts'=8] {'side','grp','pts'}, dimensions={0} | all-to-all | bytes 294912 | tf_op jit(solution)/shard_map/all_to_all | solution.py:319
  97.2 0.8 shard_map.54.refs_3_
  98.9 10.3 %all_to_all.73 = f32[32,9,1,128]{3,2,1,0:T(1,128)S(1)} all-to-all(f32[32,9,1,128]{3,2,1,0:T(1,128)S(1)} %bitcast.44), channel_id=1, replica_groups=mesh['side'=2,'grp'=2,'pts'=8] {'side','grp','pts'}, dimensions={0} | all-to-all | bytes 294912 | tf_op jit(solution)/shard_map/all_to_all | solution.py:319
  109.2 10.3 %all_to_all.74 = f32[32,9,1,128]{3,2,1,0:T(1,128)S(1)} all-to-all(f32[32,9,1,128]{3,2,1,0:T(1,128)S(1)} %bitcast.53), channel_id=1, replica_groups=mesh['side'=2,'grp'=2,'pts'=8] {'side','grp','pts'}, dimensions={0} | all-to-all | bytes 294912 | tf_op jit(solution)/shard_map/all_to_all | solution.py:319
  120.0 0.8 shard_map.58.refs_3_
  121.7 10.3 %all_to_all.75 = f32[32,9,1,128]{3,2,1,0:T(1,128)S(1)} all-to-all(f32[32,9,1,128]{3,2,1,0:T(1,128)S(1)} %bitcast.41), channel_id=1, replica_groups=mesh['side'=2,'grp'=2,'pts'=8] {'side','grp','pts'}, dimensions={0} | all-to-all | bytes 294912 | tf_op jit(solution)/shard_map/all_to_all | solution.py:319
  132.0 10.3 %all_to_all.76 = f32[32,9,1,128]{3,2,1,0:T(1,128)S(1)} all-to-all(f32[32,9,1,128]{3,2,1,0:T(1,128)S(1)} %bitcast.55), channel_id=1, replica_groups=mesh['side'=2,'grp'=2,'pts'=8] {'side','grp','pts'}, dimensions={0} | all-to-all | bytes 294912 | tf_op jit(solution)/shard_map/all_to_all | solution.py:319
  142.8 0.8 shard_map.62.refs_3_
  144.4 9.7 %all_to_all.77.refs_1_ = f32[32,4,128]{2,1,0:T(4,128)S(1)} all-to-all(f32[32,4,128]{2,1,0:T(4,128)S(1)} %get-tuple-element.37), channel_id=1, replica_groups=mesh['side'=2,'grp'=2,'pts'=8] {'side','grp','pts'}, dimensions={0} | all-to-all | bytes 131072 | tf_op jit(solution)/shard_map/all_to_all | solution.py:315
  154.1 1.6 %shard_map.64 = f32[32,256]{1,0:T(8,128)} custom-call(s32[1]{0:T(128)} %bitcast._.refs_0_, f32[32,4,128]{2,1,0:T(4,128)S(1)} %all_to_all.77.refs_1_, f32[32,256]{1,0:T(8,128)S(1)} %get-tuple-element.38.refs_2_), custom_call_target="tpu_custom_call" | custom-call | tf_op jit(solution)/shard_map/pallas_call | solution.py:271
  (33 shorter events, 7.9 us)
Async XLA Ops:
  2.6 17.2 %collective-permute-start.1 = (bf16[256,1024]{1,0:T(8,128)(2,1)S(1)}, bf16[256,1024]{1,0:T(8,128)(2,1)S(1)}, u32[]{:S(2)}, u32[]{:S(2)}) collective-permute-start(bf16[256,1024]{1,0:T(8,128)(2,1)S(1)} %get-tuple-element.30), channel_id=1, source_target_pairs={{8,0},{0,8},{9,1},{1,9},{10,2},{2,10},{11,3},{3,11},{12,4},{4,12},... | collective-permute-start | bytes 1572872 | tf_op jit(solution)/shard_map/ppermute | solution.py:324
  3.2 1.8 %collective-permute-start = (f32[40,1024]{1,0:T(8,128)S(1)}, f32[40,1024]{1,0:T(8,128)S(1)}, u32[]{:S(2)}, u32[]{:S(2)}) collective-permute-start(f32[40,1024]{1,0:T(8,128)S(1)} %get-tuple-element.27), channel_id=1, source_target_pairs={{8,0},{0,8},{9,1},{1,9},{10,2},{2,10},{11,3},{3,11},{12,4},{4,12},... | collective-permute-start | bytes 491528 | tf_op jit(solution)/shard_map/ppermute | solution.py:324
  29.7 1.3 collective-permute-start.2
  51.5 1.3 collective-permute-start.3
  74.2 1.3 collective-permute-start.4
  97.0 1.3 collective-permute-start.5
  119.8 1.3 collective-permute-start.6
  142.6 1.3 collective-permute-start.7
